TPU v7x, 32 devices: a whole 2x2x4 slice. The times are simulated.
32 devices in a mesh: fsdp: 2 (over core), ctx: 4 (over y, x), tp: 4 (over z).
Axes of the slice: x: 2, y: 2, z: 4, core: 2. Of those that a mesh axis runs over, the one named last changes fastest.
Arguments:
- tokens: bfloat16 [4096, 1024], P(('fsdp', 'ctx')), may hold values from -6 to 6
- out_grad: bfloat16 [4096, 1024], P(('fsdp', 'ctx')), may hold values from -6 to 6
- segment_ids: int32 [2, 2048], P('fsdp'), may hold values from 0 to 3, never falling along the last dimension, each value on 1 to 1024 neighbouring positions
- owner_order: int32 [2, 2048], P('fsdp'), may hold values from 0 to 2047, as said below
- attn_gain: bfloat16 [2, 1024], P(None, ('fsdp', 'ctx')), may hold values from 0.5 to 1.5
- w_query: bfloat16 [2, 1024, 1024], P(None, ('fsdp', 'ctx'), 'tp'), may hold values from -0.1875 to 0.1875
- w_key: bfloat16 [2, 1024, 1024], P(None, ('fsdp', 'ctx'), 'tp'), may hold values from -0.1875 to 0.1875
- w_value: bfloat16 [2, 1024, 1024], P(None, ('fsdp', 'ctx'), 'tp'), may hold values from -0.1875 to 0.1875
- w_out: bfloat16 [2, 1024, 1024], P(None, 'tp', ('fsdp', 'ctx')), may hold values from -0.75 to 0.75
- mlp_gain: bfloat16 [2, 1024], P(None, ('fsdp', 'ctx')), may hold values from 0.5 to 1.5
- w_gate: bfloat16 [2, 1024, 2816], P(None, ('fsdp', 'ctx'), 'tp'), may hold values from -0.1875 to 0.1875
- w_up: bfloat16 [2, 1024, 2816], P(None, ('fsdp', 'ctx'), 'tp'), may hold values from -0.1875 to 0.1875
- w_down: bfloat16 [2, 2816, 1024], P(None, 'tp', ('fsdp', 'ctx')), may hold values from -0.109375 to 0.109375
Outputs:
- outputs: bfloat16 [4096, 1024], P(('fsdp', 'ctx'))
- grad_tokens: float32 [4096, 1024], P(('fsdp', 'ctx'))
- grad_attn_gain: float32 [2, 1024], P(None, ('fsdp', 'ctx'))
- grad_w_query: float32 [2, 1024, 1024], P(None, ('fsdp', 'ctx'), 'tp')
- grad_w_key: float32 [2, 1024, 1024], P(None, ('fsdp', 'ctx'), 'tp')
- grad_w_value: float32 [2, 1024, 1024], P(None, ('fsdp', 'ctx'), 'tp')
- grad_w_out: float32 [2, 1024, 1024], P(None, 'tp', ('fsdp', 'ctx'))
- grad_mlp_gain: float32 [2, 1024], P(None, ('fsdp', 'ctx'))
- grad_w_gate: float32 [2, 1024, 2816], P(None, ('fsdp', 'ctx'), 'tp')
- grad_w_up: float32 [2, 1024, 2816], P(None, ('fsdp', 'ctx'), 'tp')
- grad_w_down: float32 [2, 2816, 1024], P(None, 'tp', ('fsdp', 'ctx'))
Inputs may be any that keep to these rules, and one draw needn't show every extreme that they name: `segment_ids`: along a row the numbers never fall; each sequence holds 1 to 1024 positions and some sequence holds exactly 1024. `owner_order`: each row is a permutation of the positions of its pack. With n = 4, owner slots c * 512 + s * 512 / n + g (g below 512 / n) hold positions from s * 512 to (s + 1) * 512 - 1.
All inputs are finite; a program needn't handle non-finite values.
Results may differ from a plain program's by a relative error of at most 0.02.
Values may be sent and summed in bfloat16 or wider, within the bound.
No kernel may reach another device: no remote copies, remote signals or barrier semaphores. Data moves between devices by JAX's collectives and lax.ppermute only.
A program may use at most 320 MiB of HBM per device.

v0:
```python
import jax
import jax.numpy as jnp
from jax import lax
from jax.sharding import PartitionSpec as P

HEAD = 64
LAYERS = 2


EPS = 1e-05
THETA = 10000.0
NEG = -1e30


def seq_positions(segment):
    index_all = jnp.arange(segment.shape[0], dtype=jnp.int32)
    run_start = jnp.concatenate([jnp.ones((1,), dtype=bool), segment[1:] != segment[:-1]])
    run_first = lax.cummax(jnp.where(run_start, index_all, jnp.zeros_like(index_all)), axis=0)
    return index_all - run_first


def rope_tables(positions):
    frequency = THETA ** (-(jnp.arange(HEAD // 2, dtype=jnp.float32) * 2.0 / HEAD))
    angles = positions.astype(jnp.float32)[:, None] * frequency[None, :]
    return (jnp.cos(angles), jnp.sin(angles))


def rotate(values, cos_tab, sine_tab):
    row_count = values.shape[0]
    by_head = values.reshape(row_count, -1, HEAD)
    first_half = by_head[:, :, : HEAD // 2]
    second_half = by_head[:, :, HEAD // 2 :]
    cos_wide = cos_tab[:, None, :]
    sine_wide = sine_tab[:, None, :]
    turned = jnp.concatenate(
        [
            first_half * cos_wide - second_half * sine_wide,
            second_half * cos_wide + first_half * sine_wide,
        ],
        axis=2,
    )
    return turned.reshape(row_count, -1)


def norm_scale(stream):
    return lax.rsqrt(jnp.mean(stream * stream, axis=-1, keepdims=True) + EPS)


def norm_back(stream, inv_scale, gain, grad_normed):
    weighted = grad_normed * gain.astype(jnp.float32)
    grad_gain = jnp.sum(grad_normed * stream * inv_scale, axis=0)
    grad_stream = inv_scale * weighted - stream * inv_scale**3 * jnp.mean(
        weighted * stream, axis=1, keepdims=True
    )
    return (grad_gain, grad_stream)


def head_total(values):
    return lax.psum(values, "tp")


def input_total(values):
    return lax.psum(values, "tp")


def gather_layer(shards, level_idx):
    return (
        lax.all_gather(shards[0][level_idx], ("fsdp", "ctx"), axis=0, tiled=True),
        lax.all_gather(shards[1][level_idx], ("fsdp", "ctx"), axis=0, tiled=True),
        lax.all_gather(shards[2][level_idx], ("fsdp", "ctx"), axis=0, tiled=True),
        lax.all_gather(shards[3][level_idx], ("fsdp", "ctx"), axis=0, tiled=True),
        lax.all_gather(shards[4][level_idx], ("fsdp", "ctx"), axis=1, tiled=True),
        lax.all_gather(shards[5][level_idx], ("fsdp", "ctx"), axis=0, tiled=True),
        lax.all_gather(shards[6][level_idx], ("fsdp", "ctx"), axis=0, tiled=True),
        lax.all_gather(shards[7][level_idx], ("fsdp", "ctx"), axis=0, tiled=True),
        lax.all_gather(shards[8][level_idx], ("fsdp", "ctx"), axis=1, tiled=True),
    )


def gather_again(shards, level_idx):
    return (
        lax.all_gather(shards[0][level_idx], ("fsdp", "ctx"), axis=0, tiled=True),
        lax.all_gather(shards[1][level_idx], ("fsdp", "ctx"), axis=0, tiled=True),
        lax.all_gather(shards[2][level_idx], ("fsdp", "ctx"), axis=0, tiled=True),
        lax.all_gather(shards[3][level_idx], ("fsdp", "ctx"), axis=0, tiled=True),
        lax.all_gather(shards[4][level_idx], ("fsdp", "ctx"), axis=1, tiled=True),
        lax.all_gather(shards[5][level_idx], ("fsdp", "ctx"), axis=0, tiled=True),
        lax.all_gather(shards[6][level_idx], ("fsdp", "ctx"), axis=0, tiled=True),
        lax.all_gather(shards[7][level_idx], ("fsdp", "ctx"), axis=0, tiled=True),
        lax.all_gather(shards[8][level_idx], ("fsdp", "ctx"), axis=1, tiled=True),
    )


def attend(queries, keys_all, values_all, visible):
    inv_root = HEAD ** (-0.5)
    head_outs = []
    log_totals = []
    for head_idx in range(queries.shape[1] // HEAD):
        start_col = head_idx * HEAD
        query_head = queries[:, start_col : start_col + HEAD]
        key_head = keys_all[:, start_col : start_col + HEAD]
        value_head = values_all[:, start_col : start_col + HEAD]
        scores = (
            jnp.einsum("qd,kd->qk", query_head, key_head, preferred_element_type=jnp.float32)
            * inv_root
        )
        scores = jnp.where(visible, scores, NEG)
        row_peak = jnp.max(scores, axis=1, keepdims=True)
        exp_scores = jnp.exp(scores - row_peak)
        row_total = jnp.sum(exp_scores, axis=1, keepdims=True)
        probs = (exp_scores / row_total).astype(jnp.bfloat16)
        head_outs.append(jnp.dot(probs, value_head, preferred_element_type=jnp.float32))
        log_totals.append(row_peak + jnp.log(row_total))
    return (jnp.concatenate(head_outs, axis=1), jnp.concatenate(log_totals, axis=1))


def attend_back(queries, keys_all, values_all, visible, log_totals, grad_out):
    inv_root = HEAD ** (-0.5)
    grad_query_list = []
    grad_key_list = []
    grad_value_list = []
    for head_idx in range(queries.shape[1] // HEAD):
        start_col = head_idx * HEAD
        query_head = queries[:, start_col : start_col + HEAD]
        key_head = keys_all[:, start_col : start_col + HEAD]
        value_head = values_all[:, start_col : start_col + HEAD]
        grad_head = grad_out[:, start_col : start_col + HEAD]
        scores = (
            jnp.einsum("qd,kd->qk", query_head, key_head, preferred_element_type=jnp.float32)
            * inv_root
        )
        scores = jnp.where(visible, scores, NEG)
        probs = jnp.exp(scores - log_totals[:, head_idx : head_idx + 1])
        grad_probs = jnp.einsum(
            "qd,kd->qk", grad_head, value_head, preferred_element_type=jnp.float32
        )
        inner_sum = jnp.sum(probs * grad_probs, axis=1, keepdims=True)
        grad_scores = (probs * (grad_probs - inner_sum)).astype(jnp.bfloat16)
        grad_query_list.append(
            jnp.dot(grad_scores, key_head, preferred_element_type=jnp.float32) * inv_root
        )
        grad_key_list.append(
            jnp.einsum("qk,qd->kd", grad_scores, query_head, preferred_element_type=jnp.float32)
            * inv_root
        )
        grad_value_list.append(
            jnp.einsum(
                "qk,qd->kd",
                probs.astype(jnp.bfloat16),
                grad_head,
                preferred_element_type=jnp.float32,
            )
        )
    return (
        jnp.concatenate(grad_query_list, axis=1),
        jnp.concatenate(grad_key_list, axis=1),
        jnp.concatenate(grad_value_list, axis=1),
    )


def forward_layer(stream, weights_full, first_values, visible, cos_tab, sine_tab):
    gain_attn, wq_full, wk_full, wv_full, wo_full, gain_mlp, wg_full, wu_full, wd_full = (
        weights_full
    )
    scale_attn = norm_scale(stream)
    normed = (stream * scale_attn * gain_attn.astype(jnp.float32)).astype(jnp.bfloat16)
    queries = rotate(
        jnp.dot(normed, wq_full, preferred_element_type=jnp.float32), cos_tab, sine_tab
    ).astype(jnp.bfloat16)
    keys_own = rotate(
        jnp.dot(normed, wk_full, preferred_element_type=jnp.float32), cos_tab, sine_tab
    ).astype(jnp.bfloat16)
    values_pre = jnp.dot(normed, wv_full, preferred_element_type=jnp.float32)
    if first_values is None:
        mixed_values = values_pre
    else:
        mixed_values = 0.5 * values_pre + 0.5 * first_values
    keys_all, values_all = (
        lax.all_gather(keys_own, "ctx", axis=0, tiled=True),
        lax.all_gather(mixed_values.astype(jnp.bfloat16), "ctx", axis=0, tiled=True),
    )
    attended, log_totals = attend(queries, keys_all, values_all, visible)
    attended = attended.astype(jnp.bfloat16)
    middle = stream + head_total(jnp.dot(attended, wo_full, preferred_element_type=jnp.float32))
    scale_mlp = norm_scale(middle)
    normed_mlp = (middle * scale_mlp * gain_mlp.astype(jnp.float32)).astype(jnp.bfloat16)
    gate_pre = jnp.dot(normed_mlp, wg_full, preferred_element_type=jnp.float32)
    upward = jnp.dot(normed_mlp, wu_full, preferred_element_type=jnp.float32)
    hidden = (gate_pre * jax.nn.sigmoid(gate_pre) * upward).astype(jnp.bfloat16)
    result = middle + head_total(jnp.dot(hidden, wd_full, preferred_element_type=jnp.float32))
    kept_state = (
        stream,
        scale_attn,
        normed,
        queries,
        keys_all,
        values_all,
        log_totals,
        attended,
        middle,
        scale_mlp,
        normed_mlp,
        gate_pre,
        upward,
        hidden,
    )
    return (result, kept_state, values_pre)


def backward_layer(
    grad_stream, kept_state, weights_full, visible, cos_tab, sine_tab, mix_factor, extra_grad
):
    (
        stream,
        scale_attn,
        normed,
        queries,
        keys_all,
        values_all,
        log_totals,
        attended,
        middle,
        scale_mlp,
        normed_mlp,
        gate_pre,
        upward,
        hidden,
    ) = kept_state
    gain_attn, wq_full, wk_full, wv_full, wo_full, gain_mlp, wg_full, wu_full, wd_full = (
        weights_full
    )
    grad_branch = grad_stream.astype(jnp.bfloat16)
    grad_wdown = jnp.einsum("tf,td->fd", hidden, grad_branch, preferred_element_type=jnp.float32)
    grad_hidden = jnp.einsum("td,fd->tf", grad_branch, wd_full, preferred_element_type=jnp.float32)
    sigmoid_gate = jax.nn.sigmoid(gate_pre)
    grad_gate = (
        grad_hidden * upward * sigmoid_gate * (1.0 + gate_pre * (1.0 - sigmoid_gate))
    ).astype(jnp.bfloat16)
    grad_upward = (grad_hidden * gate_pre * sigmoid_gate).astype(jnp.bfloat16)
    grad_wgate = jnp.einsum("td,tf->df", normed_mlp, grad_gate, preferred_element_type=jnp.float32)
    grad_wup = jnp.einsum("td,tf->df", normed_mlp, grad_upward, preferred_element_type=jnp.float32)
    grad_normed_mlp = input_total(
        jnp.einsum("tf,df->td", grad_gate, wg_full, preferred_element_type=jnp.float32)
        + jnp.einsum("tf,df->td", grad_upward, wu_full, preferred_element_type=jnp.float32)
    )
    grad_gain_mlp, grad_middle_norm = norm_back(middle, scale_mlp, gain_mlp, grad_normed_mlp)
    grad_middle = grad_stream + grad_middle_norm
    grad_attn_out = grad_middle.astype(jnp.bfloat16)
    grad_wout = jnp.einsum("th,td->hd", attended, grad_attn_out, preferred_element_type=jnp.float32)
    grad_attended = jnp.einsum(
        "td,hd->th", grad_attn_out, wo_full, preferred_element_type=jnp.float32
    ).astype(jnp.bfloat16)
    grad_queries, grad_keys_all, grad_values_all = attend_back(
        queries, keys_all, values_all, visible, log_totals, grad_attended
    )
    grad_keys, grad_values = (
        lax.psum_scatter(grad_keys_all, "ctx", scatter_dimension=0, tiled=True),
        lax.psum_scatter(grad_values_all, "ctx", scatter_dimension=0, tiled=True),
    )
    grad_query_pre = rotate(grad_queries, cos_tab, -sine_tab).astype(jnp.bfloat16)
    grad_key_pre = rotate(grad_keys, cos_tab, -sine_tab).astype(jnp.bfloat16)
    grad_value_pre = (mix_factor * grad_values + extra_grad).astype(jnp.bfloat16)
    grad_wquery = jnp.einsum(
        "td,th->dh", normed, grad_query_pre, preferred_element_type=jnp.float32
    )
    grad_wkey = jnp.einsum("td,th->dh", normed, grad_key_pre, preferred_element_type=jnp.float32)
    grad_wvalue = jnp.einsum(
        "td,th->dh", normed, grad_value_pre, preferred_element_type=jnp.float32
    )
    grad_normed = input_total(
        jnp.einsum("th,dh->td", grad_query_pre, wq_full, preferred_element_type=jnp.float32)
        + jnp.einsum("th,dh->td", grad_key_pre, wk_full, preferred_element_type=jnp.float32)
        + jnp.einsum("th,dh->td", grad_value_pre, wv_full, preferred_element_type=jnp.float32)
    )
    grad_gain_attn, grad_input_norm = norm_back(stream, scale_attn, gain_attn, grad_normed)
    grad_list = (
        grad_gain_attn,
        grad_wquery,
        grad_wkey,
        grad_wvalue,
        grad_wout,
        grad_gain_mlp,
        grad_wgate,
        grad_wup,
        grad_wdown,
    )
    return (grad_middle + grad_input_norm, grad_list, grad_values)


def local(
    tokens,
    out_grad,
    segment_ids,
    owner_order,
    attn_gain,
    w_query,
    w_key,
    w_value,
    w_out,
    mlp_gain,
    w_gate,
    w_up,
    w_down,
):
    shards = (attn_gain, w_query, w_key, w_value, w_out, mlp_gain, w_gate, w_up, w_down)
    ctx_size = lax.axis_size("ctx")
    ctx_index = lax.axis_index("ctx")
    tok_rows = tokens.shape[0]
    group_rows = tok_rows // ctx_size
    owner_rows = owner_order[0]
    segment = segment_ids[0]
    owner_grid = owner_rows.reshape(ctx_size, ctx_size, group_rows)
    local_rows = (
        lax.dynamic_index_in_dim(owner_grid, ctx_index, 1, False) - ctx_index * tok_rows
    ).reshape(tok_rows)
    stream_in, grad_in = (
        lax.all_to_all(tokens[local_rows], "ctx", split_axis=0, concat_axis=0, tiled=True),
        lax.all_to_all(out_grad[local_rows], "ctx", split_axis=0, concat_axis=0, tiled=True),
    )
    own_natural = lax.dynamic_slice_in_dim(owner_rows, ctx_index * tok_rows, tok_rows, 0)
    positions = seq_positions(segment)
    cos_tab, sine_tab = rope_tables(positions[own_natural])
    seg_query = segment[own_natural]
    seg_key = segment[owner_rows]
    visible = (seg_query[:, None] == seg_key[None, :]) & (
        owner_rows[None, :] <= own_natural[:, None]
    )
    stream = stream_in.astype(jnp.float32)
    first_values = None
    kept_layers = []
    fetched = []
    for level_idx in range(LAYERS):
        weights_full = gather_layer(shards, level_idx)
        fetched.append(weights_full)
        stream, kept_state, values_pre = forward_layer(
            stream, weights_full, first_values, visible, cos_tab, sine_tab
        )
        if first_values is None:
            first_values = values_pre
        kept_layers.append(kept_state)
    grad_stream = grad_in.astype(jnp.float32)
    carried = jnp.zeros_like(first_values)
    layer_grads = [None] * LAYERS
    for level_idx in reversed(range(LAYERS)):
        weights_full = gather_again(shards, level_idx)
        if level_idx > 0:
            grad_stream, grad_list, grad_values = backward_layer(
                grad_stream,
                kept_layers[level_idx],
                weights_full,
                visible,
                cos_tab,
                sine_tab,
                0.5,
                0.0,
            )
            carried = 0.5 * grad_values
        else:
            grad_stream, grad_list, grad_values = backward_layer(
                grad_stream,
                kept_layers[level_idx],
                weights_full,
                visible,
                cos_tab,
                sine_tab,
                1.0,
                carried,
            )
        layer_grads[level_idx] = (
            lax.psum_scatter(grad_list[0], ("fsdp", "ctx"), scatter_dimension=0, tiled=True),
            lax.psum_scatter(grad_list[1], ("fsdp", "ctx"), scatter_dimension=0, tiled=True),
            lax.psum_scatter(grad_list[2], ("fsdp", "ctx"), scatter_dimension=0, tiled=True),
            lax.psum_scatter(grad_list[3], ("fsdp", "ctx"), scatter_dimension=0, tiled=True),
            lax.psum_scatter(grad_list[4], ("fsdp", "ctx"), scatter_dimension=1, tiled=True),
            lax.psum_scatter(grad_list[5], ("fsdp", "ctx"), scatter_dimension=0, tiled=True),
            lax.psum_scatter(grad_list[6], ("fsdp", "ctx"), scatter_dimension=0, tiled=True),
            lax.psum_scatter(grad_list[7], ("fsdp", "ctx"), scatter_dimension=0, tiled=True),
            lax.psum_scatter(grad_list[8], ("fsdp", "ctx"), scatter_dimension=1, tiled=True),
        )
    stacked = [
        jnp.stack([layer_grads[level_idx][member_idx] for level_idx in range(LAYERS)])
        for member_idx in range(9)
    ]
    returned = lax.all_to_all(
        stream.astype(jnp.bfloat16), "ctx", split_axis=0, concat_axis=0, tiled=True
    ).astype(stream.dtype)
    outputs = jnp.zeros_like(returned).at[local_rows].set(returned).astype(jnp.bfloat16)
    return (
        outputs,
        grad_stream,
        stacked[0],
        stacked[1],
        stacked[2],
        stacked[3],
        stacked[4],
        stacked[5],
        stacked[6],
        stacked[7],
        stacked[8],
    )


def solution(mesh):
    return jax.shard_map(
        local,
        mesh=mesh,
        in_specs=(
            P(("fsdp", "ctx"), None),
            P(("fsdp", "ctx"), None),
            P("fsdp", None),
            P("fsdp", None),
            P(None, ("fsdp", "ctx")),
            P(None, ("fsdp", "ctx"), "tp"),
            P(None, ("fsdp", "ctx"), "tp"),
            P(None, ("fsdp", "ctx"), "tp"),
            P(None, "tp", ("fsdp", "ctx")),
            P(None, ("fsdp", "ctx")),
            P(None, ("fsdp", "ctx"), "tp"),
            P(None, ("fsdp", "ctx"), "tp"),
            P(None, "tp", ("fsdp", "ctx")),
        ),
        out_specs=(
            P(("fsdp", "ctx"), None),
            P(("fsdp", "ctx"), None),
            P(None, ("fsdp", "ctx")),
            P(None, ("fsdp", "ctx"), "tp"),
            P(None, ("fsdp", "ctx"), "tp"),
            P(None, ("fsdp", "ctx"), "tp"),
            P(None, "tp", ("fsdp", "ctx")),
            P(None, ("fsdp", "ctx")),
            P(None, ("fsdp", "ctx"), "tp"),
            P(None, ("fsdp", "ctx"), "tp"),
            P(None, "tp", ("fsdp", "ctx")),
        ),
        check_vma=False,
    )
```

profile of v0, /device:TPU:0, one launch (start us, length us, event | category | flops | bytes accessed | tf_op | source)
XLA Modules:
  0.0 1880.4 jit_solution(18176849382622210009)
XLA Ops:
  12.2 5.3 all-to-all-start
  18.8 20.6 %all-gather = bf16[1,1024]{1,0:T(2,128)(2,1)S(1)} all-gather(bf16[1,128]{1,0:T(2,128)(2,1)S(1)} %get-tuple-element.90), channel_id=2, replica_groups=mesh['fsdp'=2,'ctx'=4,'tp'=4] {'fsdp','ctx'}, dimensions={1}, use_global_device_ids=true | all-gather | bytes 2304 | tf_op jit(solution)/shard_map/all_gather | solution.py:68
  40.1 4.3 gather_fusion.1
  47.6 20.4 %gather_fusion.2 = s32[2048]{0:T(1024)} fusion(s32[2048]{0:T(1024)S(1)} %bitcast.240, s32[2048]{0:T(1024)S(1)} %broadcast_clamp_fusion), kind=kCustom, calls=%fused_computation.2 | custom fusion | bytes 24576 | tf_op jit(solution)/shard_map/gather | solution.py:324
  68.0 26.1 %all-gather.1 = bf16[1,1024,256]{2,1,0:T(8,128)(2,1)S(1)} all-gather(bf16[1,128,256]{2,1,0:T(8,128)(2,1)S(1)} %get-tuple-element.69), channel_id=3, replica_groups=mesh['fsdp'=2,'ctx'=4,'tp'=4] {'fsdp','ctx'}, dimensions={1}, use_global_device_ids=true | all-gather | bytes 589824 | tf_op jit(solution)/shard_map/all_gather | solution.py:69
  94.3 25.1 %all-gather.2 = bf16[1,1024,256]{2,1,0:T(8,128)(2,1)S(1)} all-gather(bf16[1,128,256]{2,1,0:T(8,128)(2,1)S(1)} %get-tuple-element.71), channel_id=4, replica_groups=mesh['fsdp'=2,'ctx'=4,'tp'=4] {'fsdp','ctx'}, dimensions={1}, use_global_device_ids=true | all-gather | bytes 589824 | tf_op jit(solution)/shard_map/all_gather | solution.py:70
  124.5 23.3 %all-gather.4 = bf16[1,256,1024]{2,1,0:T(8,128)(2,1)S(1)} all-gather(bf16[1,256,128]{2,1,0:T(8,128)(2,1)S(1)} %get-tuple-element.73), channel_id=6, replica_groups=mesh['fsdp'=2,'ctx'=4,'tp'=4] {'fsdp','ctx'}, dimensions={2}, use_global_device_ids=true | all-gather | bytes 589824 | tf_op jit(solution)/shard_map/all_gather | solution.py:72
  147.8 25.7 %all-gather.3 = bf16[1,1024,256]{2,1,0:T(8,128)(2,1)S(1)} all-gather(bf16[1,128,256]{2,1,0:T(8,128)(2,1)S(1)} %get-tuple-element.65), channel_id=5, replica_groups=mesh['fsdp'=2,'ctx'=4,'tp'=4] {'fsdp','ctx'}, dimensions={1}, use_global_device_ids=true | all-gather | bytes 589824 | tf_op jit(solution)/shard_map/all_gather | solution.py:71
  189.9 12.7 all-gather.31.cloned.1.call-done
  217.0 14.1 all-gather.5
  231.1 69.1 %all-reduce.14.cloned.1.call-done = f32[512,1024]{1,0:T(8,128)} async-done(((f32[512,1024]{1,0:T(8,128)}), f32[512,1024]{1,0:T(8,128)}) %all-reduce.14.cloned.1.call-update) | async-done | bytes 2097168 | tf_op jit(solution)/shard_map/psum | solution.py:59
  306.9 4.1 multiply_convert_fusion.16
  315.6 13.7 all-gather.9
  329.3 27.2 %all-gather.11 = bf16[1,1024,256]{2,1,0:T(8,128)(2,1)} all-gather(bf16[1,128,256]{2,1,0:T(8,128)(2,1)S(1)} %get-tuple-element.70), channel_id=13, replica_groups=mesh['fsdp'=2,'ctx'=4,'tp'=4] {'fsdp','ctx'}, dimensions={1}, use_global_device_ids=true | all-gather | bytes 589824 | tf_op jit(solution)/shard_map/all_gather | solution.py:70
  356.5 27.3 %all-gather.10 = bf16[1,1024,256]{2,1,0:T(8,128)(2,1)} all-gather(bf16[1,128,256]{2,1,0:T(8,128)(2,1)S(1)} %get-tuple-element.68), channel_id=12, replica_groups=mesh['fsdp'=2,'ctx'=4,'tp'=4] {'fsdp','ctx'}, dimensions={1}, use_global_device_ids=true | all-gather | bytes 589824 | tf_op jit(solution)/shard_map/all_gather | solution.py:69
  383.9 16.4 all-reduce.16.cloned.1.call-done
  405.7 23.5 %all-gather.13 = bf16[1,256,1024]{2,1,0:T(8,128)(2,1)S(1)} all-gather(bf16[1,256,128]{2,1,0:T(8,128)(2,1)S(1)} %copy-done.114), channel_id=15, replica_groups=mesh['fsdp'=2,'ctx'=4,'tp'=4] {'fsdp','ctx'}, dimensions={2}, use_global_device_ids=true | all-gather | bytes 589824 | tf_op jit(solution)/shard_map/all_gather | solution.py:72
  429.1 25.2 %all-gather.12 = bf16[1,1024,256]{2,1,0:T(8,128)(2,1)S(1)} all-gather(bf16[1,128,256]{2,1,0:T(8,128)(2,1)S(1)} %copy-done.113), channel_id=14, replica_groups=mesh['fsdp'=2,'ctx'=4,'tp'=4] {'fsdp','ctx'}, dimensions={1}, use_global_device_ids=true | all-gather | bytes 589824 | tf_op jit(solution)/shard_map/all_gather | solution.py:71
  470.1 12.4 all-gather.35.cloned.1.call-done
  502.5 24.3 %all-gather.14 = bf16[1,1024]{1,0:T(2,128)(2,1)S(1)} all-gather(bf16[1,128]{1,0:T(2,128)(2,1)S(1)} %copy-done.172), channel_id=16, replica_groups=mesh['fsdp'=2,'ctx'=4,'tp'=4] {'fsdp','ctx'}, dimensions={1}, use_global_device_ids=true | all-gather | bytes 2304 | tf_op jit(solution)/shard_map/all_gather | solution.py:73
  526.8 53.2 %all-reduce.18.cloned.1.call-done = f32[512,1024]{1,0:T(8,128)} async-done(((f32[512,1024]{1,0:T(8,128)}), f32[512,1024]{1,0:T(8,128)}) %all-reduce.18.cloned.1.call-update) | async-done | bytes 2097168 | tf_op jit(solution)/shard_map/psum | solution.py:59
  591.4 4.7 multiply_convert_fusion.13
  600.4 85.2 %all-reduce.20.cloned.1.call-done = f32[512,1024]{1,0:T(8,128)} async-done(((f32[512,1024]{1,0:T(8,128)}), f32[512,1024]{1,0:T(8,128)}) %all-reduce.20.cloned.1.call-update) | async-done | bytes 2097168 | tf_op jit(solution)/shard_map/psum | solution.py:63
  730.7 14.0 reduce-scatter.19.cloned.1.call-done
  749.9 32.8 %reduce-scatter.21.cloned.1.call-done = f32[512,256]{1,0:T(8,128)} async-done(((f32[2048,256]{1,0:T(8,128)}), f32[512,256]{1,0:T(8,128)}) %reduce-scatter.21.cloned.1.call-update) | async-done | bytes 524304 | tf_op jit(solution)/shard_map/reduce_scatter | solution.py:258
  782.7 4.4 add_add_fusion.1
  787.6 85.8 %all-reduce.22.cloned.1.call-done = f32[512,1024]{1,0:T(8,128)} async-done(((f32[512,1024]{1,0:T(8,128)}), f32[512,1024]{1,0:T(8,128)}) %all-reduce.22.cloned.1.call-update) | async-done | bytes 2097168 | tf_op jit(solution)/shard_map/psum | solution.py:63
  886.9 84.0 %all-reduce.24.cloned.1.call-done = f32[512,1024]{1,0:T(8,128)} async-done(((f32[512,1024]{1,0:T(8,128)}), f32[512,1024]{1,0:T(8,128)}) %all-reduce.24.cloned.1.call-update) | async-done | bytes 2097168 | tf_op jit(solution)/shard_map/psum | solution.py:63
  1020.3 4.2 fusion.120
  1034.3 4.1 fusion.234
  1081.5 17.2 reduce-scatter.41.cloned.1.call-done
  1098.7 39.0 %reduce-scatter.39.cloned.1.call-done = f32[256,128]{1,0:T(8,128)} async-done(((f32[256,1024]{1,0:T(8,128)}), f32[256,128]{1,0:T(8,128)}) %reduce-scatter.39.cloned.1.call-update) | async-done | bytes 131088 | tf_op jit(solution)/shard_map/reduce_scatter | solution.py:374
  1139.4 46.3 %reduce-scatter.53.cloned.1.call-done = f32[704,128]{1,0:T(8,128)} async-done(((f32[704,1024]{1,0:T(8,128)}), f32[704,128]{1,0:T(8,128)}) %reduce-scatter.53.cloned.1.call-update) | async-done | bytes 360464 | tf_op jit(solution)/shard_map/reduce_scatter | solution.py:378
  1185.7 48.0 %reduce-scatter.51.cloned.1.call-done = f32[704,128]{1,0:T(8,128)} async-done(((f32[704,1024]{1,0:T(8,128)}), f32[704,128]{1,0:T(8,128)}) %reduce-scatter.51.cloned.1.call-update) | async-done | bytes 360464 | tf_op jit(solution)/shard_map/reduce_scatter | solution.py:378
  1235.6 46.1 %reduce-scatter.49.cloned.1.call-done = f32[128,704]{0,1:T(8,128)} async-done(((f32[1024,704]{0,1:T(8,128)}), f32[128,704]{0,1:T(8,128)}) %reduce-scatter.49.cloned.1.call-update) | async-done | bytes 360464 | tf_op jit(solution)/shard_map/reduce_scatter | solution.py:377
  1281.8 48.0 %reduce-scatter.47.cloned.1.call-done = f32[128,704]{0,1:T(8,128)} async-done(((f32[1024,704]{0,1:T(8,128)}), f32[128,704]{0,1:T(8,128)}) %reduce-scatter.47.cloned.1.call-update) | async-done | bytes 360464 | tf_op jit(solution)/shard_map/reduce_scatter | solution.py:377
  1331.7 46.1 %reduce-scatter.45.cloned.1.call-done = f32[128,704]{0,1:T(8,128)} async-done(((f32[1024,704]{0,1:T(8,128)}), f32[128,704]{0,1:T(8,128)}) %reduce-scatter.45.cloned.1.call-update) | async-done | bytes 360464 | tf_op jit(solution)/shard_map/reduce_scatter | solution.py:376
  1377.9 48.1 %reduce-scatter.43.cloned.1.call-done = f32[128,704]{0,1:T(8,128)} async-done(((f32[1024,704]{0,1:T(8,128)}), f32[128,704]{0,1:T(8,128)}) %reduce-scatter.43.cloned.1.call-update) | async-done | bytes 360464 | tf_op jit(solution)/shard_map/reduce_scatter | solution.py:376
  1428.0 37.2 %reduce-scatter.37.cloned.1.call-done = f32[128,256]{1,0:T(8,128)} async-done(((f32[1024,256]{1,0:T(8,128)}), f32[128,256]{1,0:T(8,128)}) %reduce-scatter.37.cloned.1.call-update) | async-done | bytes 131088 | tf_op jit(solution)/shard_map/reduce_scatter | solution.py:373
  1465.2 39.0 %reduce-scatter.35.cloned.1.call-done = f32[128,256]{1,0:T(8,128)} async-done(((f32[1024,256]{1,0:T(8,128)}), f32[128,256]{1,0:T(8,128)}) %reduce-scatter.35.cloned.1.call-update) | async-done | bytes 131088 | tf_op jit(solution)/shard_map/reduce_scatter | solution.py:373
  1505.9 37.5 %reduce-scatter.33.cloned.1.call-done = f32[128,256]{1,0:T(8,128)} async-done(((f32[1024,256]{1,0:T(8,128)}), f32[128,256]{1,0:T(8,128)}) %reduce-scatter.33.cloned.1.call-update) | async-done | bytes 131088 | tf_op jit(solution)/shard_map/reduce_scatter | solution.py:372
  1543.4 39.0 %reduce-scatter.31.cloned.1.call-done = f32[128,256]{1,0:T(8,128)} async-done(((f32[1024,256]{1,0:T(8,128)}), f32[128,256]{1,0:T(8,128)}) %reduce-scatter.31.cloned.1.call-update) | async-done | bytes 131088 | tf_op jit(solution)/shard_map/reduce_scatter | solution.py:372
  1584.1 37.4 %reduce-scatter.29.cloned.1.call-done = f32[128,256]{1,0:T(8,128)} async-done(((f32[1024,256]{1,0:T(8,128)}), f32[128,256]{1,0:T(8,128)}) %reduce-scatter.29.cloned.1.call-update) | async-done | bytes 131088 | tf_op jit(solution)/shard_map/reduce_scatter | solution.py:371
  1621.5 39.2 %reduce-scatter.27.cloned.1.call-done = f32[128,256]{1,0:T(8,128)} async-done(((f32[1024,256]{1,0:T(8,128)}), f32[128,256]{1,0:T(8,128)}) %reduce-scatter.27.cloned.1.call-update) | async-done | bytes 131088 | tf_op jit(solution)/shard_map/reduce_scatter | solution.py:371
  1662.4 156.3 %all-reduce.26.cloned.1.call-done = (f32[512,1024]{1,0:T(8,128)}, f32[512,1024]{1,0:T(8,128)}) async-done(((f32[512,1024]{1,0:T(8,128)}, f32[512,1024]{1,0:T(8,128)}), (f32[512,1024]{1,0:T(8,128)}, f32[512,1024]{1,0:T(8,128)})) %all-reduce.26.cloned.1.call-update) | async-done | bytes 4194320 | tf_op jit(solution)/shard_map/psum | solution.py:59
  1822.6 26.5 %all-reduce.4 = (f32[1024]{0:T(1024)S(1)}, f32[1024]{0:T(1024)S(1)}, f32[1024]{0:T(1024)S(1)}, f32[1024]{0:T(1024)S(1)}) all-reduce(f32[1024]{0:T(1024)S(1)} %copy-done.145, f32[1024]{0:T(1024)S(1)} %get-tuple-element.17, f32[1024]{0:T(1024)S(1)} %copy-done.144, ...), channel_id=25, replica_groups=mesh['fsdp'=2,'ctx'=4,'tp'=4] {'fsdp','ctx'}, use_global_device_ids=true, to_apply=%region_50.51.clone | all-reduce | flops 4096 | bytes 32768
  1849.3 4.2 all-to-all-start.1
  1858.2 10.1 all-to-all-done.1
  (653 shorter events, 303.3 us)
Async XLA Ops:
  12.2 108.3 %all-to-all-start = ((bf16[4,128,1024]{2,1,0:T(8,128)(2,1)}), bf16[4,128,1024]{2,1,0:T(8,128)(2,1)S(1)}, u32[]{:S(2)}, u32[]{:S(2)}) async-start(bf16[4,128,1024]{2,1,0:T(8,128)(2,1)} %bitcast.3), calls=%async_computation | async-start | bytes 2097152 | tf_op jit(solution)/shard_map/all_to_all | solution.py:317
  17.6 157.9 %all-gather.29.cloned.1.call-start = ((), (), s32[]{:S(2)}) async-start(), calls=%async_computation.21 | async-start | bytes 1310720 | tf_op jit(solution)/shard_map/all_gather | solution.py:179
  39.4 134.1 %copy-start.131 = (f32[1,1024]{1,0:T(1,128)}, f32[1,1024]{1,0:T(1,128)S(1)}, u32[]{:S(2)}) copy-start(f32[1,1024]{1,0:T(1,128)S(1)} %convert_element_type.311) | copy-start | bytes 12292
  120.5 53.0 %copy-start.37 = (bf16[4,128,1024]{2,1,0:T(8,128)(2,1)}, bf16[4,128,1024]{2,1,0:T(8,128)(2,1)S(1)}, u32[]{:S(2)}) copy-start(bf16[4,128,1024]{2,1,0:T(8,128)(2,1)S(1)} %all-to-all-done) | copy-start | bytes 3145732
  120.9 52.7 %copy-start.133 = (f32[512]{0:T(512)}, f32[512]{0:T(512)S(1)}, u32[]{:S(2)}) copy-start(f32[512]{0:T(512)S(1)} %get-tuple-element.85) | copy-start | bytes 6148
  123.1 79.5 %all-gather.31.cloned.1.call-start = ((), (), s32[]{:S(2)}) async-start(), calls=%async_computation.22 | async-start | bytes 1310720 | tf_op jit(solution)/shard_map/all_gather | solution.py:180
  147.8 64.2 %copy-start.78 = (bf16[1,256,1024]{2,1,0:T(8,128)(2,1)}, bf16[1,256,1024]{2,1,0:T(8,128)(2,1)S(1)}, u32[]{:S(2)}) copy-start(bf16[1,256,1024]{2,1,0:T(8,128)(2,1)S(1)} %all-gather.4) | copy-start | bytes 1572868
  175.2 125.0 %all-reduce.14.cloned.1.call-start = ((), (), s32[]{:S(2)}) async-start(), calls=%async_computation.23 | async-start | bytes 4194304 | tf_op jit(solution)/shard_map/psum | solution.py:59
  213.9 86.3 %copy-start.38 = (bf16[4,128,1024]{2,1,0:T(8,128)(2,1)S(1)}, bf16[4,128,1024]{2,1,0:T(8,128)(2,1)}, u32[]{:S(2)}) copy-start(bf16[4,128,1024]{2,1,0:T(8,128)(2,1)} %copy-done.37) | copy-start | bytes 3145732
  213.9 89.2 %all-gather.37.cloned.1.call-start = ((), (), s32[]{:S(2)}) async-start(), calls=%async_computation.49 | async-start | bytes 1622016 | tf_op jit(solution)/shard_map/all_gather | solution.py:74
  214.8 92.1 %all-gather.39.cloned.1.call-start = ((), (), s32[]{:S(2)}) async-start(), calls=%async_computation.50 | async-start | bytes 1622016 | tf_op jit(solution)/shard_map/all_gather | solution.py:75
  215.6 95.4 %all-gather.41.cloned.1.call-start = ((), (), s32[]{:S(2)}) async-start(), calls=%async_computation.51 | async-start | bytes 1622016 | tf_op jit(solution)/shard_map/all_gather | solution.py:76
  216.5 183.8 %all-reduce.16.cloned.1.call-start = ((), (), s32[]{:S(2)}) async-start(), calls=%async_computation.24 | async-start | bytes 4194304 | tf_op jit(solution)/shard_map/psum | solution.py:59
  302.1 98.1 %copy-start.33 = (f32[512,1024]{1,0:T(8,128)}, f32[512,1024]{1,0:T(8,128)S(1)}, u32[]{:S(2)}) copy-start(f32[512,1024]{1,0:T(8,128)S(1)} %get-tuple-element.30) | copy-start | bytes 6291460
  315.0 141.4 %all-gather.33.cloned.1.call-start = ((), (), s32[]{:S(2)}) async-start(), calls=%async_computation.25 | async-start | bytes 1310720 | tf_op jit(solution)/shard_map/all_gather | solution.py:179
  405.6 76.9 %all-gather.35.cloned.1.call-start = ((), (), s32[]{:S(2)}) async-start(), calls=%async_computation.26 | async-start | bytes 1310720 | tf_op jit(solution)/shard_map/all_gather | solution.py:180
  405.6 50.8 %copy-start.141 = (s32[1,2048]{1,0:T(1,128)S(1)}, s32[1,2048]{1,0:T(1,128)}, u32[]{:S(2)}) copy-start(s32[1,2048]{1,0:T(1,128)} %param.16) | copy-start | bytes 24580
  429.1 62.7 %copy-start.84 = (bf16[1,256,1024]{2,1,0:T(8,128)(2,1)}, bf16[1,256,1024]{2,1,0:T(8,128)(2,1)S(1)}, u32[]{:S(2)}) copy-start(bf16[1,256,1024]{2,1,0:T(8,128)(2,1)S(1)} %all-gather.13) | copy-start | bytes 1572868
  456.3 123.8 %all-reduce.18.cloned.1.call-start = ((), (), s32[]{:S(2)}) async-start(), calls=%async_computation.27 | async-start | bytes 4194304 | tf_op jit(solution)/shard_map/psum | solution.py:59
  493.7 90.1 %all-gather.45.cloned.1.call-start = ((), (), s32[]{:S(2)}) async-start(), calls=%async_computation.53 | async-start | bytes 1622016 | tf_op jit(solution)/shard_map/all_gather | solution.py:75
  494.5 93.1 %all-gather.43.cloned.1.call-start = ((), (), s32[]{:S(2)}) async-start(), calls=%async_computation.52 | async-start | bytes 1622016 | tf_op jit(solution)/shard_map/all_gather | solution.py:74
  495.2 96.1 %all-gather.47.cloned.1.call-start = ((), (), s32[]{:S(2)}) async-start(), calls=%async_computation.54 | async-start | bytes 1622016 | tf_op jit(solution)/shard_map/all_gather | solution.py:76
  498.8 92.6 %all-to-all-start.2 = ((bf16[4,128,1024]{2,1,0:T(8,128)(2,1)}), bf16[4,128,1024]{2,1,0:T(8,128)(2,1)S(1)}, u32[]{:S(2)}, u32[]{:S(2)}) async-start(bf16[4,128,1024]{2,1,0:T(8,128)(2,1)} %bitcast.48), calls=%async_computation.2 | async-start | bytes 2097152 | tf_op jit(solution)/shard_map/all_to_all | solution.py:318
  502.4 183.2 %all-reduce.20.cloned.1.call-start = ((), (), s32[]{:S(2)}) async-start(), calls=%async_computation.28 | async-start | bytes 4194304 | tf_op jit(solution)/shard_map/psum | solution.py:63
  600.3 144.4 %reduce-scatter.19.cloned.1.call-start = ((), (), s32[]{:S(2)}) async-start(), calls=%async_computation.29 | async-start | bytes 2621440 | tf_op jit(solution)/shard_map/reduce_scatter | solution.py:257
  710.3 72.4 %reduce-scatter.21.cloned.1.call-start = ((), (), s32[]{:S(2)}) async-start(), calls=%async_computation.30 | async-start | bytes 2621440 | tf_op jit(solution)/shard_map/reduce_scatter | solution.py:258
  721.8 151.6 %all-reduce.22.cloned.1.call-start = ((), (), s32[]{:S(2)}) async-start(), calls=%async_computation.31 | async-start | bytes 4194304 | tf_op jit(solution)/shard_map/psum | solution.py:63
  787.1 183.7 %all-reduce.24.cloned.1.call-start = ((), (), s32[]{:S(2)}) async-start(), calls=%async_computation.32 | async-start | bytes 4194304 | tf_op jit(solution)/shard_map/psum | solution.py:63
  885.5 85.4 %copy-start.137 = (f32[512]{0:T(512)S(1)}, f32[512]{0:T(512)}, u32[]{:S(2)}) copy-start(f32[512]{0:T(512)} %copy-done.136) | copy-start | bytes 6148
  885.6 160.3 %reduce-scatter.25.cloned.1.call-start = ((), (), s32[]{:S(2)}) async-start(), calls=%async_computation.34 | async-start | bytes 2621440 | tf_op jit(solution)/shard_map/reduce_scatter | solution.py:258
  886.9 87.6 %copy-start.166 = (f32[512]{0:T(512)S(1)}, f32[512]{0:T(512)}, u32[]{:S(2)}) copy-start(f32[512]{0:T(512)} %get-tuple-element.79) | copy-start | bytes 6148
  987.2 73.9 %reduce-scatter.23.cloned.1.call-start = ((), (), s32[]{:S(2)}) async-start(), calls=%async_computation.33 | async-start | bytes 2621440 | tf_op jit(solution)/shard_map/reduce_scatter | solution.py:257
  1009.1 89.6 %reduce-scatter.41.cloned.1.call-start = ((), (), s32[]{:S(2)}) async-start(), calls=%async_computation.42 | async-start | bytes 1179648 | tf_op jit(solution)/shard_map/reduce_scatter | solution.py:374
  1012.4 125.3 %reduce-scatter.39.cloned.1.call-start = ((), (), s32[]{:S(2)}) async-start(), calls=%async_computation.41 | async-start | bytes 1179648 | tf_op jit(solution)/shard_map/reduce_scatter | solution.py:374
  1015.5 170.1 %reduce-scatter.53.cloned.1.call-start = ((), (), s32[]{:S(2)}) async-start(), calls=%async_computation.48 | async-start | bytes 3244032 | tf_op jit(solution)/shard_map/reduce_scatter | solution.py:378
  1019.2 214.5 %reduce-scatter.51.cloned.1.call-start = ((), (), s32[]{:S(2)}) async-start(), calls=%async_computation.47 | async-start | bytes 3244032 | tf_op jit(solution)/shard_map/reduce_scatter | solution.py:378
  1024.5 257.3 %reduce-scatter.49.cloned.1.call-start = ((), (), s32[]{:S(2)}) async-start(), calls=%async_computation.46 | async-start | bytes 3244032 | tf_op jit(solution)/shard_map/reduce_scatter | solution.py:377
  1029.3 300.4 %reduce-scatter.47.cloned.1.call-start = ((), (), s32[]{:S(2)}) async-start(), calls=%async_computation.45 | async-start | bytes 3244032 | tf_op jit(solution)/shard_map/reduce_scatter | solution.py:377
  1034.2 343.7 %reduce-scatter.45.cloned.1.call-start = ((), (), s32[]{:S(2)}) async-start(), calls=%async_computation.44 | async-start | bytes 3244032 | tf_op jit(solution)/shard_map/reduce_scatter | solution.py:376
  1038.3 387.7 %reduce-scatter.43.cloned.1.call-start = ((), (), s32[]{:S(2)}) async-start(), calls=%async_computation.43 | async-start | bytes 3244032 | tf_op jit(solution)/shard_map/reduce_scatter | solution.py:376
  1042.1 423.2 %reduce-scatter.37.cloned.1.call-start = ((), (), s32[]{:S(2)}) async-start(), calls=%async_computation.40 | async-start | bytes 1179648 | tf_op jit(solution)/shard_map/reduce_scatter | solution.py:373
  1045.8 458.4 %reduce-scatter.35.cloned.1.call-start = ((), (), s32[]{:S(2)}) async-start(), calls=%async_computation.39 | async-start | bytes 1179648 | tf_op jit(solution)/shard_map/reduce_scatter | solution.py:373
  1049.9 493.5 %reduce-scatter.33.cloned.1.call-start = ((), (), s32[]{:S(2)}) async-start(), calls=%async_computation.38 | async-start | bytes 1179648 | tf_op jit(solution)/shard_map/reduce_scatter | solution.py:372
  1052.4 530.0 %reduce-scatter.31.cloned.1.call-start = ((), (), s32[]{:S(2)}) async-start(), calls=%async_computation.37 | async-start | bytes 1179648 | tf_op jit(solution)/shard_map/reduce_scatter | solution.py:372
  1065.5 556.0 %reduce-scatter.29.cloned.1.call-start = ((), (), s32[]{:S(2)}) async-start(), calls=%async_computation.36 | async-start | bytes 1179648 | tf_op jit(solution)/shard_map/reduce_scatter | solution.py:371
  1068.0 592.7 %reduce-scatter.27.cloned.1.call-start = ((), (), s32[]{:S(2)}) async-start(), calls=%async_computation.35 | async-start | bytes 1179648 | tf_op jit(solution)/shard_map/reduce_scatter | solution.py:371
  1071.3 747.4 %all-reduce.26.cloned.1.call-start = ((), (), s32[]{:S(2)}) async-start(), calls=%async_computation.55 | async-start | bytes 8388608 | tf_op jit(solution)/shard_map/psum | solution.py:59
  1849.3 19.0 %all-to-all-start.1 = ((bf16[4,128,1024]{2,1,0:T(8,128)(2,1)}), bf16[4,128,1024]{2,1,0:T(8,128)(2,1)}, u32[]{:S(2)}, u32[]{:S(2)}) async-start(bf16[4,128,1024]{2,1,0:T(8,128)(2,1)} %bitcast.249), calls=%async_computation.1 | async-start | bytes 2097152 | tf_op jit(solution)/shard_map/all_to_all | solution.py:384
  (173 other events, 994.5 us)
Sparse Core Ops, SparseCore 0:
  123.3 29.6 all-gather.28
  175.4 27.2 all-gather.30
  214.0 86.1 all-reduce.13
  315.1 85.1 all-reduce.15
  405.7 28.6 all-gather.32
  456.4 25.9 all-gather.34
  493.9 86.1 all-reduce.17
  600.5 85.1 all-reduce.19
  710.5 34.1 reduce-scatter.18
  747.5 35.1 reduce-scatter.20
  787.3 86.1 all-reduce.21
  885.7 85.1 all-reduce.23
  987.3 34.2 reduce-scatter.24
  1024.4 35.2 reduce-scatter.22
  1062.7 35.9 reduce-scatter.40
  1101.7 35.9 reduce-scatter.38
  1140.9 44.6 reduce-scatter.52
  1188.9 44.6 reduce-scatter.50
  1237.0 44.6 reduce-scatter.48
  1285.0 44.6 reduce-scatter.46
  1333.1 44.6 reduce-scatter.44
  1381.3 44.6 reduce-scatter.42
  1429.2 35.9 reduce-scatter.36
  1468.2 35.9 reduce-scatter.34
  1507.4 35.9 reduce-scatter.32
  1546.4 35.9 reduce-scatter.30
  1585.5 35.9 reduce-scatter.28
  1624.7 35.9 reduce-scatter.26
  1663.7 154.9 all-reduce.25
Sparse Core Ops, SparseCore 1:
  216.8 25.1 all-gather.36
  244.3 25.0 all-gather.38
  271.7 25.0 all-gather.40
  496.4 31.1 all-gather.44
  530.1 25.0 all-gather.42
  557.1 25.0 all-gather.46
where the time goes:
time: 1890 us; the launch traced here: 1880 us
  waiting for transfers between devices  1200 us (63%)
  blocking collectives  302 us (16%)
  matrix products  166 us (9%)
  local copies, waits for them, and re-layouts  89.7 us (5%)
  other arithmetic  84.2 us (4%)
    psum x4, waiting for transfers between devices, head_total(): return lax.psum(values, 'tp')  295 us
    psum x3, waiting for transfers between devices, input_total(): return lax.psum(values, 'tp')  255 us
    reduce_scatter x2, waiting for transfers between devices, local(): lax.psum_scatter(grad_list[8], ('fsdp', 'ctx'), scatter_dimension=1, tile...  94.3 us
    reduce_scatter x2, waiting for transfers between devices, local(): lax.psum_scatter(grad_list[6], ('fsdp', 'ctx'), scatter_dimension=0, tile...  94.3 us
    reduce_scatter x2, waiting for transfers between devices, local(): lax.psum_scatter(grad_list[7], ('fsdp', 'ctx'), scatter_dimension=0, tile...  94.1 us
    reduce_scatter x2, waiting for transfers between devices, local(): lax.psum_scatter(grad_list[1], ('fsdp', 'ctx'), scatter_dimension=0, tile...  76.6 us
    reduce_scatter x2, waiting for transfers between devices, local(): lax.psum_scatter(grad_list[2], ('fsdp', 'ctx'), scatter_dimension=0, tile...  76.5 us
    reduce_scatter x2, waiting for transfers between devices, local(): lax.psum_scatter(grad_list[3], ('fsdp', 'ctx'), scatter_dimension=0, tile...  76.2 us
  transfers between devices with their start and end apart: 38, of which 26 were waited for; matrix products, arithmetic and copies ran while one was open for 11% of the time, Pallas kernels for 0%

commit v1 on v0

v1 whole, which is shorter than its diff:
```python
import jax
import jax.numpy as jnp
from jax import lax
from jax.sharding import PartitionSpec as P

HEAD = 64
HALF = HEAD // 2
LAYERS = 2
EPS = 1e-05
THETA = 10000.0
NEG = -1e30
BF = jnp.bfloat16
F32 = jnp.float32


def dot(left, right, left_dim, right_dim):
    return lax.dot_general(
        left, right, (((left_dim,), (right_dim,)), ((), ())), preferred_element_type=F32
    )


class Plan:
    def __init__(self):
        self.fsdp = lax.axis_size("fsdp")
        self.ctx = lax.axis_size("ctx")
        self.tp = lax.axis_size("tp")
        self.high = self.fsdp // 2
        f = lax.axis_index("fsdp")
        z = lax.axis_index("tp")
        self.c = f % 2
        self.fh = f // 2
        self.x = lax.axis_index("ctx")
        self.zl = z % 2
        self.zp = z // 2
        self.ci = self.x % 4

    def core(self, value):
        return lax.ppermute(value, "fsdp", [(i, i ^ 1) for i in range(self.fsdp)])

    def near(self, value):
        return lax.ppermute(value, "tp", [(i, i ^ 1) for i in range(self.tp)])

    def far(self, value):
        return lax.ppermute(value, "tp", [(i, i ^ 2) for i in range(self.tp)])

    def side(self, value, k):
        return lax.ppermute(value, "ctx", [(i, i ^ k) for i in range(self.ctx)])

    def peer(self, value, k):
        kh, kc = divmod(k, self.ctx)
        if k == 0:
            return value
        if kh == 0:
            return self.side(value, kc)
        pairs = []
        for f in range(self.fsdp):
            for i in range(self.ctx):
                pairs.append((f * self.ctx + i, (f ^ (2 * kh)) * self.ctx + (i ^ kc)))
        return lax.ppermute(value, ("fsdp", "ctx"), pairs)

    @property
    def peers(self):
        return self.high * self.ctx


def flip_blocks(value, axis, index):
    count = value.shape[axis]
    bit = 1
    while bit < count:
        shape = value.shape
        split = value.reshape(shape[:axis] + (count // (2 * bit), 2, bit) + shape[axis + 1 :])
        turned = jnp.flip(split, axis=axis + 1).reshape(shape)
        value = jnp.where((index & bit) != 0, turned, value)
        bit *= 2
    return value


def to_peer_order(plan, rows):
    count, width = rows.shape
    grid = rows.reshape(count, plan.high, 2, plan.ctx, width // (2 * plan.peers))
    grid = jnp.swapaxes(grid, 2, 3)
    grid = flip_blocks(grid, 2, plan.x)
    grid = flip_blocks(grid, 1, plan.fh)
    return grid.reshape(count, width)


def from_peer_order(plan, rows):
    count, width = rows.shape
    grid = rows.reshape(count, plan.high, plan.ctx, 2, width // (2 * plan.peers))
    grid = flip_blocks(grid, 2, plan.x)
    grid = flip_blocks(grid, 1, plan.fh)
    grid = jnp.swapaxes(grid, 2, 3)
    return grid.reshape(count, width)


def ordered(first_is_own, own, other, axis):
    return jnp.where(
        first_is_own,
        jnp.concatenate([own, other], axis=axis),
        jnp.concatenate([other, own], axis=axis),
    )


def gather_rows(plan, rows):
    pair = ordered(plan.zl == 0, rows, plan.near(rows), 0)
    return ordered(plan.c == 0, pair, plan.core(pair), 0)


def pick(flag, value):
    half = value.shape[0] // 2
    low, high = value[:half], value[half:]
    return (jnp.where(flag == 0, low, high), jnp.where(flag == 0, high, low))


def sum_rows(plan, partial):
    mine, theirs = pick(plan.c, partial)
    pair = mine + plan.core(theirs.astype(BF)).astype(F32)
    mine, theirs = pick(plan.zl, pair)
    return mine + plan.near(theirs.astype(BF)).astype(F32)


def gather_weight(plan, halves):
    keep = jnp.where(plan.c == 0, halves[0], halves[1])
    send = jnp.where(plan.c == 0, halves[1], halves[0])
    own = ordered(plan.c == 0, keep, plan.core(send), 1)
    other = plan.far(own)
    own_parts = [plan.peer(own, k) for k in range(plan.peers)]
    other_parts = [plan.peer(other, k) for k in range(plan.peers)]
    return jnp.concatenate(
        [jnp.concatenate(own_parts, axis=1), jnp.concatenate(other_parts, axis=1)], axis=0
    )


def scatter_grad(plan, grad):
    width = grad.shape[1] // plan.peers
    total = grad[:, :width].astype(F32)
    for k in range(1, plan.peers):
        piece = grad[:, k * width : (k + 1) * width].astype(BF)
        total = total + plan.peer(piece, k).astype(F32)
    half = total.shape[0] // 2
    own = total[:half] + plan.far(total[half:].astype(BF)).astype(F32)
    left, right = own[:, : width // 2], own[:, width // 2 :]
    mine = jnp.where(plan.c == 0, left, right)
    theirs = jnp.where(plan.c == 0, right, left)
    got = plan.core(theirs.astype(BF)).astype(F32)
    return jnp.where(plan.c == 0, jnp.stack([mine, got]), jnp.stack([got, mine]))


def split_hidden(weight):
    return weight.reshape(2, weight.shape[0] // 2, weight.shape[1])


def turn(values, cos_tab, sine_tab):
    first, second = values[..., :HALF, :], values[..., HALF:, :]
    return jnp.concatenate(
        [first * cos_tab - second * sine_tab, second * cos_tab + first * sine_tab], axis=-2
    )


def to_heads(plan, values):
    got = [lax.dynamic_index_in_dim(values, plan.ci, 0, False)]
    for k in range(1, 4):
        got.append(plan.side(lax.dynamic_index_in_dim(values, plan.ci ^ k, 0, False), k))
    blocks = flip_blocks(jnp.stack(got), 0, plan.ci)
    blocks = jnp.moveaxis(blocks, 0, -2)
    return blocks.reshape(blocks.shape[:-2] + (-1,))


def from_heads(plan, values):
    blocks = jnp.moveaxis(values.reshape(values.shape[:-1] + (4, -1)), -2, 0)
    got = [lax.dynamic_index_in_dim(blocks, plan.ci, 0, False)]
    for k in range(1, 4):
        got.append(plan.side(lax.dynamic_index_in_dim(blocks, plan.ci ^ k, 0, False), k))
    return flip_blocks(jnp.stack(got), 0, plan.ci)


def far_keys(plan, values):
    width = values.shape[-1]
    parts = plan.ctx // 4
    if parts == 1:
        return values
    got = [values] + [plan.side(values, 4 * k) for k in range(1, parts)]
    blocks = flip_blocks(jnp.stack(got), 0, plan.x // 4)
    return jnp.moveaxis(blocks, 0, -2).reshape(values.shape[:-1] + (parts * width,))


def far_keys_sum(plan, values):
    parts = plan.ctx // 4
    if parts == 1:
        return values
    blocks = jnp.moveaxis(values.reshape(values.shape[:-1] + (parts, -1)), -2, 0)
    blocks = flip_blocks(blocks, 0, plan.x // 4)
    total = blocks[0]
    for k in range(1, parts):
        total = total + plan.side(blocks[k], 4 * k)
    return total


def attend(queries, keys, values, allowed):
    scores = dot(keys, queries, 0, 0) * HEAD ** (-0.5)
    scores = jnp.where(allowed, scores, NEG)
    peak = jnp.max(scores, axis=0, keepdims=True)
    exp_scores = jnp.exp(scores - peak)
    total = jnp.sum(exp_scores, axis=0, keepdims=True)
    probs = (exp_scores / total).astype(BF)
    return (dot(values, probs, 1, 0), peak + jnp.log(total))


def attend_back(queries, keys, values, allowed, log_total, grad_out):
    scores = dot(keys, queries, 0, 0) * HEAD ** (-0.5)
    scores = jnp.where(allowed, scores, NEG)
    probs = jnp.exp(scores - log_total)
    grad_probs = dot(values, grad_out, 0, 0)
    inner = jnp.sum(probs * grad_probs, axis=0, keepdims=True)
    grad_scores = (probs * (grad_probs - inner)).astype(BF)
    return (
        dot(keys, grad_scores, 1, 0) * HEAD ** (-0.5),
        dot(queries, grad_scores, 1, 1) * HEAD ** (-0.5),
        dot(grad_out, probs.astype(BF), 1, 1),
    )


def norm_scale(stream):
    return lax.rsqrt(jnp.mean(stream * stream, axis=-1, keepdims=True) + EPS)


def norm_back(stream, scale, gain, grad_normed):
    weighted = grad_normed * gain
    grad_gain = jnp.sum(grad_normed * stream * scale, axis=0, keepdims=True)
    grad_stream = scale * weighted - stream * scale**3 * jnp.mean(
        weighted * stream, axis=1, keepdims=True
    )
    return (grad_gain, grad_stream)


def local(
    tokens,
    out_grad,
    segment_ids,
    owner_order,
    attn_gain,
    w_query,
    w_key,
    w_value,
    w_out,
    mlp_gain,
    w_gate,
    w_up,
    w_down,
):
    plan = Plan()
    tok_rows = tokens.shape[0]
    part_rows = tok_rows // 4
    model = tokens.shape[1]

    gains = jnp.concatenate([attn_gain, mlp_gain], axis=0)
    gains = jnp.concatenate([gains, jnp.zeros((12, gains.shape[1]), BF)], axis=0)
    full = []
    for level in range(LAYERS):
        parts = []
        qkv = jnp.stack(
            [split_hidden(w[level].T) for w in (w_query, w_key, w_value)], axis=1
        )
        qkv = qkv.reshape(2, -1, qkv.shape[-1])
        parts.append(gather_weight(plan, qkv))
        for w in (w_out[level], w_gate[level].T, w_up[level].T, w_down[level]):
            parts.append(gather_weight(plan, split_hidden(w)))
        full.append(parts)
    gain_pair = ordered(plan.c == 0, gains, plan.core(gains), 1)
    gain_full = jnp.concatenate(
        [plan.peer(gain_pair, k) for k in range(plan.peers)], axis=1
    ).astype(F32)

    part = plan.c * 2 + plan.zl
    other_part = (1 - plan.c) * 2 + plan.zl

    def own_rows(array):
        mine = lax.dynamic_slice_in_dim(array, part * part_rows, part_rows, 0)
        sent = lax.dynamic_slice_in_dim(array, other_part * part_rows, part_rows, 0)
        got = plan.core(sent)
        return to_peer_order(plan, jnp.where(plan.c == plan.zp, mine, got))

    stream = own_rows(tokens).astype(F32)
    grad_stream = own_rows(out_grad).astype(F32)

    segment = segment_ids
    segment = jnp.where(plan.c == plan.zp, segment, plan.core(segment))[0]
    pack = segment.shape[0]
    index_all = jnp.arange(pack, dtype=jnp.int32)
    run_start = jnp.concatenate([jnp.ones((1,), dtype=bool), segment[1:] != segment[:-1]])
    run_first = lax.cummax(jnp.where(run_start, index_all, jnp.zeros_like(index_all)), axis=0)
    positions = (index_all - run_first).astype(F32)
    frequency = THETA ** (-(jnp.arange(HALF, dtype=F32) * 2.0 / HEAD))
    angles = frequency[:, None] * positions[None, :]
    cos_all, sine_all = jnp.cos(angles), jnp.sin(angles)
    cos_own = lax.dynamic_slice_in_dim(cos_all, plan.x * tok_rows, tok_rows, 1)
    sine_own = lax.dynamic_slice_in_dim(sine_all, plan.x * tok_rows, tok_rows, 1)
    first_query = (plan.x // 4) * (4 * tok_rows)
    cos_query = lax.dynamic_slice_in_dim(cos_all, first_query, 4 * tok_rows, 1)
    sine_query = lax.dynamic_slice_in_dim(sine_all, first_query, 4 * tok_rows, 1)
    query_index = lax.dynamic_slice_in_dim(index_all, first_query, 4 * tok_rows, 0)
    query_first = lax.dynamic_slice_in_dim(run_first, first_query, 4 * tok_rows, 0)
    allowed = (index_all[:, None] <= query_index[None, :]) & (
        index_all[:, None] >= query_first[None, :]
    )

    kept = []
    first_values = None
    for level in range(LAYERS):
        w_qkv, w_o, w_g, w_u, w_d = full[level]
        scale_attn = norm_scale(stream)
        normed = (stream * scale_attn * gain_full[level : level + 1]).astype(BF)
        normed_all = gather_rows(plan, normed)
        qkv = dot(w_qkv, normed_all, 1, 1).reshape(2, 3, 2, HEAD, tok_rows)
        query = turn(qkv[:, 0], cos_own, sine_own).astype(BF)
        key = turn(qkv[:, 1], cos_own, sine_own).astype(BF)
        if level == 0:
            first_values = qkv[:, 2]
            mixed = first_values
        else:
            mixed = 0.5 * qkv[:, 2] + 0.5 * first_values
        heads = jnp.stack([query, key, mixed.astype(BF)], axis=2)
        heads = heads.reshape(4, 3, HEAD, tok_rows)
        heads = to_heads(plan, heads)
        keys_values = far_keys(plan, heads[1:])
        out, log_total = attend(heads[0], keys_values[0], keys_values[1], allowed)
        attended = from_heads(plan, out.astype(BF)).reshape(4 * HEAD, tok_rows)
        middle = stream + sum_rows(plan, dot(attended, w_o, 0, 0))
        scale_mlp = norm_scale(middle)
        normed_mlp = (middle * scale_mlp * gain_full[2 + level : 3 + level]).astype(BF)
        normed_mlp_all = gather_rows(plan, normed_mlp)
        gate = dot(normed_mlp_all, w_g, 1, 1)
        upward = dot(normed_mlp_all, w_u, 1, 1)
        hidden = (gate * jax.nn.sigmoid(gate) * upward).astype(BF)
        result = middle + sum_rows(plan, dot(hidden, w_d, 1, 0))
        kept.append(
            (
                stream,
                scale_attn,
                normed_all,
                heads[0],
                keys_values,
                log_total,
                attended,
                middle,
                scale_mlp,
                normed_mlp_all,
                gate,
                upward,
                hidden,
            )
        )
        stream = result

    def to_pack(rows):
        block = gather_rows(plan, rows)
        pairs = []
        for f in range(plan.fsdp):
            for z in range(plan.tp):
                if f % 2 == z // 2:
                    pairs.append((f * plan.tp + z, f * plan.tp + (z ^ 2)))
        got = lax.ppermute(block, ("fsdp", "tp"), pairs)
        return jnp.where(plan.c == plan.zp, block, got)

    outputs = to_pack(from_peer_order(plan, stream.astype(BF)))

    grads = [None] * LAYERS
    gain_rows = [None] * (2 * LAYERS)
    carried = None
    for level in reversed(range(LAYERS)):
        (
            stream,
            scale_attn,
            normed_all,
            query,
            keys_values,
            log_total,
            attended,
            middle,
            scale_mlp,
            normed_mlp_all,
            gate,
            upward,
            hidden,
        ) = kept[level]
        w_qkv, w_o, w_g, w_u, w_d = full[level]
        branch = gather_rows(plan, grad_stream.astype(BF))
        grad_hidden = dot(branch, w_d, 1, 1)
        sigma = jax.nn.sigmoid(gate)
        grad_gate = (grad_hidden * upward * sigma * (1.0 + gate * (1.0 - sigma))).astype(BF)
        grad_up = (grad_hidden * gate * sigma).astype(BF)
        grad_normed = sum_rows(plan, dot(grad_gate, w_g, 1, 0) + dot(grad_up, w_u, 1, 0))
        grad_down = scatter_grad(plan, dot(hidden, branch, 0, 0))
        grad_wg = scatter_grad(plan, dot(grad_gate, normed_mlp_all, 0, 0))
        grad_wu = scatter_grad(plan, dot(grad_up, normed_mlp_all, 0, 0))
        gain_rows[2 + level], through = norm_back(
            middle, scale_mlp, gain_full[2 + level : 3 + level], grad_normed
        )
        grad_middle = grad_stream + through
        branch = gather_rows(plan, grad_middle.astype(BF))
        grad_wo = scatter_grad(plan, dot(attended, branch, 1, 0))
        grad_attended = dot(w_o, branch, 1, 1).astype(BF)
        grad_attended = to_heads(plan, grad_attended.reshape(4, HEAD, tok_rows))
        grad_q, grad_k, grad_v = attend_back(
            query, keys_values[0], keys_values[1], allowed, log_total, grad_attended
        )
        grad_k = far_keys_sum(plan, grad_k)
        grad_v = far_keys_sum(plan, grad_v)
        grad_q = turn(grad_q, cos_query, -sine_query).astype(BF)
        grad_k = turn(grad_k, cos_query, -sine_query).astype(BF)
        if level > 0:
            half = 0.5 * grad_v
            carried = half if carried is None else carried + half
            grad_v = half.astype(BF)
        else:
            grad_v = (grad_v + carried).astype(BF)
        grad_heads = from_heads(plan, jnp.stack([grad_q, grad_k, grad_v]))
        grad_qkv = grad_heads.reshape(2, 2, 3, HEAD, tok_rows)
        grad_qkv = jnp.swapaxes(grad_qkv, 1, 2).reshape(-1, tok_rows)
        grad_wqkv = scatter_grad(plan, dot(grad_qkv, normed_all, 1, 0))
        grad_normed = sum_rows(plan, dot(grad_qkv, w_qkv, 0, 0))
        gain_rows[level], through = norm_back(
            stream, scale_attn, gain_full[level : level + 1], grad_normed
        )
        grad_stream = grad_middle + through
        hidden_half = grad_wqkv.shape[1] // 3
        qkv_split = grad_wqkv.reshape(2, 3, hidden_half, -1)
        qkv_split = [qkv_split[:, i].reshape(2 * hidden_half, -1).T for i in range(3)]

        def whole(halves):
            return halves.reshape(-1, halves.shape[-1])

        grads[level] = (
            qkv_split[0],
            qkv_split[1],
            qkv_split[2],
            whole(grad_wo),
            whole(grad_wg).T,
            whole(grad_wu).T,
            whole(grad_down),
        )

    gain_sum = jnp.concatenate(gain_rows + [jnp.zeros((4, model), F32)], axis=0)
    width = model // plan.peers
    total = gain_sum[:, :width]
    for k in range(1, plan.peers):
        total = total + plan.peer(gain_sum[:, k * width : (k + 1) * width], k)
    total = total + plan.far(total)
    total = total + plan.near(total)
    left, right = total[:, : width // 2], total[:, width // 2 :]
    mine = jnp.where(plan.c == 0, left, right)
    theirs = jnp.where(plan.c == 0, right, left)
    total = mine + plan.core(theirs)

    grad_block = to_pack(from_peer_order(plan, grad_stream.astype(BF)))
    group_rows = tok_rows // plan.ctx
    owner_grid = owner_order[0].reshape(plan.ctx, plan.ctx, group_rows)
    local_rows = (
        lax.dynamic_index_in_dim(owner_grid, plan.x, 1, False) - plan.x * tok_rows
    ).reshape(tok_rows)
    grad_tokens = lax.all_to_all(
        grad_block[local_rows], "ctx", split_axis=0, concat_axis=0, tiled=True
    ).astype(F32)

    stacked = [jnp.stack([grads[level][i] for level in range(LAYERS)]) for i in range(7)]
    return (
        outputs,
        grad_tokens,
        total[:2],
        stacked[0],
        stacked[1],
        stacked[2],
        stacked[3],
        total[2:4],
        stacked[4],
        stacked[5],
        stacked[6],
    )


def solution(mesh):
    columns = P(None, ("fsdp", "ctx"), "tp")
    rows = P(None, "tp", ("fsdp", "ctx"))
    gain = P(None, ("fsdp", "ctx"))
    tokens = P(("fsdp", "ctx"), None)
    return jax.shard_map(
        local,
        mesh=mesh,
        in_specs=(
            tokens,
            tokens,
            P("fsdp", None),
            P("fsdp", None),
            gain,
            columns,
            columns,
            columns,
            rows,
            gain,
            columns,
            columns,
            rows,
        ),
        out_specs=(
            tokens,
            tokens,
            gain,
            columns,
            columns,
            columns,
            rows,
            gain,
            columns,
            columns,
            rows,
        ),
        check_vma=False,
    )
```

time: 1890 us -> 823 us (0.44)
  waiting for transfers between devices: 1200 us -> 342 us
  blocking collectives: 302 us -> 0 us
  starting transfers between devices: 16.3 us -> 202 us
  local copies, waits for them, and re-layouts: 89.7 us -> 41 us
  matrix products: 166 us -> 126 us
    reduce_scatter x18 -> x0, waiting for transfers between devices: 615 us -> none  [the longest x2 94.3 us: local(): lax.psum_scatter(grad_list[8], ('fsdp', 'ctx'), scatter_dimension=1, tile...]
    psum x7 -> x0, waiting for transfers between devices: 550 us -> none  [the longest x4 295 us: head_total(): return lax.psum(values, 'tp')]
    ppermute x0 -> x205, waiting for transfers between devices: none -> 332 us  [the longest x120 178 us: side(): return lax.ppermute(value, 'ctx', [(i, i ^ k) for i in range(self.ctx)])]
    all_gather x12 -> x0, blocking collectives: 276 us -> none  [the longest x2 53.4 us: gather_layer(): lax.all_gather(shards[1][level_idx], ('fsdp', 'ctx'), axis=0, tiled=True)]
    ppermute x0 -> x205, starting transfers between devices: none -> 199 us  [the longest x120 143 us: side(): return lax.ppermute(value, 'ctx', [(i, i ^ k) for i in range(self.ctx)])]
    dot_general x90 -> x42, matrix products: 166 us -> 126 us  [dot(): lax.dot_general(left, right, (((left_dim,), (right_dim,)), ((), ())), pre...]
    unnamed x367 -> x424, local copies, waits for them, and re-layouts: 50.9 us -> 11.8 us
    gather x5 -> x1, local copies, waits for them, and re-layouts: 33.4 us -> 2.78 us  [local(): grad_block[local_rows]]
  transfers between devices with their start and end apart: 38 -> 206, of which waited for: 26 -> 109; matrix products, arithmetic and copies ran while one was open for 11% -> 28% of each run, Pallas kernels for 0% -> 0%
where the time goes in v1:
time: 823 us; the launch traced here: 814 us
  waiting for transfers between devices  342 us (42%)
  starting transfers between devices  202 us (25%)
  matrix products  126 us (15%)
  other arithmetic  96.9 us (12%)
  local copies, waits for them, and re-layouts  41 us (5%)
    ppermute x120, waiting for transfers between devices, side(): return lax.ppermute(value, 'ctx', [(i, i ^ k) for i in range(self.ctx)])  178 us
    ppermute x120, starting transfers between devices, side(): return lax.ppermute(value, 'ctx', [(i, i ^ k) for i in range(self.ctx)])  143 us
    dot_general x42, matrix products, dot(): lax.dot_general(left, right, (((left_dim,), (right_dim,)), ((), ())), pre...  126 us
    ppermute x21, waiting for transfers between devices, far(): return lax.ppermute(value, 'tp', [(i, i ^ 2) for i in range(self.tp)])  74.9 us
    ppermute x19, waiting for transfers between devices, near(): return lax.ppermute(value, 'tp', [(i, i ^ 1) for i in range(self.tp)])  74.1 us
    ppermute x21, starting transfers between devices, far(): return lax.ppermute(value, 'tp', [(i, i ^ 2) for i in range(self.tp)])  21.9 us
    convert_element_type x2, other arithmetic, attend_back(): grad_scores = (probs * (grad_probs - inner)).astype(BF)  19.1 us
    ppermute x19, starting transfers between devices, near(): return lax.ppermute(value, 'tp', [(i, i ^ 1) for i in range(self.tp)])  18.8 us
  transfers between devices with their start and end apart: 206, of which 109 were waited for; matrix products, arithmetic and copies ran while one was open for 28% of the time, Pallas kernels for 0%

profile of v1, /device:TPU:0, one launch (start us, length us, event | category | flops | bytes accessed | tf_op | source)
XLA Modules:
  0.0 814.4 jit_solution(14511891366402096973)
XLA Ops:
  7.9 3.9 collective-permute-start.12
  39.2 5.4 collective-permute-done.8
  64.7 8.9 %fusion.146 = (f32[2048]{0:T(1024)S(1)}, f32[2048,2048]{1,0:T(8,128)}) fusion(bf16[64,2048]{1,0:T(8,128)(2,1)S(1)} %bitcast.543, bf16[64,2048]{1,0:T(8,128)(2,1)S(1)} %bitcast.557, s32[2048]{0:T(1024)S(1)} %copy-done.77), kind=kOutput, calls=%fused_computation.506 | convolution fusion | flops 562034688 | bytes 17317888 | tf_op jit(solution)/shard_map/dot_general | solution.py:17
  73.6 8.1 fusion.1
  81.7 7.6 fusion.23
  109.3 7.4 collective-permute-done.31
  123.2 5.9 collective-permute-done.32
  143.7 5.2 collective-permute-done.46
  171.8 4.5 collective-permute-done.57
  182.8 7.7 collective-permute-done.59
  191.8 7.1 collective-permute-done.68
  203.3 8.1 collective-permute-done.64
  215.0 5.1 collective-permute-done.67
  231.0 3.9 collective-permute-done.72
  241.9 8.8 %fusion.147 = (f32[2048]{0:T(1024)S(1)}, f32[2048,2048]{1,0:T(8,128)}) fusion(bf16[64,2048]{1,0:T(8,128)(2,1)S(1)} %bitcast.545, bf16[64,2048]{1,0:T(8,128)(2,1)S(1)} %bitcast.559, s32[2048]{0:T(1024)S(1)} %copy-done.78), kind=kOutput, calls=%fused_computation.507 | convolution fusion | flops 562034688 | bytes 17317888 | tf_op jit(solution)/shard_map/dot_general | solution.py:17
  250.7 8.1 fusion.2
  258.8 7.5 fusion.22
  297.4 4.9 collective-permute-done.85
  310.0 4.9 collective-permute-done.108
  375.5 7.1 collective-permute-done.202
  391.1 7.0 collective-permute-done.182
  399.9 5.7 collective-permute-done.190
  406.6 5.4 collective-permute-done.192
  418.3 8.0 collective-permute-done.183
  438.7 4.5 collective-permute-done.122
  449.5 4.1 collective-permute-done.114
  467.5 4.9 collective-permute-start.116
  472.8 9.3 %fusion.148 = (bf16[64,2048]{1,0:T(8,128)(2,1)}, f32[64,2048]{1,0:T(8,128)S(1)}) fusion(bf16[64,2048]{1,0:T(8,128)(2,1)S(1)} %bitcast.534, f32[2048,2048]{1,0:T(8,128)} %get-tuple-element.202, f32[2048]{0:T(1024)S(1)} %log_add_fusion.1), kind=kOutput, calls=%fused_computation.508 | convolution fusion | flops 545521664 | bytes 17833984 | tf_op jit(solution)/shard_map/dot_general | solution.py:17
  482.1 13.3 %multiply_reduce_fusion.1 = (f32[2048]{0:T(1024)S(1)}, f32[2048,2048]{1,0:T(8,128)}) fusion(f32[2048,2048]{1,0:T(8,128)} %get-tuple-element.202, f32[2048]{0:T(1024)S(1)} %log_add_fusion.1, bf16[64,2048]{1,0:T(8,128)(2,1)S(1)} %bitcast.542, bf16[64,2048]{1,0:T(8,128)(2,1)S(1)} %bitcast.535), kind=kOutput, calls=%fused_computation.5 | convolution fusion | flops 549451776 | bytes 34095104 | tf_op jit(solution)/shard_map/dot_general | solution.py:17
  497.3 10.8 %multiply_convert_fusion.1 = bf16[2048,2048]{1,0:T(8,128)(2,1)} fusion(f32[2048,2048]{1,0:T(8,128)} %get-tuple-element.206, f32[2048,2048]{1,0:T(8,128)S(1)} %bitcast.503, f32[2048]{0:T(1024)S(1)} %get-tuple-element.205, f32[2048]{0:T(1024)S(1)} %log_add_fusion.1), kind=kLoop, calls=%fused_computation.4 | loop fusion | flops 16777216 | bytes 41959424 | tf_op jit(solution)/shard_map/convert_element_type | solution.py:215
  508.2 6.2 convolution_multiply_fusion.2
  543.5 6.6 collective-permute-done.160
  550.0 7.2 collective-permute-done.162
  559.8 7.8 collective-permute-done.163
  569.6 7.5 collective-permute-done.132
  600.9 5.1 collective-permute-done.197
  614.4 7.1 collective-permute-done.177
  628.9 8.1 collective-permute-done.187
  642.8 8.0 collective-permute-done.188
  653.0 8.3 %collective-permute-done.136 = bf16[128,1024]{1,0:T(8,128)(2,1)S(1)} collective-permute-done((bf16[128,1024]{1,0:T(8,128)(2,1)S(1)}, bf16[128,1024]{1,0:T(8,128)(2,1)S(1)}, u32[]{:S(2)}, u32[]{:S(2)}) %collective-permute-start.136) | collective-permute-done | bytes 262176 | tf_op jit(solution)/shard_map/ppermute | solution.py:41
  675.5 13.3 %multiply_reduce_fusion = (f32[2048]{0:T(1024)S(1)}, f32[2048,2048]{1,0:T(8,128)}) fusion(f32[2048,2048]{1,0:T(8,128)} %get-tuple-element.198, f32[2048]{0:T(1024)S(1)} %log_add_fusion, bf16[64,2048]{1,0:T(8,128)(2,1)S(1)} %bitcast.540, bf16[64,2048]{1,0:T(8,128)(2,1)S(1)} %bitcast.532), kind=kOutput, calls=%fused_computation.2 | convolution fusion | flops 549451776 | bytes 34095104 | tf_op jit(solution)/shard_map/dot_general | solution.py:17
  691.9 8.3 %multiply_convert_fusion = bf16[2048,2048]{1,0:T(8,128)(2,1)S(1)} fusion(f32[2048,2048]{1,0:T(8,128)} %get-tuple-element.208, f32[2048,2048]{1,0:T(8,128)S(1)} %bitcast.501, f32[2048]{0:T(1024)S(1)} %get-tuple-element.207, f32[2048]{0:T(1024)S(1)} %log_add_fusion), kind=kLoop, calls=%fused_computation.1 | loop fusion | flops 16777216 | bytes 41959424 | tf_op jit(solution)/shard_map/convert_element_type | solution.py:215
  731.7 4.5 collective-permute-done.145
  740.2 8.2 %collective-permute-done.157 = bf16[768,256]{1,0:T(8,128)(2,1)} collective-permute-done((bf16[768,256]{1,0:T(8,128)(2,1)S(1)}, bf16[768,256]{1,0:T(8,128)(2,1)}, u32[]{:S(2)}, u32[]{:S(2)}) %collective-permute-start.157) | collective-permute-done | bytes 393248 | tf_op jit(solution)/shard_map/ppermute | solution.py:47
  754.8 7.4 collective-permute-done.158
  771.1 9.4 %collective-permute-done.152 = f32[8,256]{1,0:T(8,128)S(1)} collective-permute-done((f32[8,256]{1,0:T(8,128)S(1)}, f32[8,256]{1,0:T(8,128)S(1)}, u32[]{:S(2)}, u32[]{:S(2)}) %collective-permute-start.152) | collective-permute-done | bytes 8224 | tf_op jit(solution)/shard_map/ppermute | solution.py:44
  780.6 9.2 %collective-permute-start.153 = (f32[8,256]{1,0:T(8,128)S(1)}, f32[8,256]{1,0:T(8,128)S(1)}, u32[]{:S(2)}, u32[]{:S(2)}) collective-permute-start(f32[8,256]{1,0:T(8,128)S(1)} %add.488), channel_id=1, source_target_pairs={{0,1},{1,0},{2,3},{3,2},{4,5},{5,4},{6,7},{7,6},{8,9},{9,8},{10,11... | collective-permute-start | bytes 24584 | tf_op jit(solution)/shard_map/ppermute | solution.py:41
  802.1 10.2 %all-to-all-done = bf16[4,128,1024]{2,1,0:T(8,128)(2,1)S(1)} async-done(((bf16[4,128,1024]{2,1,0:T(8,128)(2,1)}), bf16[4,128,1024]{2,1,0:T(8,128)(2,1)S(1)}, u32[]{:S(2)}, u32[]{:S(2)}) %all-to-all-start) | async-done | bytes 1048608 | tf_op jit(solution)/shard_map/all_to_all | solution.py:461
  (1176 shorter events, 462.6 us)
Async XLA Ops:
  30.3 16.9 %collective-permute-start.14 = (bf16[256,1024]{1,0:T(8,128)(2,1)S(1)}, bf16[256,1024]{1,0:T(8,128)(2,1)S(1)}, u32[]{:S(2)}, u32[]{:S(2)}) collective-permute-start(bf16[256,1024]{1,0:T(8,128)(2,1)S(1)} %maximum_select_fusion.10), channel_id=1, source_target_pairs={{0,16},{16,0},{1,17},{17,1},{2,18},{18,2},{3,19},{19,3},{4,20},{20... | collective-permute-start | bytes 1572872 | tf_op jit(solution)/shard_map/ppermute | solution.py:38
  55.7 39.5 %collective-permute-start.26 = (bf16[128,256]{1,0:T(8,128)(2,1)}, bf16[128,256]{1,0:T(8,128)(2,1)}, u32[]{:S(2)}, u32[]{:S(2)}) collective-permute-start(bf16[128,256]{1,0:T(8,128)(2,1)} %maximum_select_fusion.50), channel_id=1, source_target_pairs={{0,2},{1,3},{2,0},{3,1},{4,6},{5,7},{6,4},{7,5},{8,10},{9,11},{10,... | collective-permute-start | bytes 196616 | tf_op jit(solution)/shard_map/ppermute | solution.py:44
  118.2 16.4 %collective-permute-start.54 = (bf16[352,256]{1,0:T(8,128)(2,1)S(1)}, bf16[352,256]{1,0:T(8,128)(2,1)S(1)}, u32[]{:S(2)}, u32[]{:S(2)}) collective-permute-start(bf16[352,256]{1,0:T(8,128)(2,1)S(1)} %maximum_select_fusion.32), channel_id=1, source_target_pairs={{0,2},{1,3},{2,0},{3,1},{4,6},{5,7},{6,4},{7,5},{8,10},{9,11},{10,... | collective-permute-start | bytes 540680 | tf_op jit(solution)/shard_map/ppermute | solution.py:44
  129.2 28.3 %collective-permute-start.33 = (bf16[256,1024]{1,0:T(8,128)(2,1)S(1)}, bf16[256,1024]{1,0:T(8,128)(2,1)S(1)}, u32[]{:S(2)}, u32[]{:S(2)}) collective-permute-start(bf16[256,1024]{1,0:T(8,128)(2,1)S(1)} %maximum_select_fusion.11), channel_id=1, source_target_pairs={{0,16},{16,0},{1,17},{17,1},{2,18},{18,2},{3,19},{19,3},{4,20},{20... | collective-permute-start | bytes 1572872 | tf_op jit(solution)/shard_map/ppermute | solution.py:38
  199.1 24.4 %collective-permute-start.69 = (bf16[256,1024]{1,0:T(8,128)(2,1)S(1)}, bf16[256,1024]{1,0:T(8,128)(2,1)S(1)}, u32[]{:S(2)}, u32[]{:S(2)}) collective-permute-start(bf16[256,1024]{1,0:T(8,128)(2,1)S(1)} %maximum_select_fusion.12), channel_id=1, source_target_pairs={{0,16},{16,0},{1,17},{17,1},{2,18},{18,2},{3,19},{19,3},{4,20},{20... | collective-permute-start | bytes 1572872 | tf_op jit(solution)/shard_map/ppermute | solution.py:38
  231.0 42.3 %collective-permute-start.80 = (bf16[128,256]{1,0:T(8,128)(2,1)}, bf16[128,256]{1,0:T(8,128)(2,1)}, u32[]{:S(2)}, u32[]{:S(2)}) collective-permute-start(bf16[128,256]{1,0:T(8,128)(2,1)} %maximum_select_fusion.51), channel_id=1, source_target_pairs={{0,2},{1,3},{2,0},{3,1},{4,6},{5,7},{6,4},{7,5},{8,10},{9,11},{10,... | collective-permute-start | bytes 196616 | tf_op jit(solution)/shard_map/ppermute | solution.py:44
  279.3 23.7 %collective-permute-start.104 = (bf16[352,128]{1,0:T(8,128)(2,1)}, bf16[352,128]{1,0:T(8,128)(2,1)}, u32[]{:S(2)}, u32[]{:S(2)}) collective-permute-start(bf16[352,128]{1,0:T(8,128)(2,1)} %get-tuple-element.126), channel_id=1, source_target_pairs={{0,16},{16,0},{1,17},{17,1},{2,18},{18,2},{3,19},{19,3},{4,20},{20... | collective-permute-start | bytes 270344 | tf_op jit(solution)/shard_map/ppermute | solution.py:38
  280.7 25.4 %collective-permute-start.88 = (bf16[352,128]{1,0:T(8,128)(2,1)}, bf16[352,128]{1,0:T(8,128)(2,1)}, u32[]{:S(2)}, u32[]{:S(2)}) collective-permute-start(bf16[352,128]{1,0:T(8,128)(2,1)} %get-tuple-element.153), channel_id=1, source_target_pairs={{0,16},{16,0},{1,17},{17,1},{2,18},{18,2},{3,19},{19,3},{4,20},{20... | collective-permute-start | bytes 270344 | tf_op jit(solution)/shard_map/ppermute | solution.py:38
  297.3 33.1 %collective-permute-start.119 = (bf16[256,1024]{1,0:T(8,128)(2,1)S(1)}, bf16[256,1024]{1,0:T(8,128)(2,1)S(1)}, u32[]{:S(2)}, u32[]{:S(2)}) collective-permute-start(bf16[256,1024]{1,0:T(8,128)(2,1)S(1)} %maximum_select_fusion.15), channel_id=1, source_target_pairs={{0,16},{16,0},{1,17},{17,1},{2,18},{18,2},{3,19},{19,3},{4,20},{20... | collective-permute-start | bytes 1572872 | tf_op jit(solution)/shard_map/ppermute | solution.py:38
  302.6 15.8 %collective-permute-start.86 = (bf16[128,1024]{1,0:T(8,128)(2,1)S(1)}, bf16[128,1024]{1,0:T(8,128)(2,1)S(1)}, u32[]{:S(2)}, u32[]{:S(2)}) collective-permute-start(bf16[128,1024]{1,0:T(8,128)(2,1)S(1)} %multiply_convert_fusion.8), channel_id=1, source_target_pairs={{0,1},{1,0},{2,3},{3,2},{4,5},{5,4},{6,7},{7,6},{8,9},{9,8},{10,11... | collective-permute-start | bytes 786440 | tf_op jit(solution)/shard_map/ppermute | solution.py:41
  330.5 20.5 %collective-permute-start.87 = (bf16[256,1024]{1,0:T(8,128)(2,1)S(1)}, bf16[256,1024]{1,0:T(8,128)(2,1)S(1)}, u32[]{:S(2)}, u32[]{:S(2)}) collective-permute-start(bf16[256,1024]{1,0:T(8,128)(2,1)S(1)} %maximum_select_fusion.13), channel_id=1, source_target_pairs={{0,16},{16,0},{1,17},{17,1},{2,18},{18,2},{3,19},{19,3},{4,20},{20... | collective-permute-start | bytes 1572872 | tf_op jit(solution)/shard_map/ppermute | solution.py:38
  365.3 17.3 %collective-permute-start.202 = (bf16[704,256]{1,0:T(8,128)(2,1)S(1)}, bf16[704,256]{1,0:T(8,128)(2,1)S(1)}, u32[]{:S(2)}, u32[]{:S(2)}) collective-permute-start(bf16[704,256]{1,0:T(8,128)(2,1)S(1)} %get-tuple-element.59), channel_id=1, source_target_pairs={{0,12},{4,8},{8,4},{12,0},{1,13},{5,9},{9,5},{13,1},{2,14},{6,10},... | collective-permute-start | bytes 1081352 | tf_op jit(solution)/shard_map/ppermute | solution.py:47
  365.6 18.7 %collective-permute-start.201 = (bf16[704,256]{1,0:T(8,128)(2,1)S(1)}, bf16[704,256]{1,0:T(8,128)(2,1)S(1)}, u32[]{:S(2)}, u32[]{:S(2)}) collective-permute-start(bf16[704,256]{1,0:T(8,128)(2,1)S(1)} %get-tuple-element.60), channel_id=1, source_target_pairs={{0,8},{4,12},{8,0},{12,4},{1,9},{5,13},{9,1},{13,5},{2,10},{6,14},... | collective-permute-start | bytes 1081352 | tf_op jit(solution)/shard_map/ppermute | solution.py:47
  368.1 22.0 %collective-permute-start.180 = (bf16[704,256]{1,0:T(8,128)(2,1)S(1)}, bf16[704,256]{1,0:T(8,128)(2,1)S(1)}, u32[]{:S(2)}, u32[]{:S(2)}) collective-permute-start(bf16[704,256]{1,0:T(8,128)(2,1)S(1)} %get-tuple-element.70), channel_id=1, source_target_pairs={{0,4},{4,0},{8,12},{12,8},{1,5},{5,1},{9,13},{13,9},{2,6},{6,2},{1... | collective-permute-start | bytes 1081352 | tf_op jit(solution)/shard_map/ppermute | solution.py:47
  373.2 24.9 %collective-permute-start.182 = (bf16[704,256]{1,0:T(8,128)(2,1)S(1)}, bf16[704,256]{1,0:T(8,128)(2,1)S(1)}, u32[]{:S(2)}, u32[]{:S(2)}) collective-permute-start(bf16[704,256]{1,0:T(8,128)(2,1)S(1)} %get-tuple-element.71), channel_id=1, source_target_pairs={{0,12},{4,8},{8,4},{12,0},{1,13},{5,9},{9,5},{13,1},{2,14},{6,10},... | collective-permute-start | bytes 1081352 | tf_op jit(solution)/shard_map/ppermute | solution.py:47
  374.6 25.1 %collective-permute-start.181 = (bf16[704,256]{1,0:T(8,128)(2,1)S(1)}, bf16[704,256]{1,0:T(8,128)(2,1)S(1)}, u32[]{:S(2)}, u32[]{:S(2)}) collective-permute-start(bf16[704,256]{1,0:T(8,128)(2,1)S(1)} %get-tuple-element.72), channel_id=1, source_target_pairs={{0,8},{4,12},{8,0},{12,4},{1,9},{5,13},{9,1},{13,5},{2,10},{6,14},... | collective-permute-start | bytes 1081352 | tf_op jit(solution)/shard_map/ppermute | solution.py:47
  382.6 23.0 %collective-permute-start.190 = (bf16[704,256]{1,0:T(8,128)(2,1)S(1)}, bf16[704,256]{1,0:T(8,128)(2,1)S(1)}, u32[]{:S(2)}, u32[]{:S(2)}) collective-permute-start(bf16[704,256]{1,0:T(8,128)(2,1)S(1)} %get-tuple-element.64), channel_id=1, source_target_pairs={{0,4},{4,0},{8,12},{12,8},{1,5},{5,1},{9,13},{13,9},{2,6},{6,2},{1... | collective-permute-start | bytes 1081352 | tf_op jit(solution)/shard_map/ppermute | solution.py:47
  384.3 27.8 %collective-permute-start.192 = (bf16[704,256]{1,0:T(8,128)(2,1)S(1)}, bf16[704,256]{1,0:T(8,128)(2,1)S(1)}, u32[]{:S(2)}, u32[]{:S(2)}) collective-permute-start(bf16[704,256]{1,0:T(8,128)(2,1)S(1)} %get-tuple-element.65), channel_id=1, source_target_pairs={{0,12},{4,8},{8,4},{12,0},{1,13},{5,9},{9,5},{13,1},{2,14},{6,10},... | collective-permute-start | bytes 1081352 | tf_op jit(solution)/shard_map/ppermute | solution.py:47
  390.1 23.5 %collective-permute-start.191 = (bf16[704,256]{1,0:T(8,128)(2,1)S(1)}, bf16[704,256]{1,0:T(8,128)(2,1)S(1)}, u32[]{:S(2)}, u32[]{:S(2)}) collective-permute-start(bf16[704,256]{1,0:T(8,128)(2,1)S(1)} %get-tuple-element.66), channel_id=1, source_target_pairs={{0,8},{4,12},{8,0},{12,4},{1,9},{5,13},{9,1},{13,5},{2,10},{6,14},... | collective-permute-start | bytes 1081352 | tf_op jit(solution)/shard_map/ppermute | solution.py:47
  398.1 17.2 %collective-permute-start.112 = (bf16[256,1024]{1,0:T(8,128)(2,1)S(1)}, bf16[256,1024]{1,0:T(8,128)(2,1)S(1)}, u32[]{:S(2)}, u32[]{:S(2)}) collective-permute-start(bf16[256,1024]{1,0:T(8,128)(2,1)S(1)} %select_convert_fusion.4), channel_id=1, source_target_pairs={{0,16},{16,0},{1,17},{17,1},{2,18},{18,2},{3,19},{19,3},{4,20},{20... | collective-permute-start | bytes 1572872 | tf_op jit(solution)/shard_map/ppermute | solution.py:38
  399.7 17.2 %collective-permute-start.120 = (bf16[256,1024]{1,0:T(8,128)(2,1)S(1)}, bf16[256,1024]{1,0:T(8,128)(2,1)S(1)}, u32[]{:S(2)}, u32[]{:S(2)}) collective-permute-start(bf16[256,1024]{1,0:T(8,128)(2,1)S(1)} %select_convert_fusion.3), channel_id=1, source_target_pairs={{0,16},{16,0},{1,17},{17,1},{2,18},{18,2},{3,19},{19,3},{4,20},{20... | collective-permute-start | bytes 1572872 | tf_op jit(solution)/shard_map/ppermute | solution.py:38
  413.8 15.8 %collective-permute-start.193 = (bf16[352,256]{1,0:T(8,128)(2,1)S(1)}, bf16[352,256]{1,0:T(8,128)(2,1)S(1)}, u32[]{:S(2)}, u32[]{:S(2)}) collective-permute-start(bf16[352,256]{1,0:T(8,128)(2,1)S(1)} %slice.1341), channel_id=1, source_target_pairs={{0,2},{1,3},{2,0},{3,1},{4,6},{5,7},{6,4},{7,5},{8,10},{9,11},{10,... | collective-permute-start | bytes 540680 | tf_op jit(solution)/shard_map/ppermute | solution.py:44
  415.6 20.1 %collective-permute-start.113 = (bf16[128,1024]{1,0:T(8,128)(2,1)S(1)}, bf16[128,1024]{1,0:T(8,128)(2,1)S(1)}, u32[]{:S(2)}, u32[]{:S(2)}) collective-permute-start(bf16[128,1024]{1,0:T(8,128)(2,1)S(1)} %select_convert_fusion.12), channel_id=1, source_target_pairs={{0,1},{1,0},{2,3},{3,2},{4,5},{5,4},{6,7},{7,6},{8,9},{9,8},{10,11... | collective-permute-start | bytes 786440 | tf_op jit(solution)/shard_map/ppermute | solution.py:41
  417.2 17.7 %collective-permute-start.121 = (bf16[128,1024]{1,0:T(8,128)(2,1)S(1)}, bf16[128,1024]{1,0:T(8,128)(2,1)S(1)}, u32[]{:S(2)}, u32[]{:S(2)}) collective-permute-start(bf16[128,1024]{1,0:T(8,128)(2,1)S(1)} %select_convert_fusion.11), channel_id=1, source_target_pairs={{0,1},{1,0},{2,3},{3,2},{4,5},{5,4},{6,7},{7,6},{8,9},{9,8},{10,11... | collective-permute-start | bytes 786440 | tf_op jit(solution)/shard_map/ppermute | solution.py:41
  463.5 58.9 %collective-permute-start.170 = (bf16[256,256]{1,0:T(8,128)(2,1)}, bf16[256,256]{1,0:T(8,128)(2,1)}, u32[]{:S(2)}, u32[]{:S(2)}) collective-permute-start(bf16[256,256]{1,0:T(8,128)(2,1)} %get-tuple-element.114), channel_id=1, source_target_pairs={{0,4},{4,0},{8,12},{12,8},{1,5},{5,1},{9,13},{13,9},{2,6},{6,2},{1... | collective-permute-start | bytes 393224 | tf_op jit(solution)/shard_map/ppermute | solution.py:47
  464.8 57.5 %collective-permute-start.172 = (bf16[256,256]{1,0:T(8,128)(2,1)}, bf16[256,256]{1,0:T(8,128)(2,1)}, u32[]{:S(2)}, u32[]{:S(2)}) collective-permute-start(bf16[256,256]{1,0:T(8,128)(2,1)} %get-tuple-element.115), channel_id=1, source_target_pairs={{0,12},{4,8},{8,4},{12,0},{1,13},{5,9},{9,5},{13,1},{2,14},{6,10},... | collective-permute-start | bytes 393224 | tf_op jit(solution)/shard_map/ppermute | solution.py:47
  466.1 56.3 %collective-permute-start.171 = (bf16[256,256]{1,0:T(8,128)(2,1)}, bf16[256,256]{1,0:T(8,128)(2,1)}, u32[]{:S(2)}, u32[]{:S(2)}) collective-permute-start(bf16[256,256]{1,0:T(8,128)(2,1)} %get-tuple-element.116), channel_id=1, source_target_pairs={{0,8},{4,12},{8,0},{12,4},{1,9},{5,13},{9,1},{13,5},{2,10},{6,14},... | collective-permute-start | bytes 393224 | tf_op jit(solution)/shard_map/ppermute | solution.py:47
  467.5 114.7 %collective-permute-start.116 = (bf16[512,1024]{1,0:T(8,128)(2,1)S(1)}, bf16[512,1024]{1,0:T(8,128)(2,1)}, u32[]{:S(2)}, u32[]{:S(2)}) collective-permute-start(bf16[512,1024]{1,0:T(8,128)(2,1)S(1)} %maximum_select_fusion.4), channel_id=1, source_target_pairs={{0,2},{1,3},{18,16},{19,17},{4,6},{5,7},{22,20},{23,21},{8,10},{9,... | collective-permute-start | bytes 3145736 | tf_op jit(solution)/shard_map/ppermute | solution.py:362
  539.0 18.2 %collective-permute-start.162 = (bf16[768,256]{1,0:T(8,128)(2,1)S(1)}, bf16[768,256]{1,0:T(8,128)(2,1)S(1)}, u32[]{:S(2)}, u32[]{:S(2)}) collective-permute-start(bf16[768,256]{1,0:T(8,128)(2,1)S(1)} %get-tuple-element.48), channel_id=1, source_target_pairs={{0,12},{4,8},{8,4},{12,0},{1,13},{5,9},{9,5},{13,1},{2,14},{6,10},... | collective-permute-start | bytes 1179656 | tf_op jit(solution)/shard_map/ppermute | solution.py:47
  540.2 18.5 %collective-permute-start.161 = (bf16[768,256]{1,0:T(8,128)(2,1)S(1)}, bf16[768,256]{1,0:T(8,128)(2,1)S(1)}, u32[]{:S(2)}, u32[]{:S(2)}) collective-permute-start(bf16[768,256]{1,0:T(8,128)(2,1)S(1)} %get-tuple-element.49), channel_id=1, source_target_pairs={{0,8},{4,12},{8,0},{12,4},{1,9},{5,13},{9,1},{13,5},{2,10},{6,14},... | collective-permute-start | bytes 1179656 | tf_op jit(solution)/shard_map/ppermute | solution.py:47
  542.7 16.3 %collective-permute-start.130 = (bf16[256,1024]{1,0:T(8,128)(2,1)S(1)}, bf16[256,1024]{1,0:T(8,128)(2,1)S(1)}, u32[]{:S(2)}, u32[]{:S(2)}) collective-permute-start(bf16[256,1024]{1,0:T(8,128)(2,1)S(1)} %select_convert_fusion.2), channel_id=1, source_target_pairs={{0,16},{16,0},{1,17},{17,1},{2,18},{18,2},{3,19},{19,3},{4,20},{20... | collective-permute-start | bytes 1572872 | tf_op jit(solution)/shard_map/ppermute | solution.py:38
  587.4 18.6 %collective-permute-start.197 = (bf16[704,256]{1,0:T(8,128)(2,1)S(1)}, bf16[704,256]{1,0:T(8,128)(2,1)S(1)}, u32[]{:S(2)}, u32[]{:S(2)}) collective-permute-start(bf16[704,256]{1,0:T(8,128)(2,1)S(1)} %get-tuple-element.56), channel_id=1, source_target_pairs={{0,12},{4,8},{8,4},{12,0},{1,13},{5,9},{9,5},{13,1},{2,14},{6,10},... | collective-permute-start | bytes 1081352 | tf_op jit(solution)/shard_map/ppermute | solution.py:47
  589.5 19.0 %collective-permute-start.196 = (bf16[704,256]{1,0:T(8,128)(2,1)S(1)}, bf16[704,256]{1,0:T(8,128)(2,1)S(1)}, u32[]{:S(2)}, u32[]{:S(2)}) collective-permute-start(bf16[704,256]{1,0:T(8,128)(2,1)S(1)} %get-tuple-element.57), channel_id=1, source_target_pairs={{0,8},{4,12},{8,0},{12,4},{1,9},{5,13},{9,1},{13,5},{2,10},{6,14},... | collective-permute-start | bytes 1081352 | tf_op jit(solution)/shard_map/ppermute | solution.py:47
  593.4 18.8 %collective-permute-start.175 = (bf16[704,256]{1,0:T(8,128)(2,1)S(1)}, bf16[704,256]{1,0:T(8,128)(2,1)S(1)}, u32[]{:S(2)}, u32[]{:S(2)}) collective-permute-start(bf16[704,256]{1,0:T(8,128)(2,1)S(1)} %get-tuple-element.67), channel_id=1, source_target_pairs={{0,4},{4,0},{8,12},{12,8},{1,5},{5,1},{9,13},{13,9},{2,6},{6,2},{1... | collective-permute-start | bytes 1081352 | tf_op jit(solution)/shard_map/ppermute | solution.py:47
  594.9 26.6 %collective-permute-start.177 = (bf16[704,256]{1,0:T(8,128)(2,1)S(1)}, bf16[704,256]{1,0:T(8,128)(2,1)S(1)}, u32[]{:S(2)}, u32[]{:S(2)}) collective-permute-start(bf16[704,256]{1,0:T(8,128)(2,1)S(1)} %get-tuple-element.68), channel_id=1, source_target_pairs={{0,12},{4,8},{8,4},{12,0},{1,13},{5,9},{9,5},{13,1},{2,14},{6,10},... | collective-permute-start | bytes 1081352 | tf_op jit(solution)/shard_map/ppermute | solution.py:47
  600.5 23.4 %collective-permute-start.176 = (bf16[704,256]{1,0:T(8,128)(2,1)S(1)}, bf16[704,256]{1,0:T(8,128)(2,1)S(1)}, u32[]{:S(2)}, u32[]{:S(2)}) collective-permute-start(bf16[704,256]{1,0:T(8,128)(2,1)S(1)} %get-tuple-element.69), channel_id=1, source_target_pairs={{0,8},{4,12},{8,0},{12,4},{1,9},{5,13},{9,1},{13,5},{2,10},{6,14},... | collective-permute-start | bytes 1081352 | tf_op jit(solution)/shard_map/ppermute | solution.py:47
  606.0 21.7 %collective-permute-start.185 = (bf16[704,256]{1,0:T(8,128)(2,1)S(1)}, bf16[704,256]{1,0:T(8,128)(2,1)S(1)}, u32[]{:S(2)}, u32[]{:S(2)}) collective-permute-start(bf16[704,256]{1,0:T(8,128)(2,1)S(1)} %get-tuple-element.61), channel_id=1, source_target_pairs={{0,4},{4,0},{8,12},{12,8},{1,5},{5,1},{9,13},{13,9},{2,6},{6,2},{1... | collective-permute-start | bytes 1081352 | tf_op jit(solution)/shard_map/ppermute | solution.py:47
  608.5 28.5 %collective-permute-start.187 = (bf16[704,256]{1,0:T(8,128)(2,1)S(1)}, bf16[704,256]{1,0:T(8,128)(2,1)S(1)}, u32[]{:S(2)}, u32[]{:S(2)}) collective-permute-start(bf16[704,256]{1,0:T(8,128)(2,1)S(1)} %get-tuple-element.62), channel_id=1, source_target_pairs={{0,12},{4,8},{8,4},{12,0},{1,13},{5,9},{9,5},{13,1},{2,14},{6,10},... | collective-permute-start | bytes 1081352 | tf_op jit(solution)/shard_map/ppermute | solution.py:47
  612.2 27.1 %collective-permute-start.186 = (bf16[704,256]{1,0:T(8,128)(2,1)S(1)}, bf16[704,256]{1,0:T(8,128)(2,1)S(1)}, u32[]{:S(2)}, u32[]{:S(2)}) collective-permute-start(bf16[704,256]{1,0:T(8,128)(2,1)S(1)} %get-tuple-element.63), channel_id=1, source_target_pairs={{0,8},{4,12},{8,0},{12,4},{1,9},{5,13},{9,1},{13,5},{2,10},{6,14},... | collective-permute-start | bytes 1081352 | tf_op jit(solution)/shard_map/ppermute | solution.py:47
  621.5 18.2 %collective-permute-start.134 = (bf16[256,1024]{1,0:T(8,128)(2,1)S(1)}, bf16[256,1024]{1,0:T(8,128)(2,1)S(1)}, u32[]{:S(2)}, u32[]{:S(2)}) collective-permute-start(bf16[256,1024]{1,0:T(8,128)(2,1)S(1)} %select_convert_fusion.1), channel_id=1, source_target_pairs={{0,16},{16,0},{1,17},{17,1},{2,18},{18,2},{3,19},{19,3},{4,20},{20... | collective-permute-start | bytes 1572872 | tf_op jit(solution)/shard_map/ppermute | solution.py:38
  623.9 16.5 %collective-permute-start.198 = (bf16[352,256]{1,0:T(8,128)(2,1)S(1)}, bf16[352,256]{1,0:T(8,128)(2,1)S(1)}, u32[]{:S(2)}, u32[]{:S(2)}) collective-permute-start(bf16[352,256]{1,0:T(8,128)(2,1)S(1)} %slice.1340), channel_id=1, source_target_pairs={{0,2},{1,3},{2,0},{3,1},{4,6},{5,7},{6,4},{7,5},{8,10},{9,11},{10,... | collective-permute-start | bytes 540680 | tf_op jit(solution)/shard_map/ppermute | solution.py:44
  671.6 38.0 %collective-permute-start.165 = (bf16[256,256]{1,0:T(8,128)(2,1)}, bf16[256,256]{1,0:T(8,128)(2,1)S(1)}, u32[]{:S(2)}, u32[]{:S(2)}) collective-permute-start(bf16[256,256]{1,0:T(8,128)(2,1)} %get-tuple-element.111), channel_id=1, source_target_pairs={{0,4},{4,0},{8,12},{12,8},{1,5},{5,1},{9,13},{13,9},{2,6},{6,2},{1... | collective-permute-start | bytes 393224 | tf_op jit(solution)/shard_map/ppermute | solution.py:47
  671.7 37.9 %collective-permute-start.167 = (bf16[256,256]{1,0:T(8,128)(2,1)}, bf16[256,256]{1,0:T(8,128)(2,1)S(1)}, u32[]{:S(2)}, u32[]{:S(2)}) collective-permute-start(bf16[256,256]{1,0:T(8,128)(2,1)} %get-tuple-element.112), channel_id=1, source_target_pairs={{0,12},{4,8},{8,4},{12,0},{1,13},{5,9},{9,5},{13,1},{2,14},{6,10},... | collective-permute-start | bytes 393224 | tf_op jit(solution)/shard_map/ppermute | solution.py:47
  673.1 36.5 %collective-permute-start.166 = (bf16[256,256]{1,0:T(8,128)(2,1)}, bf16[256,256]{1,0:T(8,128)(2,1)}, u32[]{:S(2)}, u32[]{:S(2)}) collective-permute-start(bf16[256,256]{1,0:T(8,128)(2,1)} %get-tuple-element.113), channel_id=1, source_target_pairs={{0,8},{4,12},{8,0},{12,4},{1,9},{5,13},{9,1},{13,5},{2,10},{6,14},... | collective-permute-start | bytes 393224 | tf_op jit(solution)/shard_map/ppermute | solution.py:47
  728.8 19.6 %collective-permute-start.157 = (bf16[768,256]{1,0:T(8,128)(2,1)S(1)}, bf16[768,256]{1,0:T(8,128)(2,1)}, u32[]{:S(2)}, u32[]{:S(2)}) collective-permute-start(bf16[768,256]{1,0:T(8,128)(2,1)S(1)} %get-tuple-element.45), channel_id=1, source_target_pairs={{0,12},{4,8},{8,4},{12,0},{1,13},{5,9},{9,5},{13,1},{2,14},{6,10},... | collective-permute-start | bytes 1179656 | tf_op jit(solution)/shard_map/ppermute | solution.py:47
  730.6 19.2 %collective-permute-start.156 = (bf16[768,256]{1,0:T(8,128)(2,1)S(1)}, bf16[768,256]{1,0:T(8,128)(2,1)}, u32[]{:S(2)}, u32[]{:S(2)}) collective-permute-start(bf16[768,256]{1,0:T(8,128)(2,1)S(1)} %get-tuple-element.46), channel_id=1, source_target_pairs={{0,8},{4,12},{8,0},{12,4},{1,9},{5,13},{9,1},{13,5},{2,10},{6,14},... | collective-permute-start | bytes 1179656 | tf_op jit(solution)/shard_map/ppermute | solution.py:47
  762.8 28.9 %collective-permute-start.148 = (bf16[512,1024]{1,0:T(8,128)(2,1)S(1)}, bf16[512,1024]{1,0:T(8,128)(2,1)S(1)}, u32[]{:S(2)}, u32[]{:S(2)}) collective-permute-start(bf16[512,1024]{1,0:T(8,128)(2,1)S(1)} %maximum_select_fusion.9), channel_id=1, source_target_pairs={{0,2},{1,3},{18,16},{19,17},{4,6},{5,7},{22,20},{23,21},{8,10},{9,... | collective-permute-start | bytes 3145736 | tf_op jit(solution)/shard_map/ppermute | solution.py:362
  794.7 17.6 %all-to-all-start = ((bf16[4,128,1024]{2,1,0:T(8,128)(2,1)}), bf16[4,128,1024]{2,1,0:T(8,128)(2,1)S(1)}, u32[]{:S(2)}, u32[]{:S(2)}) async-start(bf16[4,128,1024]{2,1,0:T(8,128)(2,1)} %bitcast.191), calls=%async_computation | async-start | bytes 2097152 | tf_op jit(solution)/shard_map/all_to_all | solution.py:461
  (363 other events, 3454.5 us)

commit v2 on v1

v2 whole, which is shorter than its diff:
```python
import functools

import jax
import jax.numpy as jnp
from jax import lax
from jax.experimental import pallas as pl
from jax.experimental.pallas import tpu as pltpu
from jax.sharding import PartitionSpec as P

HEAD = 64
HALF = HEAD // 2
LAYERS = 2
EPS = 1e-05
THETA = 10000.0
NEG = -1e30
BF = jnp.bfloat16
F32 = jnp.float32
IN_VMEM = pl.BlockSpec(memory_space=pltpu.VMEM)
IN_SMEM = pl.BlockSpec(memory_space=pltpu.SMEM)


def dot(left, right, left_dim, right_dim):
    return lax.dot_general(
        left, right, (((left_dim,), (right_dim,)), ((), ())), preferred_element_type=F32
    )


def mm(left, right):
    return jnp.dot(left, right, preferred_element_type=F32)


class Plan:
    def __init__(self):
        self.fsdp = lax.axis_size("fsdp")
        self.ctx = lax.axis_size("ctx")
        self.tp = lax.axis_size("tp")
        self.high = self.fsdp // 2
        f = lax.axis_index("fsdp")
        z = lax.axis_index("tp")
        self.c = f % 2
        self.fh = f // 2
        self.x = lax.axis_index("ctx")
        self.zl = z % 2
        self.zp = z // 2
        self.ci = self.x % 4
        self.part = self.c * 2 + self.zl
        self.peers = self.high * self.ctx

    def core(self, value):
        return lax.ppermute(value, "fsdp", [(i, i ^ 1) for i in range(self.fsdp)])

    def near(self, value):
        return lax.ppermute(value, "tp", [(i, i ^ 1) for i in range(self.tp)])

    def far(self, value):
        return lax.ppermute(value, "tp", [(i, i ^ 2) for i in range(self.tp)])

    def side(self, value, k):
        return lax.ppermute(value, "ctx", [(i, i ^ k) for i in range(self.ctx)])

    def high_fsdp(self, value, k):
        return lax.ppermute(value, "fsdp", [(i, i ^ (2 * k)) for i in range(self.fsdp)])


def flip_list(blocks, index):
    bit = 1
    while bit < len(blocks):
        on = (index & bit) != 0
        blocks = [jnp.where(on, blocks[i ^ bit], blocks[i]) for i in range(len(blocks))]
        bit *= 2
    return blocks


def place(blocks, index, axis):
    width = blocks[0].shape[axis]
    shape = list(blocks[0].shape)
    shape[axis] = width * len(blocks)
    full = jnp.zeros(shape, blocks[0].dtype)
    for i, block in enumerate(blocks):
        full = lax.dynamic_update_slice_in_dim(full, block, (index ^ i) * width, axis)
    return full


def to_block_order(plan, rows):
    width = rows.shape[1] // (2 * plan.peers)
    parts = []
    for h in range(plan.high):
        for x in range(plan.ctx):
            for c in range(2):
                start = ((h * 2 + c) * plan.ctx + x) * width
                parts.append(rows[:, start : start + width])
    return jnp.concatenate(parts, axis=1)


def from_block_order(plan, rows):
    width = rows.shape[1] // (2 * plan.peers)
    parts = []
    for h in range(plan.high):
        for c in range(2):
            for x in range(plan.ctx):
                start = ((h * plan.ctx + x) * 2 + c) * width
                parts.append(rows[:, start : start + width])
    return jnp.concatenate(parts, axis=1)


def gather_rows(plan, rows):
    pair = jnp.concatenate([rows, plan.near(rows)], axis=0)
    return jnp.concatenate([pair, plan.core(pair)], axis=0)


def sum_rows(plan, partial):
    half = partial.shape[0] // 2
    pair = partial[:half] + plan.core(partial[half:].astype(BF)).astype(F32)
    half = half // 2
    return pair[:half] + plan.near(pair[half:].astype(BF)).astype(F32)


def natural_rows(plan, rows):
    count = rows.shape[0] // 4
    parts = [
        lax.dynamic_slice_in_dim(rows, (plan.part ^ i) * count, count, 0) for i in range(4)
    ]
    return jnp.concatenate(parts, axis=0)


def own_columns(plan, halves):
    keep = lax.dynamic_index_in_dim(halves, plan.c, 0, False)
    got = plan.core(lax.dynamic_index_in_dim(halves, 1 - plan.c, 0, False))
    return jnp.where(
        plan.c == 0,
        jnp.concatenate([keep, got], axis=1),
        jnp.concatenate([got, keep], axis=1),
    )


def all_columns(plan, rows, direct):
    if direct and plan.peers == 4:
        return place([rows] + [plan.side(rows, k) for k in range(1, 4)], plan.x, 1)
    full = lax.all_gather(rows, "ctx", axis=1, tiled=True)
    if plan.high > 1:
        parts = [full] + [plan.high_fsdp(full, k) for k in range(1, plan.high)]
        full = place(parts, plan.fh, 1)
    return full


def columns_sum(plan, grad, direct):
    if plan.high > 1:
        width = grad.shape[1] // plan.high
        parts = [
            lax.dynamic_slice_in_dim(grad, (plan.fh ^ k) * width, width, 1)
            for k in range(plan.high)
        ]
        grad = parts[0]
        for k in range(1, plan.high):
            grad = grad + plan.high_fsdp(parts[k], k)
    if direct and plan.ctx == 4:
        width = grad.shape[1] // 4
        parts = [
            lax.dynamic_slice_in_dim(grad, (plan.x ^ k) * width, width, 1) for k in range(4)
        ]
        total = parts[0].astype(F32)
        for k in range(1, 4):
            total = total + plan.side(parts[k], k).astype(F32)
        return total
    return lax.psum_scatter(grad, "ctx", scatter_dimension=1, tiled=True).astype(F32)


def gather_weights(plan, groups, direct):
    own = own_columns(plan, jnp.concatenate(groups, axis=1))
    far = plan.far(own)
    parts = []
    start = 0
    for group in groups:
        rows = group.shape[1]
        parts += [own[start : start + rows], far[start : start + rows]]
        start += rows
    return all_columns(plan, jnp.concatenate(parts, axis=0), direct)


def scatter_grads(plan, grads, direct):
    total = columns_sum(plan, jnp.concatenate(grads, axis=0), direct)
    mine, far = [], []
    start = 0
    for grad in grads:
        rows = grad.shape[0] // 2
        mine.append(total[start : start + rows])
        far.append(total[start + rows : start + 2 * rows])
        start += 2 * rows
    got = plan.far(jnp.concatenate(far, axis=0).astype(BF)).astype(F32)
    own = jnp.concatenate(mine, axis=0) + got
    width = own.shape[1]
    left, right = own[:, : width // 2], own[:, width // 2 :]
    kept = jnp.where(plan.c == 0, left, right)
    got = plan.core(jnp.where(plan.c == 0, right, left).astype(BF)).astype(F32)
    low = jnp.where(plan.c == 0, kept, got)
    high = jnp.where(plan.c == 0, got, kept)
    out = []
    start = 0
    for grad in grads:
        rows = grad.shape[0] // 2
        out.append((low[start : start + rows], high[start : start + rows]))
        start += rows
    return out


def split_hidden(weight):
    return weight.reshape(2, weight.shape[0] // 2, weight.shape[1])


def turn(values, cos_tab, sine_tab):
    first, second = values[..., :HALF, :], values[..., HALF:, :]
    return jnp.concatenate(
        [first * cos_tab - second * sine_tab, second * cos_tab + first * sine_tab], axis=-2
    )


def to_heads(plan, values):
    got = [lax.dynamic_index_in_dim(values, plan.ci, 0, False)]
    for k in range(1, 4):
        got.append(plan.side(lax.dynamic_index_in_dim(values, plan.ci ^ k, 0, False), k))
    return got


def from_heads(plan, blocks):
    got = [blocks[0]] + [plan.side(blocks[k], k) for k in range(1, 4)]
    return place([block[None] for block in got], plan.ci, 0)


def more_keys(plan, blocks):
    full = list(blocks)
    for m in range(1, plan.ctx // 4):
        full += [plan.side(block, 4 * m) for block in blocks]
    return full


def more_keys_sum(plan, blocks):
    total = list(blocks[:4])
    for m in range(1, plan.ctx // 4):
        total = [total[k] + plan.side(blocks[4 * m + k], 4 * m) for k in range(4)]
    return total


def seen(first_row, part, key_block, query_block, size):
    turned = part * (size // 4)
    key = key_block * size + (lax.broadcasted_iota(jnp.int32, (size, 1), 0) ^ turned)
    query = query_block * size + (lax.broadcasted_iota(jnp.int32, (1, size), 1) ^ turned)
    return (key <= query) & (key >= first_row)


def attend_kernel(count, place_ref, first_ref, *refs):
    blocks, (out_ref, low_ref, lse_ref, kt_ref, v_ref) = refs[:count], refs[count:]
    size = blocks[0].shape[2]
    x, part = place_ref[0], place_ref[1]
    for k in range(count):
        kt_ref[x ^ k] = blocks[k][1].T
        v_ref[x ^ k] = blocks[k][2]
    for k in range(4):
        block = x ^ k
        query = blocks[k][0] * BF(HEAD ** (-0.5))
        first_row = first_ref[k]

        def step(kb, carry):
            peak, total, acc = carry
            s = mm(kt_ref[kb], query)
            s = jnp.where(seen(first_row, part, kb, block, size), s, NEG)
            top = jnp.maximum(peak, jnp.max(s, axis=0, keepdims=True))
            p = jnp.exp(s - top)
            fade = jnp.exp(peak - top)
            total = fade * total + jnp.sum(p, axis=0, keepdims=True)
            return top, total, fade * acc + mm(v_ref[kb], p.astype(BF))

        start = (
            jnp.full((1, size), NEG, F32),
            jnp.zeros((1, size), F32),
            jnp.zeros((HEAD, size), F32),
        )
        peak, total, acc = lax.fori_loop(place_ref[2 + block], block + 1, step, start)
        acc = acc / total
        out_ref[k] = acc
        low_ref[k] = acc.astype(BF)
        lse_ref[k] = peak + jnp.log(total)


def attend(where_all, first_query, blocks):
    count = len(blocks)
    size = blocks[0].shape[2]
    return pl.pallas_call(
        functools.partial(attend_kernel, count),
        out_shape=(
            jax.ShapeDtypeStruct((4, HEAD, size), F32),
            jax.ShapeDtypeStruct((4, HEAD, size), BF),
            jax.ShapeDtypeStruct((4, 1, size), F32),
        ),
        in_specs=[IN_SMEM] + [IN_VMEM] * (1 + count),
        out_specs=(IN_VMEM,) * 3,
        scratch_shapes=[
            pltpu.VMEM((count, size, HEAD), BF),
            pltpu.VMEM((count, HEAD, size), BF),
        ],
        name="attend",
    )(where_all, first_query, *blocks)


def back_kernel(count, place_ref, first_ref, out_ref, lse_ref, *refs):
    blocks, grads = refs[:count], refs[count : count + 4]
    dq_ref, dk_ref, dv_ref, kt_ref, vt_ref, k_ref, dks_ref, dvs_ref = refs[count + 4 :]
    size = blocks[0].shape[2]
    x, part = place_ref[0], place_ref[1]
    for k in range(count):
        kt_ref[x ^ k] = blocks[k][1].T
        vt_ref[x ^ k] = blocks[k][2].T
        k_ref[x ^ k] = blocks[k][1]
    dks_ref[...] = jnp.zeros_like(dks_ref)
    dvs_ref[...] = jnp.zeros_like(dvs_ref)
    for k in range(4):
        block = x ^ k
        query = blocks[k][0] * BF(HEAD ** (-0.5))
        query_t = query.T
        grad = grads[k][...]
        grad_t = grad.T
        delta = jnp.sum(grad.astype(F32) * out_ref[k], axis=0, keepdims=True)
        lse = lse_ref[k]
        first_row = first_ref[k]

        def step(kb, dq):
            s = mm(kt_ref[kb], query)
            p = jnp.where(seen(first_row, part, kb, block, size), jnp.exp(s - lse), 0.0)
            dp = mm(vt_ref[kb], grad)
            ds = (p * (dp - delta)).astype(BF)
            dvs_ref[kb] += mm(p.astype(BF), grad_t)
            dks_ref[kb] += mm(ds, query_t)
            return dq + mm(k_ref[kb], ds)

        dq = lax.fori_loop(
            place_ref[2 + block], block + 1, step, jnp.zeros((HEAD, size), F32)
        )
        dq_ref[k] = dq * HEAD ** (-0.5)
    for k in range(count):
        dk_ref[k] = dks_ref[x ^ k].T
        dv_ref[k] = dvs_ref[x ^ k].T


def attend_back(where_all, first_query, blocks, grads, out, log_total):
    count = len(blocks)
    size = blocks[0].shape[2]
    return pl.pallas_call(
        functools.partial(back_kernel, count),
        out_shape=(
            jax.ShapeDtypeStruct((4, HEAD, size), F32),
            jax.ShapeDtypeStruct((count, HEAD, size), F32),
            jax.ShapeDtypeStruct((count, HEAD, size), F32),
        ),
        in_specs=[IN_SMEM] + [IN_VMEM] * (3 + count + 4),
        out_specs=(IN_VMEM,) * 3,
        scratch_shapes=[
            pltpu.VMEM((count, size, HEAD), BF),
            pltpu.VMEM((count, size, HEAD), BF),
            pltpu.VMEM((count, HEAD, size), BF),
            pltpu.VMEM((count, size, HEAD), F32),
            pltpu.VMEM((count, size, HEAD), F32),
        ],
        name="attend_back",
    )(where_all, first_query, out, log_total, *blocks, *grads)


def norm_scale(stream):
    return lax.rsqrt(jnp.mean(stream * stream, axis=-1, keepdims=True) + EPS)


def norm_back(stream, scale, gain, grad_normed):
    weighted = grad_normed * gain
    grad_gain = jnp.sum(grad_normed * stream * scale, axis=0, keepdims=True)
    grad_stream = scale * weighted - stream * scale**3 * jnp.mean(
        weighted * stream, axis=1, keepdims=True
    )
    return (grad_gain, grad_stream)


def local(
    tokens,
    out_grad,
    segment_ids,
    owner_order,
    attn_gain,
    w_query,
    w_key,
    w_value,
    w_out,
    mlp_gain,
    w_gate,
    w_up,
    w_down,
):
    plan = Plan()
    tok_rows = tokens.shape[0]
    part_rows = tok_rows // 4
    model = tokens.shape[1]

    gains = jnp.concatenate([attn_gain, mlp_gain], axis=0)
    gains = jnp.concatenate([gains, jnp.zeros((12, gains.shape[1]), BF)], axis=0)
    full = []
    for level in range(LAYERS):
        qkv = jnp.concatenate(
            [split_hidden(w[level].T) for w in (w_query, w_key, w_value)], axis=1
        )
        w_attn = gather_weights(plan, [qkv, split_hidden(w_out[level])], level == 0)
        w_mlp = gather_weights(
            plan,
            [split_hidden(w) for w in (w_gate[level].T, w_up[level].T, w_down[level])],
            False,
        )
        cut = 2 * qkv.shape[1]
        gated = 2 * w_gate.shape[2]
        full.append((w_attn[:cut], w_attn[cut:], w_mlp[:gated], w_mlp[gated:]))
    got = plan.core(gains)
    gain_pair = jnp.where(
        plan.c == 0,
        jnp.concatenate([gains, got], axis=1),
        jnp.concatenate([got, gains], axis=1),
    )
    gain_full = all_columns(plan, gain_pair, True).astype(F32)

    def own_rows(array):
        mine = lax.dynamic_slice_in_dim(array, plan.part * part_rows, part_rows, 0)
        got = plan.core(
            lax.dynamic_slice_in_dim(array, (plan.part ^ 2) * part_rows, part_rows, 0)
        )
        return to_block_order(plan, jnp.where(plan.c == plan.zp, mine, got))

    stream = own_rows(tokens).astype(F32)
    grad_stream = own_rows(out_grad).astype(F32)

    segment = jnp.where(plan.c == plan.zp, segment_ids, plan.core(segment_ids))[0]
    pack = segment.shape[0]
    index_all = jnp.arange(pack, dtype=jnp.int32)
    run_start = jnp.concatenate([jnp.ones((1,), dtype=bool), segment[1:] != segment[:-1]])
    run_first = lax.cummax(jnp.where(run_start, index_all, jnp.zeros_like(index_all)), axis=0)
    where_all = jnp.concatenate(
        [jnp.stack([plan.x, plan.part]).astype(jnp.int32), run_first[::tok_rows] // tok_rows]
    )

    def by_peer(row):
        grid = row.reshape(plan.ctx, 4, part_rows)
        blocks = [lax.dynamic_index_in_dim(grid, plan.x ^ k, 0, False) for k in range(4)]
        grid = jnp.stack(blocks)
        return jnp.concatenate(flip_list([grid[:, i] for i in range(4)], plan.part), axis=1)

    positions = by_peer((index_all - run_first).astype(F32))
    first_query = by_peer(run_first)[:, None, :]
    frequency = THETA ** (-(jnp.arange(HALF, dtype=F32) * 2.0 / HEAD))
    angles = frequency[None, :, None] * positions[:, None, :]
    cos_all, sine_all = jnp.cos(angles), jnp.sin(angles)
    cos_own, sine_own = cos_all[0], sine_all[0]

    kept = []
    first_values = None
    for level in range(LAYERS):
        w_qkv, w_o, w_gu, w_d = full[level]
        width = w_d.shape[0]
        scale_attn = norm_scale(stream)
        normed = (stream * scale_attn * gain_full[level : level + 1]).astype(BF)
        normed_all = gather_rows(plan, normed)
        qkv = dot(w_qkv, normed_all, 1, 1).reshape(2, 3, 2, HEAD, tok_rows)
        query = turn(qkv[:, 0], cos_own, sine_own).astype(BF)
        key = turn(qkv[:, 1], cos_own, sine_own).astype(BF)
        if level == 0:
            first_values = qkv[:, 2]
            mixed = first_values
        else:
            mixed = 0.5 * qkv[:, 2] + 0.5 * first_values
        heads = jnp.stack([query, key, mixed.astype(BF)], axis=2)
        heads = more_keys(plan, to_heads(plan, heads.reshape(4, 3, HEAD, tok_rows)))
        out, out_low, log_total = attend(where_all, first_query, heads)
        attended = from_heads(plan, [out_low[k] for k in range(4)])
        attended = attended.reshape(4 * HEAD, tok_rows)
        middle = stream + sum_rows(plan, dot(attended, w_o, 0, 0))
        scale_mlp = norm_scale(middle)
        normed_mlp = (middle * scale_mlp * gain_full[2 + level : 3 + level]).astype(BF)
        normed_mlp_all = gather_rows(plan, normed_mlp)
        gate_up = dot(normed_mlp_all, w_gu, 1, 1)
        gate, upward = gate_up[:, :width], gate_up[:, width:]
        hidden = (gate * jax.nn.sigmoid(gate) * upward).astype(BF)
        result = middle + sum_rows(plan, dot(hidden, w_d, 1, 0))
        kept.append(
            (
                stream,
                scale_attn,
                normed_all,
                heads,
                out,
                log_total,
                attended,
                middle,
                scale_mlp,
                normed_mlp_all,
                gate_up,
                hidden,
            )
        )
        stream = result

    def to_pack(rows):
        block = gather_rows(plan, rows)
        pairs = []
        for f in range(plan.fsdp):
            for z in range(plan.tp):
                if f % 2 == z // 2:
                    pairs.append((f * plan.tp + z, f * plan.tp + (z ^ 2)))
        got = lax.ppermute(block, ("fsdp", "tp"), pairs)
        return jnp.where(plan.c == plan.zp, block, got)

    outputs = natural_rows(plan, to_pack(from_block_order(plan, stream.astype(BF))))

    grads = [None] * LAYERS
    gain_rows = [None] * (2 * LAYERS)
    carried = None
    for level in reversed(range(LAYERS)):
        (
            stream,
            scale_attn,
            normed_all,
            heads,
            out,
            log_total,
            attended,
            middle,
            scale_mlp,
            normed_mlp_all,
            gate_up,
            hidden,
        ) = kept[level]
        w_qkv, w_o, w_gu, w_d = full[level]
        width = w_d.shape[0]
        branch = gather_rows(plan, grad_stream.astype(BF))
        grad_hidden = dot(branch, w_d, 1, 1)
        gate, upward = gate_up[:, :width], gate_up[:, width:]
        sigma = jax.nn.sigmoid(gate)
        grad_gate = (grad_hidden * upward * sigma * (1.0 + gate * (1.0 - sigma))).astype(BF)
        grad_up = (grad_hidden * gate * sigma).astype(BF)
        grad_gu = jnp.concatenate([grad_gate, grad_up], axis=1)
        grad_normed = sum_rows(plan, dot(grad_gu, w_gu, 1, 0))
        grad_wgu = dot(grad_gu, normed_mlp_all, 0, 0).astype(BF)
        grad_wd = dot(hidden, branch, 0, 0).astype(BF)
        grad_wg, grad_wu, grad_wd = scatter_grads(
            plan, [grad_wgu[:width], grad_wgu[width:], grad_wd], False
        )
        gain_rows[2 + level], through = norm_back(
            middle, scale_mlp, gain_full[2 + level : 3 + level], grad_normed
        )
        grad_middle = grad_stream + through
        branch = gather_rows(plan, grad_middle.astype(BF))
        grad_wo = dot(attended, branch, 1, 0).astype(BF)
        grad_attended = dot(w_o, branch, 1, 1).astype(BF)
        grad_attended = to_heads(plan, grad_attended.reshape(4, HEAD, tok_rows))
        grad_q, grad_k, grad_v = attend_back(
            where_all, first_query, heads, grad_attended, out, log_total
        )
        grad_k = more_keys_sum(plan, grad_k)
        grad_v = more_keys_sum(plan, grad_v)
        if level > 0:
            grad_v = [0.5 * block for block in grad_v]
            if carried is None:
                carried = grad_v
            else:
                carried = [left + right for left, right in zip(carried, grad_v)]
        else:
            grad_v = [left + right for left, right in zip(grad_v, carried)]
        grad_heads = [
            jnp.stack(
                [
                    turn(grad_q[k], cos_all[k], -sine_all[k]).astype(BF),
                    turn(grad_k[k], cos_all[k], -sine_all[k]).astype(BF),
                    grad_v[k].astype(BF),
                ]
            )
            for k in range(4)
        ]
        grad_qkv = from_heads(plan, grad_heads).reshape(2, 2, 3, HEAD, tok_rows)
        grad_qkv = jnp.swapaxes(grad_qkv, 1, 2).reshape(-1, tok_rows)
        grad_wqkv = dot(grad_qkv, normed_all, 1, 0).astype(BF)
        grad_wqkv, grad_wo = scatter_grads(plan, [grad_wqkv, grad_wo], level == 0)
        grad_normed = sum_rows(plan, dot(grad_qkv, w_qkv, 0, 0))
        gain_rows[level], through = norm_back(
            stream, scale_attn, gain_full[level : level + 1], grad_normed
        )
        grad_stream = grad_middle + through
        third = grad_wqkv[0].shape[0] // 3

        def member(i):
            rows = [half[i * third : (i + 1) * third] for half in grad_wqkv]
            return jnp.concatenate(rows, axis=0).T

        grads[level] = (
            member(0),
            member(1),
            member(2),
            jnp.concatenate(grad_wo, axis=0),
            jnp.concatenate(grad_wg, axis=0).T,
            jnp.concatenate(grad_wu, axis=0).T,
            jnp.concatenate(grad_wd, axis=0),
        )

    gain_sum = jnp.concatenate(gain_rows + [jnp.zeros((4, model), F32)], axis=0)
    total = columns_sum(plan, gain_sum, True)
    width = total.shape[1]
    total = total + plan.far(total)
    total = total + plan.near(total)
    left, right = total[:, : width // 2], total[:, width // 2 :]
    mine = jnp.where(plan.c == 0, left, right)
    theirs = jnp.where(plan.c == 0, right, left)
    total = mine + plan.core(theirs)

    grad_block = to_pack(from_block_order(plan, grad_stream.astype(BF)))
    group_rows = tok_rows // plan.ctx
    owner_grid = owner_order[0].reshape(plan.ctx, plan.ctx, group_rows)
    local_rows = (
        lax.dynamic_index_in_dim(owner_grid, plan.x, 1, False) - plan.x * tok_rows
    ).reshape(tok_rows)
    local_rows = local_rows ^ (plan.part * part_rows)
    grad_tokens = lax.all_to_all(
        grad_block[local_rows], "ctx", split_axis=0, concat_axis=0, tiled=True
    ).astype(F32)

    stacked = [jnp.stack([grads[level][i] for level in range(LAYERS)]) for i in range(7)]
    return (
        outputs,
        grad_tokens,
        total[:2],
        stacked[0],
        stacked[1],
        stacked[2],
        stacked[3],
        total[2:4],
        stacked[4],
        stacked[5],
        stacked[6],
    )


def solution(mesh):
    columns = P(None, ("fsdp", "ctx"), "tp")
    rows = P(None, "tp", ("fsdp", "ctx"))
    gain = P(None, ("fsdp", "ctx"))
    tokens = P(("fsdp", "ctx"), None)
    return jax.shard_map(
        local,
        mesh=mesh,
        in_specs=(
            tokens,
            tokens,
            P("fsdp", None),
            P("fsdp", None),
            gain,
            columns,
            columns,
            columns,
            rows,
            gain,
            columns,
            columns,
            rows,
        ),
        out_specs=(
            tokens,
            tokens,
            gain,
            columns,
            columns,
            columns,
            rows,
            gain,
            columns,
            columns,
            rows,
        ),
        check_vma=False,
    )
```

time: 823 us -> 652 us (0.79)
  starting transfers between devices: 202 us -> 94.3 us
  matrix products: 126 us -> 55.8 us
  other arithmetic: 96.9 us -> 58.4 us
  Pallas kernels: 0 us -> 36.8 us
  between operations: 5.92 us -> 17.3 us
  waiting for transfers between devices: 342 us -> 333 us
  local copies, waits for them, and re-layouts: 41 us -> 49.3 us
    ppermute x120 -> x36, starting transfers between devices: 143 us -> 44.3 us  [side(): return lax.ppermute(value, 'ctx', [(i, i ^ k) for i in range(self.ctx)])]
    ppermute x120 -> x36, waiting for transfers between devices: 178 us -> 97.6 us  [side(): return lax.ppermute(value, 'ctx', [(i, i ^ k) for i in range(self.ctx)])]
    dot_general x42 -> x24, matrix products: 126 us -> 55.8 us  [dot(): lax.dot_general(left, right, (((left_dim,), (right_dim,)), ((), ())), pre...]
    pallas_call x0 -> x4, Pallas kernels: none -> 36.8 us  [the longest x2 20.9 us: attend_back(): pl.pallas_call(functools.partial(back_kernel, count), out_shape=(jax.Shap...]
    ppermute x21 -> x9, waiting for transfers between devices: 74.9 us -> 109 us  [far(): return lax.ppermute(value, 'tp', [(i, i ^ 2) for i in range(self.tp)])]
    ppermute x19, waiting for transfers between devices: 74.1 us -> 98.2 us  [near(): return lax.ppermute(value, 'tp', [(i, i ^ 1) for i in range(self.tp)])]
    convert_element_type x31 -> x9, other arithmetic: 21.3 us -> 2.19 us  [the longest x2 1.24 us: local(): grad_v[k].astype(BF)]
    select_n x65 -> x15, other arithmetic: 21.8 us -> 3.93 us  [the longest x2 2.05 us: own_rows(): return to_block_order(plan, jnp.where(plan.c == plan.zp, mine, got))]
  transfers between devices with their start and end apart: 206 -> 104, of which waited for: 109 -> 67; matrix products, arithmetic and copies ran while one was open for 28% -> 20% of each run, Pallas kernels for 0% -> 4%
where the time goes in v2:
time: 652 us; the launch traced here: 645 us
  waiting for transfers between devices  333 us (51%)
  starting transfers between devices  94.3 us (14%)
  other arithmetic  58.4 us (9%)
  matrix products  55.8 us (9%)
  local copies, waits for them, and re-layouts  49.3 us (8%)
  Pallas kernels  36.8 us (6%)
  between operations  17.3 us (3%)
    ppermute x9, waiting for transfers between devices, far(): return lax.ppermute(value, 'tp', [(i, i ^ 2) for i in range(self.tp)])  109 us
    ppermute x19, waiting for transfers between devices, near(): return lax.ppermute(value, 'tp', [(i, i ^ 1) for i in range(self.tp)])  98.2 us
    ppermute x36, waiting for transfers between devices, side(): return lax.ppermute(value, 'ctx', [(i, i ^ k) for i in range(self.ctx)])  97.6 us
    dot_general x24, matrix products, dot(): lax.dot_general(left, right, (((left_dim,), (right_dim,)), ((), ())), pre...  55.8 us
    ppermute x36, starting transfers between devices, side(): return lax.ppermute(value, 'ctx', [(i, i ^ k) for i in range(self.ctx)])  44.3 us
    pallas_call x2, Pallas kernels, attend_back(): pl.pallas_call(functools.partial(back_kernel, count), out_shape=(jax.Shap...  20.9 us
    ppermute x31, waiting for transfers between devices, core(): return lax.ppermute(value, 'fsdp', [(i, i ^ 1) for i in range(self.fsdp)])  16.6 us
    ppermute x31, starting transfers between devices, core(): return lax.ppermute(value, 'fsdp', [(i, i ^ 1) for i in range(self.fsdp)])  16.1 us
  transfers between devices with their start and end apart: 104, of which 67 were waited for; matrix products, arithmetic and copies ran while one was open for 20% of the time, Pallas kernels for 4%

profile of v2, /device:TPU:0, one launch (start us, length us, event | category | flops | bytes accessed | tf_op | source)
XLA Modules:
  0.0 644.5 jit_solution(6127197289621221120)
XLA Ops:
  26.8 3.7 collective-permute-done.10
  37.7 19.1 %collective-permute-done.3 = bf16[512,256]{1,0:T(8,128)(2,1)S(1)} collective-permute-done((bf16[512,256]{1,0:T(8,128)(2,1)S(1)}, bf16[512,256]{1,0:T(8,128)(2,1)S(1)}, u32[]{:S(2)}, u32[]{:S(2)}) %collective-permute-start.3) | collective-permute-done | bytes 262176 | tf_op jit(solution)/shard_map/ppermute | solution.py:56
  60.5 6.8 %collective-permute-done.24 = bf16[1056,256]{1,0:T(8,128)(2,1)S(1)} collective-permute-done((bf16[1056,256]{1,0:T(8,128)(2,1)S(1)}, bf16[1056,256]{1,0:T(8,128)(2,1)S(1)}, u32[]{:S(2)}, u32[]{:S(2)}) %collective-permute-start.24) | collective-permute-done | bytes 540704 | tf_op jit(solution)/shard_map/ppermute | solution.py:56
  69.2 3.3 collective-permute-done.4
  74.3 6.3 collective-permute-done.5
  82.5 5.3 collective-permute-done.6
  103.6 7.8 %attend.2 = (f32[4,64,512]{2,1,0:T(8,128)}, bf16[4,64,512]{2,1,0:T(8,128)(2,1)}, f32[4,1,512]{2,1,0:T(1,128)}) custom-call(s32[6]{0:T(128)} %pad_add_fusion.2.place_ref, s32[4,1,512]{2,1,0:T(1,128)} %broadcast_in_dim.84.first_ref, bf16[3,64,512]{2,1,0:T(8,128)(2,1)} %get-tuple-element.168.refs_0_, bf16[3,64,512]{2,1,0:T(8,128)(2,1)} %copy-done.30, ...), custom_call_target="tpu_custom_call" | custom-call | tf_op jit(solution)/shard_map/attend/pallas_call | solution.py:287
  129.6 5.3 collective-permute-done.20
  139.2 3.7 collective-permute-start.28
  144.6 10.5 %collective-permute-done.28 = bf16[512,256]{1,0:T(8,128)(2,1)S(1)} collective-permute-done((bf16[512,256]{1,0:T(8,128)(2,1)S(1)}, bf16[512,256]{1,0:T(8,128)(2,1)S(1)}, u32[]{:S(2)}, u32[]{:S(2)}) %collective-permute-start.28) | collective-permute-done | bytes 262176 | tf_op jit(solution)/shard_map/ppermute | solution.py:56
  156.4 3.9 fusion.6
  160.8 3.3 fusion.22
  168.7 23.7 %collective-permute-done.42 = bf16[1056,256]{1,0:T(8,128)(2,1)S(1)} collective-permute-done((bf16[1056,256]{1,0:T(8,128)(2,1)S(1)}, bf16[1056,256]{1,0:T(8,128)(2,1)S(1)}, u32[]{:S(2)}, u32[]{:S(2)}) %collective-permute-start.42) | collective-permute-done | bytes 540704 | tf_op jit(solution)/shard_map/ppermute | solution.py:56
  193.4 8.2 %collective-permute-done.29 = bf16[128,1024]{1,0:T(8,128)(2,1)S(1)} collective-permute-done((bf16[128,1024]{1,0:T(8,128)(2,1)S(1)}, bf16[128,1024]{1,0:T(8,128)(2,1)S(1)}, u32[]{:S(2)}, u32[]{:S(2)}) %collective-permute-start.29) | collective-permute-done | bytes 262176 | tf_op jit(solution)/shard_map/ppermute | solution.py:53
  214.2 7.4 %collective-permute-done.31.refs_1_ = bf16[3,64,512]{2,1,0:T(8,128)(2,1)S(1)} collective-permute-done((bf16[3,64,512]{2,1,0:T(8,128)(2,1)S(1)}, bf16[3,64,512]{2,1,0:T(8,128)(2,1)S(1)}, u32[]{:S(2)}, u32[]{:S(2)}) %collective-permute-start.31) | collective-permute-done | bytes 196640 | tf_op jit(solution)/shard_map/ppermute | solution.py:59
  224.3 4.2 collective-permute-done.33.refs_3_
  229.2 8.2 %attend.3 = (f32[4,64,512]{2,1,0:T(8,128)}, bf16[4,64,512]{2,1,0:T(8,128)(2,1)}, f32[4,1,512]{2,1,0:T(1,128)}) custom-call(s32[6]{0:T(128)} %pad_add_fusion.2.place_ref, s32[4,1,512]{2,1,0:T(1,128)} %broadcast_in_dim.84.first_ref, bf16[3,64,512]{2,1,0:T(8,128)(2,1)} %get-tuple-element.164.refs_0_, bf16[3,64,512]{2,1,0:T(8,128)(2,1)} %copy-done.33, ...), custom_call_target="tpu_custom_call" | custom-call | tf_op jit(solution)/shard_map/attend/pallas_call | solution.py:287
  253.4 8.3 %collective-permute-done.38 = bf16[128,1024]{1,0:T(8,128)(2,1)S(1)} collective-permute-done((bf16[128,1024]{1,0:T(8,128)(2,1)S(1)}, bf16[128,1024]{1,0:T(8,128)(2,1)S(1)}, u32[]{:S(2)}, u32[]{:S(2)}) %collective-permute-start.38) | collective-permute-done | bytes 262176 | tf_op jit(solution)/shard_map/ppermute | solution.py:53
  262.4 7.3 %collective-permute-done.39 = bf16[128,1024]{1,0:T(8,128)(2,1)S(1)} collective-permute-done((bf16[128,1024]{1,0:T(8,128)(2,1)S(1)}, bf16[128,1024]{1,0:T(8,128)(2,1)S(1)}, u32[]{:S(2)}, u32[]{:S(2)}) %collective-permute-start.39) | collective-permute-done | bytes 262176 | tf_op jit(solution)/shard_map/ppermute | solution.py:53
  271.1 8.2 %collective-permute-done.49 = bf16[128,1024]{1,0:T(8,128)(2,1)S(1)} collective-permute-done((bf16[128,1024]{1,0:T(8,128)(2,1)S(1)}, bf16[128,1024]{1,0:T(8,128)(2,1)S(1)}, u32[]{:S(2)}, u32[]{:S(2)}) %collective-permute-start.49) | collective-permute-done | bytes 262176 | tf_op jit(solution)/shard_map/ppermute | solution.py:53
  280.8 3.9 fusion.2
  294.0 6.8 %collective-permute-done.52 = bf16[128,1024]{1,0:T(8,128)(2,1)S(1)} collective-permute-done((bf16[128,1024]{1,0:T(8,128)(2,1)S(1)}, bf16[128,1024]{1,0:T(8,128)(2,1)S(1)}, u32[]{:S(2)}, u32[]{:S(2)}) %collective-permute-start.52) | collective-permute-done | bytes 262176 | tf_op jit(solution)/shard_map/ppermute | solution.py:53
  301.6 4.3 collective-permute-done.44
  307.6 7.2 %collective-permute-done.53 = bf16[128,1024]{1,0:T(8,128)(2,1)S(1)} collective-permute-done((bf16[128,1024]{1,0:T(8,128)(2,1)S(1)}, bf16[128,1024]{1,0:T(8,128)(2,1)S(1)}, u32[]{:S(2)}, u32[]{:S(2)}) %collective-permute-start.53) | collective-permute-done | bytes 262176 | tf_op jit(solution)/shard_map/ppermute | solution.py:53
  326.6 10.4 %attend_back.2 = (f32[4,64,512]{2,1,0:T(8,128)}, f32[4,64,512]{2,1,0:T(8,128)}, f32[4,64,512]{2,1,0:T(8,128)}) custom-call(s32[6]{0:T(128)} %pad_add_fusion.2.place_ref, s32[4,1,512]{2,1,0:T(1,128)} %broadcast_in_dim.84.first_ref, f32[4,64,512]{2,1,0:T(8,128)} %get-tuple-element.25.out_ref, f32[4,1,512]{2,1,0:T(1,128)} %get-tuple-element.26.lse_ref, ...), custom_call_target="tpu_custom_call" | custom-call | tf_op jit(solution)/shard_map/attend_back/pallas_call | solution.py:346
  344.0 6.8 %collective-permute-done.58 = bf16[3,64,512]{2,1,0:T(8,128)(2,1)S(1)} collective-permute-done((bf16[3,64,512]{2,1,0:T(8,128)(2,1)S(1)}, bf16[3,64,512]{2,1,0:T(8,128)(2,1)S(1)}, u32[]{:S(2)}, u32[]{:S(2)}) %collective-permute-start.58) | collective-permute-done | bytes 196640 | tf_op jit(solution)/shard_map/ppermute | solution.py:59
  367.7 5.8 collective-permute-done.62
  377.2 7.3 %collective-permute-done.63 = bf16[128,1024]{1,0:T(8,128)(2,1)S(1)} collective-permute-done((bf16[128,1024]{1,0:T(8,128)(2,1)S(1)}, bf16[128,1024]{1,0:T(8,128)(2,1)S(1)}, u32[]{:S(2)}, u32[]{:S(2)}) %collective-permute-start.63) | collective-permute-done | bytes 262176 | tf_op jit(solution)/shard_map/ppermute | solution.py:53
  394.9 6.2 collective-permute-done.45
  402.0 4.3 collective-permute-done.66
  414.8 3.7 collective-permute-done.67
  420.4 5.1 convolution_convert_fusion.1
  440.3 10.5 %attend_back.3 = (f32[4,64,512]{2,1,0:T(8,128)}, f32[4,64,512]{2,1,0:T(8,128)}, f32[4,64,512]{2,1,0:T(8,128)}) custom-call(s32[6]{0:T(128)} %pad_add_fusion.2.place_ref, s32[4,1,512]{2,1,0:T(1,128)} %broadcast_in_dim.84.first_ref, f32[4,64,512]{2,1,0:T(8,128)} %get-tuple-element.30.out_ref, f32[4,1,512]{2,1,0:T(1,128)} %get-tuple-element.31.lse_ref, ...), custom_call_target="tpu_custom_call" | custom-call | tf_op jit(solution)/shard_map/attend_back/pallas_call | solution.py:346
  458.0 6.6 %collective-permute-done.72 = bf16[3,64,512]{2,1,0:T(8,128)(2,1)S(1)} collective-permute-done((bf16[3,64,512]{2,1,0:T(8,128)(2,1)S(1)}, bf16[3,64,512]{2,1,0:T(8,128)(2,1)S(1)}, u32[]{:S(2)}, u32[]{:S(2)}) %collective-permute-start.72) | collective-permute-done | bytes 196640 | tf_op jit(solution)/shard_map/ppermute | solution.py:59
  478.4 4.5 collective-permute-done.86
  482.9 3.6 collective-permute-done.87
  486.5 15.2 %collective-permute-done.88 = bf16[1024,256]{1,0:T(8,128)(2,1)} collective-permute-done((bf16[1024,256]{1,0:T(8,128)(2,1)S(1)}, bf16[1024,256]{1,0:T(8,128)(2,1)}, u32[]{:S(2)}, u32[]{:S(2)}) %collective-permute-start.88) | collective-permute-done | bytes 524320 | tf_op jit(solution)/shard_map/ppermute | solution.py:59
  506.4 5.0 collective-permute-done.89
  511.5 4.1 collective-permute-done.76
  524.7 10.4 %collective-permute-done.83 = f32[8,256]{1,0:T(8,128)S(1)} collective-permute-done((f32[8,256]{1,0:T(8,128)S(1)}, f32[8,256]{1,0:T(8,128)S(1)}, u32[]{:S(2)}, u32[]{:S(2)}) %collective-permute-start.83) | collective-permute-done | bytes 8224 | tf_op jit(solution)/shard_map/ppermute | solution.py:56
  535.2 3.6 collective-permute-done.84
  540.7 6.9 %collective-permute-done.77 = bf16[128,1024]{1,0:T(8,128)(2,1)S(1)} collective-permute-done((bf16[128,1024]{1,0:T(8,128)(2,1)S(1)}, bf16[128,1024]{1,0:T(8,128)(2,1)S(1)}, u32[]{:S(2)}, u32[]{:S(2)}) %collective-permute-start.77) | collective-permute-done | bytes 262176 | tf_op jit(solution)/shard_map/ppermute | solution.py:53
  556.6 7.9 %collective-permute-done.79 = bf16[512,1024]{1,0:T(8,128)(2,1)} collective-permute-done((bf16[512,1024]{1,0:T(8,128)(2,1)S(1)}, bf16[512,1024]{1,0:T(8,128)(2,1)}, u32[]{:S(2)}, u32[]{:S(2)}) %collective-permute-start.79) | collective-permute-done | bytes 1048608 | tf_op jit(solution)/shard_map/ppermute | solution.py:509
  569.5 3.5 all-to-all-start
  575.5 4.2 collective-permute-start.95
  584.1 8.7 %collective-permute-done.95 = bf16[1056,256]{1,0:T(8,128)(2,1)S(1)} collective-permute-done((bf16[1056,256]{1,0:T(8,128)(2,1)S(1)}, bf16[1056,256]{1,0:T(8,128)(2,1)S(1)}, u32[]{:S(2)}, u32[]{:S(2)}) %collective-permute-start.95) | collective-permute-done | bytes 540704 | tf_op jit(solution)/shard_map/ppermute | solution.py:56
  593.0 11.8 %collective-permute-start.96 = (bf16[1056,128]{1,0:T(8,128)(2,1)S(1)}, bf16[1056,128]{1,0:T(8,128)(2,1)S(1)}, u32[]{:S(2)}, u32[]{:S(2)}) collective-permute-start(bf16[1056,128]{1,0:T(8,128)(2,1)S(1)} %select_convert_fusion), channel_id=1, source_target_pairs={{0,16},{16,0},{1,17},{17,1},{2,18},{18,2},{3,19},{19,3},{4,20},{20... | collective-permute-start | bytes 811016 | tf_op jit(solution)/shard_map/ppermute | solution.py:50
  607.3 25.2 %collective-permute-done.93 = bf16[1056,256]{1,0:T(8,128)(2,1)S(1)} collective-permute-done((bf16[1056,256]{1,0:T(8,128)(2,1)S(1)}, bf16[1056,256]{1,0:T(8,128)(2,1)S(1)}, u32[]{:S(2)}, u32[]{:S(2)}) %collective-permute-start.93) | collective-permute-done | bytes 540704 | tf_op jit(solution)/shard_map/ppermute | solution.py:56
  (708 shorter events, 268.9 us)
Async XLA Ops:
  7.2 149.2 %all-gather.4.cloned.1.call-start = ((), (), s32[]{:S(2)}) async-start(), calls=%async_computation.4 | async-start | bytes 5406720 | tf_op jit(solution)/shard_map/all_gather | solution.py:139
  8.3 25.0 %collective-permute-start = (bf16[128,1024]{1,0:T(8,128)(2,1)S(1)}, bf16[128,1024]{1,0:T(8,128)(2,1)S(1)}, u32[]{:S(2)}, u32[]{:S(2)}) collective-permute-start(bf16[128,1024]{1,0:T(8,128)(2,1)S(1)} %constant_dynamic-slice_fusion.18), channel_id=1, source_target_pairs={{0,16},{16,0},{1,17},{17,1},{2,18},{18,2},{3,19},{19,3},{4,20},{20... | collective-permute-start | bytes 786440 | tf_op jit(solution)/shard_map/ppermute | solution.py:50
  9.6 9.9 %collective-permute-start.7 = (bf16[16,128]{1,0:T(8,128)(2,1)S(1)}, bf16[16,128]{1,0:T(8,128)(2,1)S(1)}, u32[]{:S(2)}, u32[]{:S(2)}) collective-permute-start(bf16[16,128]{1,0:T(8,128)(2,1)S(1)} %pad_maximum_fusion.73), channel_id=1, source_target_pairs={{0,16},{16,0},{1,17},{17,1},{2,18},{18,2},{3,19},{19,3},{4,20},{20... | collective-permute-start | bytes 12296 | tf_op jit(solution)/shard_map/ppermute | solution.py:50
  16.2 14.4 %collective-permute-start.2 = (bf16[512,128]{1,0:T(8,128)(2,1)S(1)}, bf16[512,128]{1,0:T(8,128)(2,1)S(1)}, u32[]{:S(2)}, u32[]{:S(2)}) collective-permute-start(bf16[512,128]{1,0:T(8,128)(2,1)S(1)} %get-tuple-element.245), channel_id=1, source_target_pairs={{0,16},{16,0},{1,17},{17,1},{2,18},{18,2},{3,19},{19,3},{4,20},{20... | collective-permute-start | bytes 393224 | tf_op jit(solution)/shard_map/ppermute | solution.py:50
  18.9 16.4 %collective-permute-start.23 = (bf16[1056,128]{1,0:T(8,128)(2,1)S(1)}, bf16[1056,128]{1,0:T(8,128)(2,1)S(1)}, u32[]{:S(2)}, u32[]{:S(2)}) collective-permute-start(bf16[1056,128]{1,0:T(8,128)(2,1)S(1)} %get-tuple-element.196), channel_id=1, source_target_pairs={{0,16},{16,0},{1,17},{17,1},{2,18},{18,2},{3,19},{19,3},{4,20},{20... | collective-permute-start | bytes 811016 | tf_op jit(solution)/shard_map/ppermute | solution.py:50
  30.7 26.1 %collective-permute-start.3 = (bf16[512,256]{1,0:T(8,128)(2,1)S(1)}, bf16[512,256]{1,0:T(8,128)(2,1)S(1)}, u32[]{:S(2)}, u32[]{:S(2)}) collective-permute-start(bf16[512,256]{1,0:T(8,128)(2,1)S(1)} %maximum_select_fusion.2), channel_id=1, source_target_pairs={{0,2},{1,3},{2,0},{3,1},{4,6},{5,7},{6,4},{7,5},{8,10},{9,11},{10,... | collective-permute-start | bytes 786440 | tf_op jit(solution)/shard_map/ppermute | solution.py:56
  35.5 31.8 %collective-permute-start.24 = (bf16[1056,256]{1,0:T(8,128)(2,1)S(1)}, bf16[1056,256]{1,0:T(8,128)(2,1)S(1)}, u32[]{:S(2)}, u32[]{:S(2)}) collective-permute-start(bf16[1056,256]{1,0:T(8,128)(2,1)S(1)} %maximum_select_fusion), channel_id=1, source_target_pairs={{0,2},{1,3},{2,0},{3,1},{4,6},{5,7},{6,4},{7,5},{8,10},{9,11},{10,... | collective-permute-start | bytes 1622024 | tf_op jit(solution)/shard_map/ppermute | solution.py:56
  36.0 33.0 %collective-permute-start.11 = (bf16[128,1024]{1,0:T(8,128)(2,1)S(1)}, bf16[128,1024]{1,0:T(8,128)(2,1)S(1)}, u32[]{:S(2)}, u32[]{:S(2)}) collective-permute-start(bf16[128,1024]{1,0:T(8,128)(2,1)S(1)} %fusion.26), channel_id=1, source_target_pairs={{0,1},{1,0},{2,3},{3,2},{4,5},{5,4},{6,7},{7,6},{8,9},{9,8},{10,11... | collective-permute-start | bytes 786440 | tf_op jit(solution)/shard_map/ppermute | solution.py:53
  59.5 13.0 %collective-permute-start.4 = (bf16[1024,256]{1,0:T(8,128)(2,1)}, bf16[1024,256]{1,0:T(8,128)(2,1)}, u32[]{:S(2)}, u32[]{:S(2)}) collective-permute-start(bf16[1024,256]{1,0:T(8,128)(2,1)} %get-tuple-element.202), channel_id=1, source_target_pairs={{0,4},{4,0},{8,12},{12,8},{1,5},{5,1},{9,13},{13,9},{2,6},{6,2},{1... | collective-permute-start | bytes 1572872 | tf_op jit(solution)/shard_map/ppermute | solution.py:59
  60.0 20.7 %collective-permute-start.5 = (bf16[1024,256]{1,0:T(8,128)(2,1)}, bf16[1024,256]{1,0:T(8,128)(2,1)}, u32[]{:S(2)}, u32[]{:S(2)}) collective-permute-start(bf16[1024,256]{1,0:T(8,128)(2,1)} %get-tuple-element.202), channel_id=1, source_target_pairs={{0,8},{4,12},{8,0},{12,4},{1,9},{5,13},{9,1},{13,5},{2,10},{6,14},... | collective-permute-start | bytes 1572872 | tf_op jit(solution)/shard_map/ppermute | solution.py:59
  68.5 135.1 %all-gather.6.cloned.1.call-start = ((), (), s32[]{:S(2)}) async-start(), calls=%async_computation.5 | async-start | bytes 2621440 | tf_op jit(solution)/shard_map/all_gather | solution.py:139
  68.7 19.2 %collective-permute-start.6 = (bf16[1024,256]{1,0:T(8,128)(2,1)}, bf16[1024,256]{1,0:T(8,128)(2,1)S(1)}, u32[]{:S(2)}, u32[]{:S(2)}) collective-permute-start(bf16[1024,256]{1,0:T(8,128)(2,1)} %get-tuple-element.202), channel_id=1, source_target_pairs={{0,12},{4,8},{8,4},{12,0},{1,13},{5,9},{9,5},{13,1},{2,14},{6,10},... | collective-permute-start | bytes 1572872 | tf_op jit(solution)/shard_map/ppermute | solution.py:59
  69.1 19.6 %collective-permute-start.12 = (bf16[256,1024]{1,0:T(8,128)(2,1)S(1)}, bf16[256,1024]{1,0:T(8,128)(2,1)S(1)}, u32[]{:S(2)}, u32[]{:S(2)}) collective-permute-start(bf16[256,1024]{1,0:T(8,128)(2,1)S(1)} %pad_maximum_fusion.30), channel_id=1, source_target_pairs={{0,16},{16,0},{1,17},{17,1},{2,18},{18,2},{3,19},{19,3},{4,20},{20... | collective-permute-start | bytes 1572872 | tf_op jit(solution)/shard_map/ppermute | solution.py:50
  93.1 9.8 %collective-permute-start.14 = (bf16[3,64,512]{2,1,0:T(8,128)(2,1)S(1)}, bf16[3,64,512]{2,1,0:T(8,128)(2,1)S(1)}, u32[]{:S(2)}, u32[]{:S(2)}) collective-permute-start(bf16[3,64,512]{2,1,0:T(8,128)(2,1)S(1)} %get-tuple-element.166), channel_id=1, source_target_pairs={{0,8},{4,12},{8,0},{12,4},{1,9},{5,13},{9,1},{13,5},{2,10},{6,14},... | collective-permute-start | bytes 589832 | tf_op jit(solution)/shard_map/ppermute | solution.py:59
  139.2 16.0 %collective-permute-start.28 = (bf16[512,256]{1,0:T(8,128)(2,1)S(1)}, bf16[512,256]{1,0:T(8,128)(2,1)S(1)}, u32[]{:S(2)}, u32[]{:S(2)}) collective-permute-start(bf16[512,256]{1,0:T(8,128)(2,1)S(1)} %maximum_select_fusion.3), channel_id=1, source_target_pairs={{0,2},{1,3},{2,0},{3,1},{4,6},{5,7},{6,4},{7,5},{8,10},{9,11},{10,... | collective-permute-start | bytes 786440 | tf_op jit(solution)/shard_map/ppermute | solution.py:56
  143.8 12.6 %collective-permute-start.22 = (bf16[256,1024]{1,0:T(8,128)(2,1)S(1)}, bf16[256,1024]{1,0:T(8,128)(2,1)}, u32[]{:S(2)}, u32[]{:S(2)}) collective-permute-start(bf16[256,1024]{1,0:T(8,128)(2,1)S(1)} %pad_maximum_fusion.31), channel_id=1, source_target_pairs={{0,16},{16,0},{1,17},{17,1},{2,18},{18,2},{3,19},{19,3},{4,20},{20... | collective-permute-start | bytes 1572872 | tf_op jit(solution)/shard_map/ppermute | solution.py:50
  144.5 19.7 %collective-permute-start.41 = (bf16[1056,128]{1,0:T(8,128)(2,1)S(1)}, bf16[1056,128]{1,0:T(8,128)(2,1)}, u32[]{:S(2)}, u32[]{:S(2)}) collective-permute-start(bf16[1056,128]{1,0:T(8,128)(2,1)S(1)} %get-tuple-element.194), channel_id=1, source_target_pairs={{0,16},{16,0},{1,17},{17,1},{2,18},{18,2},{3,19},{19,3},{4,20},{20... | collective-permute-start | bytes 811016 | tf_op jit(solution)/shard_map/ppermute | solution.py:50
  156.1 124.7 %all-gather.8.cloned.1.call-start = ((), (), s32[]{:S(2)}) async-start(), calls=%async_computation.6 | async-start | bytes 5406720 | tf_op jit(solution)/shard_map/all_gather | solution.py:139
  165.5 26.9 %collective-permute-start.42 = (bf16[1056,256]{1,0:T(8,128)(2,1)S(1)}, bf16[1056,256]{1,0:T(8,128)(2,1)S(1)}, u32[]{:S(2)}, u32[]{:S(2)}) collective-permute-start(bf16[1056,256]{1,0:T(8,128)(2,1)S(1)} %maximum_select_fusion.1), channel_id=1, source_target_pairs={{0,2},{1,3},{2,0},{3,1},{4,6},{5,7},{6,4},{7,5},{8,10},{9,11},{10,... | collective-permute-start | bytes 1622024 | tf_op jit(solution)/shard_map/ppermute | solution.py:56
  166.3 26.1 %collective-permute-start.26 = (bf16[128,1024]{1,0:T(8,128)(2,1)S(1)}, bf16[128,1024]{1,0:T(8,128)(2,1)S(1)}, u32[]{:S(2)}, u32[]{:S(2)}) collective-permute-start(bf16[128,1024]{1,0:T(8,128)(2,1)S(1)} %slice.1855), channel_id=1, source_target_pairs={{0,1},{1,0},{2,3},{3,2},{4,5},{5,4},{6,7},{7,6},{8,9},{9,8},{10,11... | collective-permute-start | bytes 786440 | tf_op jit(solution)/shard_map/ppermute | solution.py:53
  203.6 317.1 %reduce-scatter.4.cloned.1.call-start = ((), (), s32[]{:S(2)}) async-start(), calls=%async_computation.7 | async-start | bytes 2621440 | tf_op jit(solution)/shard_map/reduce_scatter | solution.py:165
  209.7 12.0 %collective-permute-start.31 = (bf16[3,64,512]{2,1,0:T(8,128)(2,1)S(1)}, bf16[3,64,512]{2,1,0:T(8,128)(2,1)S(1)}, u32[]{:S(2)}, u32[]{:S(2)}) collective-permute-start(bf16[3,64,512]{2,1,0:T(8,128)(2,1)S(1)} %get-tuple-element.163), channel_id=1, source_target_pairs={{0,4},{4,0},{8,12},{12,8},{1,5},{5,1},{9,13},{13,9},{2,6},{6,2},{1... | collective-permute-start | bytes 589832 | tf_op jit(solution)/shard_map/ppermute | solution.py:59
  210.2 14.1 %collective-permute-start.32 = (bf16[3,64,512]{2,1,0:T(8,128)(2,1)S(1)}, bf16[3,64,512]{2,1,0:T(8,128)(2,1)S(1)}, u32[]{:S(2)}, u32[]{:S(2)}) collective-permute-start(bf16[3,64,512]{2,1,0:T(8,128)(2,1)S(1)} %get-tuple-element.162), channel_id=1, source_target_pairs={{0,8},{4,12},{8,0},{12,4},{1,9},{5,13},{9,1},{13,5},{2,10},{6,14},... | collective-permute-start | bytes 589832 | tf_op jit(solution)/shard_map/ppermute | solution.py:59
  210.2 18.3 %collective-permute-start.33 = (bf16[3,64,512]{2,1,0:T(8,128)(2,1)S(1)}, bf16[3,64,512]{2,1,0:T(8,128)(2,1)S(1)}, u32[]{:S(2)}, u32[]{:S(2)}) collective-permute-start(bf16[3,64,512]{2,1,0:T(8,128)(2,1)S(1)} %get-tuple-element.161), channel_id=1, source_target_pairs={{0,12},{4,8},{8,4},{12,0},{1,13},{5,9},{9,5},{13,1},{2,14},{6,10},... | collective-permute-start | bytes 589832 | tf_op jit(solution)/shard_map/ppermute | solution.py:59
  214.1 25.1 %collective-permute-start.48 = (bf16[128,1024]{1,0:T(8,128)(2,1)S(1)}, bf16[128,1024]{1,0:T(8,128)(2,1)S(1)}, u32[]{:S(2)}, u32[]{:S(2)}) collective-permute-start(bf16[128,1024]{1,0:T(8,128)(2,1)S(1)} %constant_dynamic-slice_fusion.5), channel_id=1, source_target_pairs={{0,16},{16,0},{1,17},{17,1},{2,18},{18,2},{3,19},{19,3},{4,20},{20... | collective-permute-start | bytes 786440 | tf_op jit(solution)/shard_map/ppermute | solution.py:50
  270.5 10.4 %collective-permute-start.40 = (bf16[256,1024]{1,0:T(8,128)(2,1)}, bf16[256,1024]{1,0:T(8,128)(2,1)}, u32[]{:S(2)}, u32[]{:S(2)}) collective-permute-start(bf16[256,1024]{1,0:T(8,128)(2,1)} %pad_maximum_fusion.34), channel_id=1, source_target_pairs={{0,16},{16,0},{1,17},{17,1},{2,18},{18,2},{3,19},{19,3},{4,20},{20... | collective-permute-start | bytes 1572872 | tf_op jit(solution)/shard_map/ppermute | solution.py:50
  293.1 12.7 %collective-permute-start.44 = (bf16[128,1024]{1,0:T(8,128)(2,1)S(1)}, bf16[128,1024]{1,0:T(8,128)(2,1)S(1)}, u32[]{:S(2)}, u32[]{:S(2)}) collective-permute-start(bf16[128,1024]{1,0:T(8,128)(2,1)S(1)} %slice.1853), channel_id=1, source_target_pairs={{0,1},{1,0},{2,3},{3,2},{4,5},{5,4},{6,7},{7,6},{8,9},{9,8},{10,11... | collective-permute-start | bytes 786440 | tf_op jit(solution)/shard_map/ppermute | solution.py:53
  340.2 10.7 %collective-permute-start.60 = (bf16[3,64,512]{2,1,0:T(8,128)(2,1)S(1)}, bf16[3,64,512]{2,1,0:T(8,128)(2,1)S(1)}, u32[]{:S(2)}, u32[]{:S(2)}) collective-permute-start(bf16[3,64,512]{2,1,0:T(8,128)(2,1)S(1)} %pad_maximum_fusion.67), channel_id=1, source_target_pairs={{0,12},{4,8},{8,4},{12,0},{1,13},{5,9},{9,5},{13,1},{2,14},{6,10},... | collective-permute-start | bytes 589832 | tf_op jit(solution)/shard_map/ppermute | solution.py:59
  355.5 218.7 %reduce-scatter.8.cloned.1.call-start = ((), (), s32[]{:S(2)}) async-start(), calls=%async_computation.9 | async-start | bytes 5406720 | tf_op jit(solution)/shard_map/reduce_scatter | solution.py:165
  367.5 237.3 %reduce-scatter.6.cloned.1.call-start = ((), (), s32[]{:S(2)}) async-start(), calls=%async_computation.8 | async-start | bytes 5406720 | tf_op jit(solution)/shard_map/reduce_scatter | solution.py:165
  394.4 11.8 %collective-permute-start.66 = (bf16[128,1024]{1,0:T(8,128)(2,1)}, bf16[128,1024]{1,0:T(8,128)(2,1)}, u32[]{:S(2)}, u32[]{:S(2)}) collective-permute-start(bf16[128,1024]{1,0:T(8,128)(2,1)} %slice.1850), channel_id=1, source_target_pairs={{0,1},{1,0},{2,3},{3,2},{4,5},{5,4},{6,7},{7,6},{8,9},{9,8},{10,11... | collective-permute-start | bytes 786440 | tf_op jit(solution)/shard_map/ppermute | solution.py:53
  402.0 9.5 %collective-permute-start.46 = (bf16[256,1024]{1,0:T(8,128)(2,1)}, bf16[256,1024]{1,0:T(8,128)(2,1)S(1)}, u32[]{:S(2)}, u32[]{:S(2)}) collective-permute-start(bf16[256,1024]{1,0:T(8,128)(2,1)} %pad_maximum_fusion.35), channel_id=1, source_target_pairs={{0,16},{16,0},{1,17},{17,1},{2,18},{18,2},{3,19},{19,3},{4,20},{20... | collective-permute-start | bytes 1572872 | tf_op jit(solution)/shard_map/ppermute | solution.py:50
  412.6 144.1 %collective-permute-start.47 = (bf16[512,1024]{1,0:T(8,128)(2,1)}, bf16[512,1024]{1,0:T(8,128)(2,1)}, u32[]{:S(2)}, u32[]{:S(2)}) collective-permute-start(bf16[512,1024]{1,0:T(8,128)(2,1)} %pad_maximum_fusion.9), channel_id=1, source_target_pairs={{0,2},{1,3},{18,16},{19,17},{4,6},{5,7},{22,20},{23,21},{8,10},{9,... | collective-permute-start | bytes 3145736 | tf_op jit(solution)/shard_map/ppermute | solution.py:509
  454.1 11.4 %collective-permute-start.74 = (bf16[3,64,512]{2,1,0:T(8,128)(2,1)S(1)}, bf16[3,64,512]{2,1,0:T(8,128)(2,1)S(1)}, u32[]{:S(2)}, u32[]{:S(2)}) collective-permute-start(bf16[3,64,512]{2,1,0:T(8,128)(2,1)S(1)} %pad_maximum_fusion.70), channel_id=1, source_target_pairs={{0,12},{4,8},{8,4},{12,0},{1,13},{5,9},{9,5},{13,1},{2,14},{6,10},... | collective-permute-start | bytes 589832 | tf_op jit(solution)/shard_map/ppermute | solution.py:59
  455.1 9.5 %collective-permute-start.72 = (bf16[3,64,512]{2,1,0:T(8,128)(2,1)S(1)}, bf16[3,64,512]{2,1,0:T(8,128)(2,1)S(1)}, u32[]{:S(2)}, u32[]{:S(2)}) collective-permute-start(bf16[3,64,512]{2,1,0:T(8,128)(2,1)S(1)} %pad_maximum_fusion.68), channel_id=1, source_target_pairs={{0,4},{4,0},{8,12},{12,8},{1,5},{5,1},{9,13},{13,9},{2,6},{6,2},{1... | collective-permute-start | bytes 589832 | tf_op jit(solution)/shard_map/ppermute | solution.py:59
  467.8 15.1 %collective-permute-start.86 = (bf16[1024,256]{1,0:T(8,128)(2,1)}, bf16[1024,256]{1,0:T(8,128)(2,1)}, u32[]{:S(2)}, u32[]{:S(2)}) collective-permute-start(bf16[1024,256]{1,0:T(8,128)(2,1)} %get-tuple-element.97), channel_id=1, source_target_pairs={{0,4},{4,0},{8,12},{12,8},{1,5},{5,1},{9,13},{13,9},{2,6},{6,2},{1... | collective-permute-start | bytes 1572872 | tf_op jit(solution)/shard_map/ppermute | solution.py:59
  468.0 18.5 %collective-permute-start.87 = (bf16[1024,256]{1,0:T(8,128)(2,1)}, bf16[1024,256]{1,0:T(8,128)(2,1)}, u32[]{:S(2)}, u32[]{:S(2)}) collective-permute-start(bf16[1024,256]{1,0:T(8,128)(2,1)} %get-tuple-element.98), channel_id=1, source_target_pairs={{0,8},{4,12},{8,0},{12,4},{1,9},{5,13},{9,1},{13,5},{2,10},{6,14},... | collective-permute-start | bytes 1572872 | tf_op jit(solution)/shard_map/ppermute | solution.py:59
  469.4 32.3 %collective-permute-start.88 = (bf16[1024,256]{1,0:T(8,128)(2,1)S(1)}, bf16[1024,256]{1,0:T(8,128)(2,1)}, u32[]{:S(2)}, u32[]{:S(2)}) collective-permute-start(bf16[1024,256]{1,0:T(8,128)(2,1)S(1)} %get-tuple-element.99), channel_id=1, source_target_pairs={{0,12},{4,8},{8,4},{12,0},{1,13},{5,9},{9,5},{13,1},{2,14},{6,10},... | collective-permute-start | bytes 1572872 | tf_op jit(solution)/shard_map/ppermute | solution.py:59
  475.9 27.8 %collective-permute-start.75 = (bf16[256,1024]{1,0:T(8,128)(2,1)}, bf16[256,1024]{1,0:T(8,128)(2,1)}, u32[]{:S(2)}, u32[]{:S(2)}) collective-permute-start(bf16[256,1024]{1,0:T(8,128)(2,1)} %slice.1841), channel_id=1, source_target_pairs={{0,16},{16,0},{1,17},{17,1},{2,18},{18,2},{3,19},{19,3},{4,20},{20... | collective-permute-start | bytes 1572872 | tf_op jit(solution)/shard_map/ppermute | solution.py:50
  506.3 9.3 %collective-permute-start.76 = (bf16[128,1024]{1,0:T(8,128)(2,1)S(1)}, bf16[128,1024]{1,0:T(8,128)(2,1)S(1)}, u32[]{:S(2)}, u32[]{:S(2)}) collective-permute-start(bf16[128,1024]{1,0:T(8,128)(2,1)S(1)} %slice.1849), channel_id=1, source_target_pairs={{0,1},{1,0},{2,3},{3,2},{4,5},{5,4},{6,7},{7,6},{8,9},{9,8},{10,11... | collective-permute-start | bytes 786440 | tf_op jit(solution)/shard_map/ppermute | solution.py:53
  511.4 29.1 %collective-permute-start.90 = (bf16[512,128]{1,0:T(8,128)(2,1)S(1)}, bf16[512,128]{1,0:T(8,128)(2,1)S(1)}, u32[]{:S(2)}, u32[]{:S(2)}) collective-permute-start(bf16[512,128]{1,0:T(8,128)(2,1)S(1)} %select_convert_fusion.3), channel_id=1, source_target_pairs={{0,16},{16,0},{1,17},{17,1},{2,18},{18,2},{3,19},{19,3},{4,20},{20... | collective-permute-start | bytes 393224 | tf_op jit(solution)/shard_map/ppermute | solution.py:50
  521.6 26.1 %collective-permute-start.91 = (bf16[512,256]{1,0:T(8,128)(2,1)S(1)}, bf16[512,256]{1,0:T(8,128)(2,1)S(1)}, u32[]{:S(2)}, u32[]{:S(2)}) collective-permute-start(bf16[512,256]{1,0:T(8,128)(2,1)S(1)} %pad_maximum_fusion.60), channel_id=1, source_target_pairs={{0,2},{1,3},{2,0},{3,1},{4,6},{5,7},{6,4},{7,5},{8,10},{9,11},{10,... | collective-permute-start | bytes 786440 | tf_op jit(solution)/shard_map/ppermute | solution.py:56
  524.7 10.5 %collective-permute-start.83 = (f32[8,256]{1,0:T(8,128)S(1)}, f32[8,256]{1,0:T(8,128)S(1)}, u32[]{:S(2)}, u32[]{:S(2)}) collective-permute-start(f32[8,256]{1,0:T(8,128)S(1)} %fusion.58), channel_id=1, source_target_pairs={{0,2},{1,3},{2,0},{3,1},{4,6},{5,7},{6,4},{7,5},{8,10},{9,11},{10,... | collective-permute-start | bytes 24584 | tf_op jit(solution)/shard_map/ppermute | solution.py:56
  550.7 13.8 %collective-permute-start.79 = (bf16[512,1024]{1,0:T(8,128)(2,1)S(1)}, bf16[512,1024]{1,0:T(8,128)(2,1)}, u32[]{:S(2)}, u32[]{:S(2)}) collective-permute-start(bf16[512,1024]{1,0:T(8,128)(2,1)S(1)} %pad_maximum_fusion.15), channel_id=1, source_target_pairs={{0,2},{1,3},{18,16},{19,17},{4,6},{5,7},{22,20},{23,21},{8,10},{9,... | collective-permute-start | bytes 3145736 | tf_op jit(solution)/shard_map/ppermute | solution.py:509
  569.5 12.9 %all-to-all-start = ((bf16[4,128,1024]{2,1,0:T(8,128)(2,1)}), bf16[4,128,1024]{2,1,0:T(8,128)(2,1)S(1)}, u32[]{:S(2)}, u32[]{:S(2)}) async-start(bf16[4,128,1024]{2,1,0:T(8,128)(2,1)} %bitcast.126), calls=%async_computation | async-start | bytes 2097152 | tf_op jit(solution)/shard_map/all_to_all | solution.py:620
  575.5 17.4 %collective-permute-start.95 = (bf16[1056,256]{1,0:T(8,128)(2,1)S(1)}, bf16[1056,256]{1,0:T(8,128)(2,1)S(1)}, u32[]{:S(2)}, u32[]{:S(2)}) collective-permute-start(bf16[1056,256]{1,0:T(8,128)(2,1)S(1)} %pad_maximum_fusion.28), channel_id=1, source_target_pairs={{0,2},{1,3},{2,0},{3,1},{4,6},{5,7},{6,4},{7,5},{8,10},{9,11},{10,... | collective-permute-start | bytes 1622024 | tf_op jit(solution)/shard_map/ppermute | solution.py:56
  593.0 13.0 %collective-permute-start.96 = (bf16[1056,128]{1,0:T(8,128)(2,1)S(1)}, bf16[1056,128]{1,0:T(8,128)(2,1)S(1)}, u32[]{:S(2)}, u32[]{:S(2)}) collective-permute-start(bf16[1056,128]{1,0:T(8,128)(2,1)S(1)} %select_convert_fusion), channel_id=1, source_target_pairs={{0,16},{16,0},{1,17},{17,1},{2,18},{18,2},{3,19},{19,3},{4,20},{20... | collective-permute-start | bytes 811016 | tf_op jit(solution)/shard_map/ppermute | solution.py:50
  605.9 26.5 %collective-permute-start.93 = (bf16[1056,256]{1,0:T(8,128)(2,1)S(1)}, bf16[1056,256]{1,0:T(8,128)(2,1)S(1)}, u32[]{:S(2)}, u32[]{:S(2)}) collective-permute-start(bf16[1056,256]{1,0:T(8,128)(2,1)S(1)} %pad_maximum_fusion.27), channel_id=1, source_target_pairs={{0,2},{1,3},{2,0},{3,1},{4,6},{5,7},{6,4},{7,5},{8,10},{9,11},{10,... | collective-permute-start | bytes 1622024 | tf_op jit(solution)/shard_map/ppermute | solution.py:56
  (159 other events, 1069.3 us)
Sparse Core Ops, SparseCore 0:
  68.6 61.1 all-gather.3
  156.2 33.2 all-gather.5
  203.7 60.8 all-gather.7
  355.6 32.4 reduce-scatter.3
  391.0 56.4 reduce-scatter.7
  478.5 57.2 reduce-scatter.5

commit v3 on v2

--- a/solution.py
+++ b/solution.py
@@ -165,29 +165,30 @@
     return lax.psum_scatter(grad, "ctx", scatter_dimension=1, tiled=True).astype(F32)
 
 
-def gather_weights(plan, groups, direct):
-    own = own_columns(plan, jnp.concatenate(groups, axis=1))
-    far = plan.far(own)
+def tie(value, *others):
+    return lax.optimization_barrier((value, *others))[0]
+
+
+def with_far(own, far, counts):
     parts = []
     start = 0
-    for group in groups:
-        rows = group.shape[1]
+    for rows in counts:
         parts += [own[start : start + rows], far[start : start + rows]]
         start += rows
-    return all_columns(plan, jnp.concatenate(parts, axis=0), direct)
-
-
-def scatter_grads(plan, grads, direct):
-    total = columns_sum(plan, jnp.concatenate(grads, axis=0), direct)
+    return jnp.concatenate(parts, axis=0)
+
+
+def far_halves(total, counts):
     mine, far = [], []
     start = 0
-    for grad in grads:
-        rows = grad.shape[0] // 2
+    for rows in counts:
         mine.append(total[start : start + rows])
         far.append(total[start + rows : start + 2 * rows])
         start += 2 * rows
-    got = plan.far(jnp.concatenate(far, axis=0).astype(BF)).astype(F32)
-    own = jnp.concatenate(mine, axis=0) + got
+    return jnp.concatenate(mine, axis=0), jnp.concatenate(far, axis=0).astype(BF)
+
+
+def core_halves(plan, own, counts):
     width = own.shape[1]
     left, right = own[:, : width // 2], own[:, width // 2 :]
     kept = jnp.where(plan.c == 0, left, right)
@@ -196,8 +197,7 @@
     high = jnp.where(plan.c == 0, got, kept)
     out = []
     start = 0
-    for grad in grads:
-        rows = grad.shape[0] // 2
+    for rows in counts:
         out.append((low[start : start + rows], high[start : start + rows]))
         start += rows
     return out
@@ -398,20 +398,41 @@
 
     gains = jnp.concatenate([attn_gain, mlp_gain], axis=0)
     gains = jnp.concatenate([gains, jnp.zeros((12, gains.shape[1]), BF)], axis=0)
-    full = []
-    for level in range(LAYERS):
-        qkv = jnp.concatenate(
-            [split_hidden(w[level].T) for w in (w_query, w_key, w_value)], axis=1
-        )
-        w_attn = gather_weights(plan, [qkv, split_hidden(w_out[level])], level == 0)
-        w_mlp = gather_weights(
-            plan,
-            [split_hidden(w) for w in (w_gate[level].T, w_up[level].T, w_down[level])],
-            False,
-        )
-        cut = 2 * qkv.shape[1]
-        gated = 2 * w_gate.shape[2]
-        full.append((w_attn[:cut], w_attn[cut:], w_mlp[:gated], w_mlp[gated:]))
+    qkv_rows = 3 * w_query.shape[2] // 2
+    out_rows = w_out.shape[1] // 2
+    mlp_rows = w_down.shape[1] // 2
+    counts = [qkv_rows, out_rows] + [mlp_rows] * 3
+
+    def own_weights(level):
+        qkv = [split_hidden(w[level].T) for w in (w_query, w_key, w_value)]
+        return [
+            jnp.concatenate(qkv, axis=1),
+            split_hidden(w_out[level]),
+            split_hidden(w_gate[level].T),
+            split_hidden(w_up[level].T),
+            split_hidden(w_down[level]),
+        ]
+
+    groups = own_weights(0)
+    own = own_columns(plan, groups[0])
+    far_first = plan.far(own)
+    w_qkv = all_columns(plan, with_far(own, far_first, counts[:1]), True)
+    own = tie(own_columns(plan, jnp.concatenate(groups[1:], axis=1)), far_first)
+    far_rest = plan.far(own)
+    rest = with_far(own, far_rest, counts[1:])
+    w_o = all_columns(plan, tie(rest[: 2 * out_rows], w_qkv), True)
+    w_mlp = all_columns(plan, tie(rest[2 * out_rows :], w_qkv), False)
+    full = [(w_qkv, w_o, w_mlp)]
+    far_later = []
+    for level in range(1, LAYERS):
+        own = own_columns(plan, jnp.concatenate(own_weights(level), axis=1))
+        far_rest = plan.far(tie(own, far_rest))
+        far_later.append(far_rest)
+        rest = with_far(own, far_rest, counts)
+        cut = 2 * (qkv_rows + out_rows)
+        w_attn = all_columns(plan, rest[:cut], False)
+        w_mlp = all_columns(plan, rest[cut:], False)
+        full.append((w_attn[: 2 * qkv_rows], w_attn[2 * qkv_rows :], w_mlp))
     got = plan.core(gains)
     gain_pair = jnp.where(
         plan.c == 0,
@@ -455,8 +476,9 @@
     kept = []
     first_values = None
     for level in range(LAYERS):
-        w_qkv, w_o, w_gu, w_d = full[level]
-        width = w_d.shape[0]
+        w_qkv, w_o, w_mlp = full[level]
+        width = 2 * mlp_rows
+        w_gu, w_d = w_mlp[: 2 * width], w_mlp[2 * width :]
         scale_attn = norm_scale(stream)
         normed = (stream * scale_attn * gain_full[level : level + 1]).astype(BF)
         normed_all = gather_rows(plan, normed)
@@ -473,7 +495,10 @@
         out, out_low, log_total = attend(where_all, first_query, heads)
         attended = from_heads(plan, [out_low[k] for k in range(4)])
         attended = attended.reshape(4 * HEAD, tok_rows)
-        middle = stream + sum_rows(plan, dot(attended, w_o, 0, 0))
+        branch = sum_rows(plan, dot(attended, w_o, 0, 0))
+        if level < len(far_later):
+            branch = tie(branch, far_later[level])
+        middle = stream + branch
         scale_mlp = norm_scale(middle)
         normed_mlp = (middle * scale_mlp * gain_full[2 + level : 3 + level]).astype(BF)
         normed_mlp_all = gather_rows(plan, normed_mlp)
@@ -500,20 +525,19 @@
         stream = result
 
     def to_pack(rows):
-        block = gather_rows(plan, rows)
-        pairs = []
-        for f in range(plan.fsdp):
-            for z in range(plan.tp):
-                if f % 2 == z // 2:
-                    pairs.append((f * plan.tp + z, f * plan.tp + (z ^ 2)))
-        got = lax.ppermute(block, ("fsdp", "tp"), pairs)
-        return jnp.where(plan.c == plan.zp, block, got)
-
-    outputs = natural_rows(plan, to_pack(from_block_order(plan, stream.astype(BF))))
+        other = plan.far(rows)
+        mine = jnp.where(plan.c == plan.zp, rows, other)
+        got = plan.core(jnp.where(plan.c == plan.zp, other, rows))
+        count = rows.shape[0]
+        near = plan.near(jnp.concatenate([mine, got], axis=0))
+        return jnp.concatenate([mine, near[:count], got, near[count:]], axis=0)
+
+    last = from_block_order(plan, stream.astype(BF))
 
     grads = [None] * LAYERS
     gain_rows = [None] * (2 * LAYERS)
     carried = None
+    later_sums = []
     for level in reversed(range(LAYERS)):
         (
             stream,
@@ -529,8 +553,9 @@
             gate_up,
             hidden,
         ) = kept[level]
-        w_qkv, w_o, w_gu, w_d = full[level]
-        width = w_d.shape[0]
+        w_qkv, w_o, w_mlp = full[level]
+        width = 2 * mlp_rows
+        w_gu, w_d = w_mlp[: 2 * width], w_mlp[2 * width :]
         branch = gather_rows(plan, grad_stream.astype(BF))
         grad_hidden = dot(branch, w_d, 1, 1)
         gate, upward = gate_up[:, :width], gate_up[:, width:]
@@ -539,18 +564,31 @@
         grad_up = (grad_hidden * gate * sigma).astype(BF)
         grad_gu = jnp.concatenate([grad_gate, grad_up], axis=1)
         grad_normed = sum_rows(plan, dot(grad_gu, w_gu, 1, 0))
+        grad_wd = dot(hidden, branch, 0, 0).astype(BF)
         grad_wgu = dot(grad_gu, normed_mlp_all, 0, 0).astype(BF)
-        grad_wd = dot(hidden, branch, 0, 0).astype(BF)
-        grad_wg, grad_wu, grad_wd = scatter_grads(
-            plan, [grad_wgu[:width], grad_wgu[width:], grad_wd], False
-        )
+        if level > 0:
+            grad_mlp = jnp.concatenate([grad_wgu, grad_wd], axis=0)
+            grad_normed = tie(grad_normed, grad_mlp)
+            sum_mlp = columns_sum(plan, grad_mlp, False)
+        else:
+            sum_wd = columns_sum(plan, grad_wd, False)
         gain_rows[2 + level], through = norm_back(
             middle, scale_mlp, gain_full[2 + level : 3 + level], grad_normed
         )
         grad_middle = grad_stream + through
         branch = gather_rows(plan, grad_middle.astype(BF))
+        if level == 0:
+            branch, *sums = lax.optimization_barrier((branch, *later_sums))
+            mine, far = far_halves(jnp.concatenate(sums, axis=0), counts * (LAYERS - 1))
+            far_sums = plan.far(far)
         grad_wo = dot(attended, branch, 1, 0).astype(BF)
         grad_attended = dot(w_o, branch, 1, 1).astype(BF)
+        if level == 0:
+            grad_out = jnp.concatenate([grad_wgu, grad_wo], axis=0)
+            grad_attended = tie(grad_attended, grad_out, outputs)
+            sum_gu = columns_sum(plan, grad_out, False)
+        elif level == LAYERS - 1:
+            outputs = natural_rows(plan, to_pack(tie(last, grad_attended)))
         grad_attended = to_heads(plan, grad_attended.reshape(4, HEAD, tok_rows))
         grad_q, grad_k, grad_v = attend_back(
             where_all, first_query, heads, grad_attended, out, log_total
@@ -577,20 +615,29 @@
         ]
         grad_qkv = from_heads(plan, grad_heads).reshape(2, 2, 3, HEAD, tok_rows)
         grad_qkv = jnp.swapaxes(grad_qkv, 1, 2).reshape(-1, tok_rows)
+        if level == 0:
+            grad_qkv, far_sums = lax.optimization_barrier((grad_qkv, far_sums))
+            later = core_halves(plan, mine + far_sums.astype(F32), counts * (LAYERS - 1))
         grad_wqkv = dot(grad_qkv, normed_all, 1, 0).astype(BF)
-        grad_wqkv, grad_wo = scatter_grads(plan, [grad_wqkv, grad_wo], level == 0)
+        if level > 0:
+            sum_attn = columns_sum(plan, jnp.concatenate([grad_wqkv, grad_wo], axis=0), False)
+            later_sums += [sum_attn, sum_mlp]
+        else:
+            sum_qkv = columns_sum(plan, grad_wqkv, True)
         grad_normed = sum_rows(plan, dot(grad_qkv, w_qkv, 0, 0))
         gain_rows[level], through = norm_back(
             stream, scale_attn, gain_full[level : level + 1], grad_normed
         )
         grad_stream = grad_middle + through
-        third = grad_wqkv[0].shape[0] // 3
+
+    def weight_grads(grad_qkv, grad_wo, grad_wg, grad_wu, grad_wd):
+        third = qkv_rows // 3
 
         def member(i):
-            rows = [half[i * third : (i + 1) * third] for half in grad_wqkv]
+            rows = [half[i * third : (i + 1) * third] for half in grad_qkv]
             return jnp.concatenate(rows, axis=0).T
 
-        grads[level] = (
+        return (
             member(0),
             member(1),
             member(2),
@@ -600,15 +647,8 @@
             jnp.concatenate(grad_wd, axis=0),
         )
 
-    gain_sum = jnp.concatenate(gain_rows + [jnp.zeros((4, model), F32)], axis=0)
-    total = columns_sum(plan, gain_sum, True)
-    width = total.shape[1]
-    total = total + plan.far(total)
-    total = total + plan.near(total)
-    left, right = total[:, : width // 2], total[:, width // 2 :]
-    mine = jnp.where(plan.c == 0, left, right)
-    theirs = jnp.where(plan.c == 0, right, left)
-    total = mine + plan.core(theirs)
+    for i, level in enumerate(reversed(range(1, LAYERS))):
+        grads[level] = weight_grads(*later[5 * i : 5 * i + 5])
 
     grad_block = to_pack(from_block_order(plan, grad_stream.astype(BF)))
     group_rows = tok_rows // plan.ctx
@@ -620,6 +660,23 @@
     grad_tokens = lax.all_to_all(
         grad_block[local_rows], "ctx", split_axis=0, concat_axis=0, tiled=True
     ).astype(F32)
+
+    mlp_counts = [mlp_rows, mlp_rows, out_rows, mlp_rows]
+    mine, far = far_halves(jnp.concatenate([sum_gu, sum_wd], axis=0), mlp_counts)
+    rest = core_halves(plan, mine + plan.far(far).astype(F32), mlp_counts)
+    mine, far = far_halves(sum_qkv, [qkv_rows])
+    first = core_halves(plan, mine + plan.far(far).astype(F32), [qkv_rows])
+    grads[0] = weight_grads(first[0], rest[2], rest[0], rest[1], rest[3])
+
+    gain_sum = jnp.concatenate(gain_rows + [jnp.zeros((4, model), F32)], axis=0)
+    total = columns_sum(plan, tie(gain_sum, grad_block), True)
+    width = total.shape[1]
+    total = total + plan.far(total)
+    total = total + plan.near(total)
+    left, right = total[:, : width // 2], total[:, width // 2 :]
+    mine = jnp.where(plan.c == 0, left, right)
+    theirs = jnp.where(plan.c == 0, right, left)
+    total = mine + plan.core(theirs)
 
     stacked = [jnp.stack([grads[level][i] for level in range(LAYERS)]) for i in range(7)]
     return (

time: 652 us -> 687 us (1.054)
  waiting for transfers between devices: 333 us -> 371 us
  starting transfers between devices: 94.3 us -> 87.1 us
    ppermute x19, waiting for transfers between devices: 98.2 us -> 139 us  [near(): return lax.ppermute(value, 'tp', [(i, i ^ 1) for i in range(self.tp)])]
    reduce_scatter x3 -> x4, waiting for transfers between devices: 0.01 us -> 31.8 us  [columns_sum(): lax.psum_scatter(grad, 'ctx', scatter_dimension=1, tiled=True).astype(F32)]
    ppermute x9, waiting for transfers between devices: 109 us -> 87.5 us  [far(): return lax.ppermute(value, 'tp', [(i, i ^ 2) for i in range(self.tp)])]
    ppermute x31 -> x29, starting transfers between devices: 16.1 us -> 3.98 us  [core(): return lax.ppermute(value, 'fsdp', [(i, i ^ 1) for i in range(self.fsdp)])]
    unnamed x243 -> x233, local copies, waits for them, and re-layouts: 15.5 us -> 25.8 us
    ppermute x2 -> x0, waiting for transfers between devices: 7.93 us -> none  [to_pack(): got = lax.ppermute(block, ('fsdp', 'tp'), pairs)]
    ppermute x36 -> x39, starting transfers between devices: 44.3 us -> 48.7 us  [side(): return lax.ppermute(value, 'ctx', [(i, i ^ k) for i in range(self.ctx)])]
    ppermute x36 -> x39, waiting for transfers between devices: 97.6 us -> 93.6 us  [side(): return lax.ppermute(value, 'ctx', [(i, i ^ k) for i in range(self.ctx)])]
  transfers between devices with their start and end apart: 104 -> 104, of which waited for: 67 -> 64; matrix products, arithmetic and copies ran while one was open for 20% -> 18% of each run, Pallas kernels for 4% -> 4%
where the time goes in v3:
time: 687 us; the launch traced here: 676 us
  waiting for transfers between devices  371 us (54%)
  starting transfers between devices  87.1 us (13%)
  other arithmetic  56.6 us (8%)
  matrix products  54.2 us (8%)
  local copies, waits for them, and re-layouts  52.7 us (8%)
  Pallas kernels  36.6 us (5%)
  between operations  17.4 us (3%)
    ppermute x19, waiting for transfers between devices, near(): return lax.ppermute(value, 'tp', [(i, i ^ 1) for i in range(self.tp)])  139 us
    ppermute x39, waiting for transfers between devices, side(): return lax.ppermute(value, 'ctx', [(i, i ^ k) for i in range(self.ctx)])  93.6 us
    ppermute x9, waiting for transfers between devices, far(): return lax.ppermute(value, 'tp', [(i, i ^ 2) for i in range(self.tp)])  87.5 us
    dot_general x24, matrix products, dot(): lax.dot_general(left, right, (((left_dim,), (right_dim,)), ((), ())), pre...  54.2 us
    ppermute x39, starting transfers between devices, side(): return lax.ppermute(value, 'ctx', [(i, i ^ k) for i in range(self.ctx)])  48.7 us
    reduce_scatter x4, waiting for transfers between devices, columns_sum(): lax.psum_scatter(grad, 'ctx', scatter_dimension=1, tiled=True).astype(F32)  31.8 us
    unnamed x233, local copies, waits for them, and re-layouts  25.8 us
    pallas_call x2, Pallas kernels, attend_back(): pl.pallas_call(functools.partial(back_kernel, count), out_shape=(jax.Shap...  20.7 us
  transfers between devices with their start and end apart: 104, of which 64 were waited for; matrix products, arithmetic and copies ran while one was open for 18% of the time, Pallas kernels for 4%

profile of v3, /device:TPU:0, one launch (start us, length us, event | category | flops | bytes accessed | tf_op | source)
XLA Modules:
  0.0 675.5 jit_solution(11039052895896856457)
XLA Ops:
  34.7 6.1 collective-permute-done.3
  47.4 5.6 collective-permute-done.4
  53.7 6.8 %collective-permute-done.6 = bf16[768,256]{1,0:T(8,128)(2,1)S(1)} collective-permute-done((bf16[768,256]{1,0:T(8,128)(2,1)S(1)}, bf16[768,256]{1,0:T(8,128)(2,1)S(1)}, u32[]{:S(2)}, u32[]{:S(2)}) %collective-permute-start.6) | collective-permute-done | bytes 393248 | tf_op jit(solution)/shard_map/ppermute | solution.py:59
  60.5 11.6 %collective-permute-done.20 = bf16[1184,256]{1,0:T(8,128)(2,1)S(1)} collective-permute-done((bf16[1184,256]{1,0:T(8,128)(2,1)S(1)}, bf16[1184,256]{1,0:T(8,128)(2,1)S(1)}, u32[]{:S(2)}, u32[]{:S(2)}) %collective-permute-start.20) | collective-permute-done | bytes 606240 | tf_op jit(solution)/shard_map/ppermute | solution.py:56
  90.7 7.1 %collective-permute-done.13.refs_1_ = bf16[3,64,512]{2,1,0:T(8,128)(2,1)S(1)} collective-permute-done((bf16[3,64,512]{2,1,0:T(8,128)(2,1)S(1)}, bf16[3,64,512]{2,1,0:T(8,128)(2,1)S(1)}, u32[]{:S(2)}, u32[]{:S(2)}) %collective-permute-start.13) | collective-permute-done | bytes 196640 | tf_op jit(solution)/shard_map/ppermute | solution.py:59
  97.9 7.8 %collective-permute-done.15.refs_3_ = bf16[3,64,512]{2,1,0:T(8,128)(2,1)S(1)} collective-permute-done((bf16[3,64,512]{2,1,0:T(8,128)(2,1)S(1)}, bf16[3,64,512]{2,1,0:T(8,128)(2,1)S(1)}, u32[]{:S(2)}, u32[]{:S(2)}) %collective-permute-start.15) | collective-permute-done | bytes 196640 | tf_op jit(solution)/shard_map/ppermute | solution.py:59
  106.4 7.8 %attend.2 = (f32[4,64,512]{2,1,0:T(8,128)}, bf16[4,64,512]{2,1,0:T(8,128)(2,1)}, f32[4,1,512]{2,1,0:T(1,128)}) custom-call(s32[6]{0:T(128)} %pad_add_fusion.2.place_ref, s32[4,1,512]{2,1,0:T(1,128)} %broadcast_in_dim.87.first_ref, bf16[3,64,512]{2,1,0:T(8,128)(2,1)} %get-tuple-element.202.refs_0_, bf16[3,64,512]{2,1,0:T(8,128)(2,1)} %copy-done.33, ...), custom_call_target="tpu_custom_call" | custom-call | tf_op jit(solution)/shard_map/attend/pallas_call | solution.py:287
  127.9 22.7 %collective-permute-done.25 = bf16[128,1024]{1,0:T(8,128)(2,1)S(1)} collective-permute-done((bf16[128,1024]{1,0:T(8,128)(2,1)S(1)}, bf16[128,1024]{1,0:T(8,128)(2,1)S(1)}, u32[]{:S(2)}, u32[]{:S(2)}) %collective-permute-start.25) | collective-permute-done | bytes 262176 | tf_op jit(solution)/shard_map/ppermute | solution.py:53
  150.7 12.5 %collective-permute-done.27 = bf16[1568,256]{1,0:T(8,128)(2,1)S(1)} collective-permute-done((bf16[1568,256]{1,0:T(8,128)(2,1)S(1)}, bf16[1568,256]{1,0:T(8,128)(2,1)S(1)}, u32[]{:S(2)}, u32[]{:S(2)}) %collective-permute-start.27) | collective-permute-done | bytes 802848 | tf_op jit(solution)/shard_map/ppermute | solution.py:56
  163.6 8.3 %collective-permute-done.28 = bf16[128,1024]{1,0:T(8,128)(2,1)S(1)} collective-permute-done((bf16[128,1024]{1,0:T(8,128)(2,1)S(1)}, bf16[128,1024]{1,0:T(8,128)(2,1)S(1)}, u32[]{:S(2)}, u32[]{:S(2)}) %collective-permute-start.28) | collective-permute-done | bytes 262176 | tf_op jit(solution)/shard_map/ppermute | solution.py:53
  174.0 3.8 fusion.6
  184.7 8.1 %collective-permute-done.31 = bf16[128,1024]{1,0:T(8,128)(2,1)S(1)} collective-permute-done((bf16[128,1024]{1,0:T(8,128)(2,1)S(1)}, bf16[128,1024]{1,0:T(8,128)(2,1)S(1)}, u32[]{:S(2)}, u32[]{:S(2)}) %collective-permute-start.31) | collective-permute-done | bytes 262176 | tf_op jit(solution)/shard_map/ppermute | solution.py:53
  193.6 7.2 %collective-permute-done.32 = bf16[128,1024]{1,0:T(8,128)(2,1)S(1)} collective-permute-done((bf16[128,1024]{1,0:T(8,128)(2,1)S(1)}, bf16[128,1024]{1,0:T(8,128)(2,1)S(1)}, u32[]{:S(2)}, u32[]{:S(2)}) %collective-permute-start.32) | collective-permute-done | bytes 262176 | tf_op jit(solution)/shard_map/ppermute | solution.py:53
  202.6 5.6 all-gather.6.cloned.1.call-done
  217.8 3.8 collective-permute-done.34.refs_1_
  224.8 4.6 collective-permute-done.36.refs_3_
  230.1 8.2 %attend.3 = (f32[4,64,512]{2,1,0:T(8,128)}, bf16[4,64,512]{2,1,0:T(8,128)(2,1)}, f32[4,1,512]{2,1,0:T(1,128)}) custom-call(s32[6]{0:T(128)} %pad_add_fusion.2.place_ref, s32[4,1,512]{2,1,0:T(1,128)} %broadcast_in_dim.87.first_ref, bf16[3,64,512]{2,1,0:T(8,128)(2,1)} %get-tuple-element.198.refs_0_, bf16[3,64,512]{2,1,0:T(8,128)(2,1)} %copy-done.36, ...), custom_call_target="tpu_custom_call" | custom-call | tf_op jit(solution)/shard_map/attend/pallas_call | solution.py:287
  255.5 7.1 %collective-permute-done.41 = bf16[128,1024]{1,0:T(8,128)(2,1)S(1)} collective-permute-done((bf16[128,1024]{1,0:T(8,128)(2,1)S(1)}, bf16[128,1024]{1,0:T(8,128)(2,1)S(1)}, u32[]{:S(2)}, u32[]{:S(2)}) %collective-permute-start.41) | collective-permute-done | bytes 262176 | tf_op jit(solution)/shard_map/ppermute | solution.py:53
  264.2 6.3 collective-permute-done.42
  272.7 7.5 %collective-permute-done.47 = bf16[128,1024]{1,0:T(8,128)(2,1)S(1)} collective-permute-done((bf16[128,1024]{1,0:T(8,128)(2,1)S(1)}, bf16[128,1024]{1,0:T(8,128)(2,1)S(1)}, u32[]{:S(2)}, u32[]{:S(2)}) %collective-permute-start.47) | collective-permute-done | bytes 262176 | tf_op jit(solution)/shard_map/ppermute | solution.py:53
  281.0 3.9 fusion.2
  305.8 5.8 collective-permute-done.50
  312.4 4.4 collective-permute-done.45
  318.3 6.6 collective-permute-done.51
  335.8 10.3 %attend_back.2 = (f32[4,64,512]{2,1,0:T(8,128)}, f32[4,64,512]{2,1,0:T(8,128)}, f32[4,64,512]{2,1,0:T(8,128)}) custom-call(s32[6]{0:T(128)} %pad_add_fusion.2.place_ref, s32[4,1,512]{2,1,0:T(1,128)} %broadcast_in_dim.87.first_ref, f32[4,64,512]{2,1,0:T(8,128)} %get-tuple-element.46.out_ref, f32[4,1,512]{2,1,0:T(1,128)} %get-tuple-element.47.lse_ref, ...), custom_call_target="tpu_custom_call" | custom-call | tf_op jit(solution)/shard_map/attend_back/pallas_call | solution.py:346
  353.2 4.0 collective-permute-done.59
  357.2 3.5 collective-permute-done.60
  370.5 7.1 %collective-permute-done.63 = bf16[128,1024]{1,0:T(8,128)(2,1)S(1)} collective-permute-done((bf16[128,1024]{1,0:T(8,128)(2,1)S(1)}, bf16[128,1024]{1,0:T(8,128)(2,1)S(1)}, u32[]{:S(2)}, u32[]{:S(2)}) %collective-permute-start.63) | collective-permute-done | bytes 262176 | tf_op jit(solution)/shard_map/ppermute | solution.py:53
  379.9 6.3 collective-permute-done.64
  392.2 3.8 multiply_convert_fusion.1
  396.0 4.3 fusion.4
  402.0 15.1 %collective-permute-done.53 = bf16[128,1024]{1,0:T(8,128)(2,1)S(1)} collective-permute-done((bf16[128,1024]{1,0:T(8,128)(2,1)S(1)}, bf16[128,1024]{1,0:T(8,128)(2,1)S(1)}, u32[]{:S(2)}, u32[]{:S(2)}) %collective-permute-start.53) | collective-permute-done | bytes 262176 | tf_op jit(solution)/shard_map/ppermute | solution.py:56
  422.9 5.7 collective-permute-done.67
  430.4 9.5 %collective-permute-done.55 = bf16[256,1024]{1,0:T(8,128)(2,1)S(1)} collective-permute-done((bf16[256,1024]{1,0:T(8,128)(2,1)S(1)}, bf16[256,1024]{1,0:T(8,128)(2,1)S(1)}, u32[]{:S(2)}, u32[]{:S(2)}) %collective-permute-start.55) | collective-permute-done | bytes 524320 | tf_op jit(solution)/shard_map/ppermute | solution.py:53
  440.0 5.0 collective-permute-done.68
  447.0 4.4 convolution_convert_fusion
  455.5 31.7 %reduce-scatter.7.cloned.1.call-done = bf16[2112,256]{1,0:T(8,128)(2,1)} async-done(((bf16[2112,1024]{1,0:T(8,128)(2,1)}), bf16[2112,256]{1,0:T(8,128)(2,1)}) %reduce-scatter.7.cloned.1.call-update) | async-done | bytes 1081360 | tf_op jit(solution)/shard_map/reduce_scatter | solution.py:165
  509.5 10.5 %attend_back.3 = (f32[4,64,512]{2,1,0:T(8,128)}, f32[4,64,512]{2,1,0:T(8,128)}, f32[4,64,512]{2,1,0:T(8,128)}) custom-call(s32[6]{0:T(128)} %pad_add_fusion.2.place_ref, s32[4,1,512]{2,1,0:T(1,128)} %broadcast_in_dim.87.first_ref, f32[4,64,512]{2,1,0:T(8,128)} %get-tuple-element.51.out_ref, f32[4,1,512]{2,1,0:T(1,128)} %get-tuple-element.52.lse_ref, ...), custom_call_target="tpu_custom_call" | custom-call | tf_op jit(solution)/shard_map/attend_back/pallas_call | solution.py:346
  527.1 5.3 collective-permute-done.73
  532.4 4.0 collective-permute-done.74
  547.4 7.4 %collective-permute-done.90 = bf16[768,256]{1,0:T(8,128)(2,1)S(1)} collective-permute-done((bf16[768,256]{1,0:T(8,128)(2,1)S(1)}, bf16[768,256]{1,0:T(8,128)(2,1)S(1)}, u32[]{:S(2)}, u32[]{:S(2)}) %collective-permute-start.90) | collective-permute-done | bytes 393248 | tf_op jit(solution)/shard_map/ppermute | solution.py:59
  554.8 6.5 collective-permute-done.89
  563.6 4.8 collective-permute-start.78
  568.5 8.6 %collective-permute-done.78 = bf16[128,1024]{1,0:T(8,128)(2,1)S(1)} collective-permute-done((bf16[128,1024]{1,0:T(8,128)(2,1)S(1)}, bf16[128,1024]{1,0:T(8,128)(2,1)S(1)}, u32[]{:S(2)}, u32[]{:S(2)}) %collective-permute-start.78) | collective-permute-done | bytes 262176 | tf_op jit(solution)/shard_map/ppermute | solution.py:53
  579.1 12.6 %collective-permute-done.79 = bf16[128,1024]{1,0:T(8,128)(2,1)S(1)} collective-permute-done((bf16[128,1024]{1,0:T(8,128)(2,1)S(1)}, bf16[128,1024]{1,0:T(8,128)(2,1)S(1)}, u32[]{:S(2)}, u32[]{:S(2)}) %collective-permute-start.79) | collective-permute-done | bytes 262176 | tf_op jit(solution)/shard_map/ppermute | solution.py:56
  594.9 12.5 %collective-permute-done.81 = bf16[256,1024]{1,0:T(8,128)(2,1)S(1)} collective-permute-done((bf16[256,1024]{1,0:T(8,128)(2,1)S(1)}, bf16[256,1024]{1,0:T(8,128)(2,1)S(1)}, u32[]{:S(2)}, u32[]{:S(2)}) %collective-permute-start.81) | collective-permute-done | bytes 524320 | tf_op jit(solution)/shard_map/ppermute | solution.py:53
  624.6 3.6 all-to-all-start
  634.0 26.6 %collective-permute-done.94 = bf16[1184,256]{1,0:T(8,128)(2,1)S(1)} collective-permute-done((bf16[1184,256]{1,0:T(8,128)(2,1)S(1)}, bf16[1184,256]{1,0:T(8,128)(2,1)S(1)}, u32[]{:S(2)}, u32[]{:S(2)}) %collective-permute-start.94) | collective-permute-done | bytes 606240 | tf_op jit(solution)/shard_map/ppermute | solution.py:56
  (703 shorter events, 265.9 us)
Async XLA Ops:
  7.2 166.8 %all-gather.4.cloned.1.call-start = ((), (), s32[]{:S(2)}) async-start(), calls=%async_computation.5 | async-start | bytes 5406720 | tf_op jit(solution)/shard_map/all_gather | solution.py:139
  12.4 113.1 %collective-permute-start.26 = (bf16[1568,128]{1,0:T(8,128)(2,1)}, bf16[1568,128]{1,0:T(8,128)(2,1)}, u32[]{:S(2)}, u32[]{:S(2)}) collective-permute-start(bf16[1568,128]{1,0:T(8,128)(2,1)} %get-tuple-element.194), channel_id=1, source_target_pairs={{0,16},{16,0},{1,17},{17,1},{2,18},{18,2},{3,19},{19,3},{4,20},{20... | collective-permute-start | bytes 1204232 | tf_op jit(solution)/shard_map/ppermute | solution.py:50
  13.7 29.4 %collective-permute-start.19 = (bf16[1184,128]{1,0:T(8,128)(2,1)S(1)}, bf16[1184,128]{1,0:T(8,128)(2,1)}, u32[]{:S(2)}, u32[]{:S(2)}) collective-permute-start(bf16[1184,128]{1,0:T(8,128)(2,1)S(1)} %get-tuple-element.218), channel_id=1, source_target_pairs={{0,16},{16,0},{1,17},{17,1},{2,18},{18,2},{3,19},{19,3},{4,20},{20... | collective-permute-start | bytes 909320 | tf_op jit(solution)/shard_map/ppermute | solution.py:50
  14.1 16.8 %collective-permute-start.2 = (bf16[384,128]{1,0:T(8,128)(2,1)S(1)}, bf16[384,128]{1,0:T(8,128)(2,1)S(1)}, u32[]{:S(2)}, u32[]{:S(2)}) collective-permute-start(bf16[384,128]{1,0:T(8,128)(2,1)S(1)} %get-tuple-element.267), channel_id=1, source_target_pairs={{0,16},{16,0},{1,17},{17,1},{2,18},{18,2},{3,19},{19,3},{4,20},{20... | collective-permute-start | bytes 294920 | tf_op jit(solution)/shard_map/ppermute | solution.py:50
  16.1 17.5 %collective-permute-start = (bf16[128,1024]{1,0:T(8,128)(2,1)S(1)}, bf16[128,1024]{1,0:T(8,128)(2,1)S(1)}, u32[]{:S(2)}, u32[]{:S(2)}) collective-permute-start(bf16[128,1024]{1,0:T(8,128)(2,1)S(1)} %constant_dynamic-slice_fusion.21), channel_id=1, source_target_pairs={{0,16},{16,0},{1,17},{17,1},{2,18},{18,2},{3,19},{19,3},{4,20},{20... | collective-permute-start | bytes 786440 | tf_op jit(solution)/shard_map/ppermute | solution.py:50
  41.0 12.1 %collective-permute-start.4 = (bf16[768,256]{1,0:T(8,128)(2,1)S(1)}, bf16[768,256]{1,0:T(8,128)(2,1)S(1)}, u32[]{:S(2)}, u32[]{:S(2)}) collective-permute-start(bf16[768,256]{1,0:T(8,128)(2,1)S(1)} %get-tuple-element.234), channel_id=1, source_target_pairs={{0,4},{4,0},{8,12},{12,8},{1,5},{5,1},{9,13},{13,9},{2,6},{6,2},{1... | collective-permute-start | bytes 1179656 | tf_op jit(solution)/shard_map/ppermute | solution.py:59
  41.6 12.1 %collective-permute-start.5 = (bf16[768,256]{1,0:T(8,128)(2,1)S(1)}, bf16[768,256]{1,0:T(8,128)(2,1)S(1)}, u32[]{:S(2)}, u32[]{:S(2)}) collective-permute-start(bf16[768,256]{1,0:T(8,128)(2,1)S(1)} %get-tuple-element.234), channel_id=1, source_target_pairs={{0,8},{4,12},{8,0},{12,4},{1,9},{5,13},{9,1},{13,5},{2,10},{6,14},... | collective-permute-start | bytes 1179656 | tf_op jit(solution)/shard_map/ppermute | solution.py:59
  44.4 27.8 %collective-permute-start.20 = (bf16[1184,256]{1,0:T(8,128)(2,1)S(1)}, bf16[1184,256]{1,0:T(8,128)(2,1)S(1)}, u32[]{:S(2)}, u32[]{:S(2)}) collective-permute-start(bf16[1184,256]{1,0:T(8,128)(2,1)S(1)} %maximum_select_fusion.1), channel_id=1, source_target_pairs={{0,2},{1,3},{2,0},{3,1},{4,6},{5,7},{6,4},{7,5},{8,10},{9,11},{10,... | collective-permute-start | bytes 1818632 | tf_op jit(solution)/shard_map/ppermute | solution.py:56
  45.3 15.2 %collective-permute-start.6 = (bf16[768,256]{1,0:T(8,128)(2,1)S(1)}, bf16[768,256]{1,0:T(8,128)(2,1)S(1)}, u32[]{:S(2)}, u32[]{:S(2)}) collective-permute-start(bf16[768,256]{1,0:T(8,128)(2,1)S(1)} %get-tuple-element.234), channel_id=1, source_target_pairs={{0,12},{4,8},{8,4},{12,0},{1,13},{5,9},{9,5},{13,1},{2,14},{6,10},... | collective-permute-start | bytes 1179656 | tf_op jit(solution)/shard_map/ppermute | solution.py:59
  53.1 22.7 %collective-permute-start.11 = (bf16[128,1024]{1,0:T(8,128)(2,1)}, bf16[128,1024]{1,0:T(8,128)(2,1)}, u32[]{:S(2)}, u32[]{:S(2)}) collective-permute-start(bf16[128,1024]{1,0:T(8,128)(2,1)} %fusion.22), channel_id=1, source_target_pairs={{0,1},{1,0},{2,3},{3,2},{4,5},{5,4},{6,7},{7,6},{8,9},{9,8},{10,11... | collective-permute-start | bytes 786440 | tf_op jit(solution)/shard_map/ppermute | solution.py:53
  75.7 132.5 %all-gather.6.cloned.1.call-start = ((), (), s32[]{:S(2)}) async-start(), calls=%async_computation.6 | async-start | bytes 2621440 | tf_op jit(solution)/shard_map/all_gather | solution.py:139
  85.8 12.0 %collective-permute-start.13 = (bf16[3,64,512]{2,1,0:T(8,128)(2,1)S(1)}, bf16[3,64,512]{2,1,0:T(8,128)(2,1)S(1)}, u32[]{:S(2)}, u32[]{:S(2)}) collective-permute-start(bf16[3,64,512]{2,1,0:T(8,128)(2,1)S(1)} %get-tuple-element.201), channel_id=1, source_target_pairs={{0,4},{4,0},{8,12},{12,8},{1,5},{5,1},{9,13},{13,9},{2,6},{6,2},{1... | collective-permute-start | bytes 589832 | tf_op jit(solution)/shard_map/ppermute | solution.py:59
  86.2 11.7 %collective-permute-start.14 = (bf16[3,64,512]{2,1,0:T(8,128)(2,1)S(1)}, bf16[3,64,512]{2,1,0:T(8,128)(2,1)S(1)}, u32[]{:S(2)}, u32[]{:S(2)}) collective-permute-start(bf16[3,64,512]{2,1,0:T(8,128)(2,1)S(1)} %get-tuple-element.200), channel_id=1, source_target_pairs={{0,8},{4,12},{8,0},{12,4},{1,9},{5,13},{9,1},{13,5},{2,10},{6,14},... | collective-permute-start | bytes 589832 | tf_op jit(solution)/shard_map/ppermute | solution.py:59
  87.6 18.1 %collective-permute-start.15 = (bf16[3,64,512]{2,1,0:T(8,128)(2,1)S(1)}, bf16[3,64,512]{2,1,0:T(8,128)(2,1)S(1)}, u32[]{:S(2)}, u32[]{:S(2)}) collective-permute-start(bf16[3,64,512]{2,1,0:T(8,128)(2,1)S(1)} %get-tuple-element.199), channel_id=1, source_target_pairs={{0,12},{4,8},{8,4},{12,0},{1,13},{5,9},{9,5},{13,1},{2,14},{6,10},... | collective-permute-start | bytes 589832 | tf_op jit(solution)/shard_map/ppermute | solution.py:59
  89.3 26.6 %collective-permute-start.23 = (bf16[256,256]{1,0:T(8,128)(2,1)}, bf16[256,256]{1,0:T(8,128)(2,1)S(1)}, u32[]{:S(2)}, u32[]{:S(2)}) collective-permute-start(bf16[256,256]{1,0:T(8,128)(2,1)} %pad_maximum_fusion.64), channel_id=1, source_target_pairs={{0,12},{4,8},{8,4},{12,0},{1,13},{5,9},{9,5},{13,1},{2,14},{6,10},... | collective-permute-start | bytes 393224 | tf_op jit(solution)/shard_map/ppermute | solution.py:59
  126.8 36.4 %collective-permute-start.27 = (bf16[1568,256]{1,0:T(8,128)(2,1)S(1)}, bf16[1568,256]{1,0:T(8,128)(2,1)S(1)}, u32[]{:S(2)}, u32[]{:S(2)}) collective-permute-start(bf16[1568,256]{1,0:T(8,128)(2,1)S(1)} %maximum_select_fusion), channel_id=1, source_target_pairs={{0,2},{1,3},{2,0},{3,1},{4,6},{5,7},{6,4},{7,5},{8,10},{9,11},{10,... | collective-permute-start | bytes 2408456 | tf_op jit(solution)/shard_map/ppermute | solution.py:56
  127.5 23.1 %collective-permute-start.25 = (bf16[128,1024]{1,0:T(8,128)(2,1)S(1)}, bf16[128,1024]{1,0:T(8,128)(2,1)S(1)}, u32[]{:S(2)}, u32[]{:S(2)}) collective-permute-start(bf16[128,1024]{1,0:T(8,128)(2,1)S(1)} %slice.1825), channel_id=1, source_target_pairs={{0,1},{1,0},{2,3},{3,2},{4,5},{5,4},{6,7},{7,6},{8,9},{9,8},{10,11... | collective-permute-start | bytes 786440 | tf_op jit(solution)/shard_map/ppermute | solution.py:53
  172.9 108.1 %all-gather.8.cloned.1.call-start = ((), (), s32[]{:S(2)}) async-start(), calls=%async_computation.7 | async-start | bytes 5406720 | tf_op jit(solution)/shard_map/all_gather | solution.py:139
  202.5 249.0 %reduce-scatter.5.cloned.1.call-start = ((), (), s32[]{:S(2)}) async-start(), calls=%async_computation.8 | async-start | bytes 2621440 | tf_op jit(solution)/shard_map/reduce_scatter | solution.py:165
  215.2 14.2 %collective-permute-start.36 = (bf16[3,64,512]{2,1,0:T(8,128)(2,1)S(1)}, bf16[3,64,512]{2,1,0:T(8,128)(2,1)S(1)}, u32[]{:S(2)}, u32[]{:S(2)}) collective-permute-start(bf16[3,64,512]{2,1,0:T(8,128)(2,1)S(1)} %get-tuple-element.195), channel_id=1, source_target_pairs={{0,12},{4,8},{8,4},{12,0},{1,13},{5,9},{9,5},{13,1},{2,14},{6,10},... | collective-permute-start | bytes 589832 | tf_op jit(solution)/shard_map/ppermute | solution.py:59
  217.7 22.2 %collective-permute-start.46 = (bf16[128,1024]{1,0:T(8,128)(2,1)S(1)}, bf16[128,1024]{1,0:T(8,128)(2,1)S(1)}, u32[]{:S(2)}, u32[]{:S(2)}) collective-permute-start(bf16[128,1024]{1,0:T(8,128)(2,1)S(1)} %constant_dynamic-slice_fusion.12), channel_id=1, source_target_pairs={{0,16},{16,0},{1,17},{17,1},{2,18},{18,2},{3,19},{19,3},{4,20},{20... | collective-permute-start | bytes 786440 | tf_op jit(solution)/shard_map/ppermute | solution.py:50
  290.3 10.4 %collective-permute-start.49 = (bf16[256,1024]{1,0:T(8,128)(2,1)}, bf16[256,1024]{1,0:T(8,128)(2,1)}, u32[]{:S(2)}, u32[]{:S(2)}) collective-permute-start(bf16[256,1024]{1,0:T(8,128)(2,1)} %slice.1813), channel_id=1, source_target_pairs={{0,16},{16,0},{1,17},{17,1},{2,18},{18,2},{3,19},{19,3},{4,20},{20... | collective-permute-start | bytes 1572872 | tf_op jit(solution)/shard_map/ppermute | solution.py:50
  304.9 11.8 %collective-permute-start.45 = (bf16[128,1024]{1,0:T(8,128)(2,1)S(1)}, bf16[128,1024]{1,0:T(8,128)(2,1)S(1)}, u32[]{:S(2)}, u32[]{:S(2)}) collective-permute-start(bf16[128,1024]{1,0:T(8,128)(2,1)S(1)} %slice.1822), channel_id=1, source_target_pairs={{0,1},{1,0},{2,3},{3,2},{4,5},{5,4},{6,7},{7,6},{8,9},{9,8},{10,11... | collective-permute-start | bytes 786440 | tf_op jit(solution)/shard_map/ppermute | solution.py:53
  364.5 89.1 %reduce-scatter.11.cloned.1.call-start = ((), (), s32[]{:S(2)}) async-start(), calls=%async_computation.11 | async-start | bytes 1802240 | tf_op jit(solution)/shard_map/reduce_scatter | solution.py:165
  391.2 96.1 %reduce-scatter.7.cloned.1.call-start = ((), (), s32[]{:S(2)}) async-start(), calls=%async_computation.9 | async-start | bytes 5406720 | tf_op jit(solution)/shard_map/reduce_scatter | solution.py:165
  391.8 236.6 %reduce-scatter.9.cloned.1.call-start = ((), (), s32[]{:S(2)}) async-start(), calls=%async_computation.10 | async-start | bytes 4259840 | tf_op jit(solution)/shard_map/reduce_scatter | solution.py:165
  401.7 16.1 %collective-permute-start.66 = (bf16[256,1024]{1,0:T(8,128)(2,1)S(1)}, bf16[256,1024]{1,0:T(8,128)(2,1)}, u32[]{:S(2)}, u32[]{:S(2)}) collective-permute-start(bf16[256,1024]{1,0:T(8,128)(2,1)S(1)} %slice.1811), channel_id=1, source_target_pairs={{0,16},{16,0},{1,17},{17,1},{2,18},{18,2},{3,19},{19,3},{4,20},{20... | collective-permute-start | bytes 1572872 | tf_op jit(solution)/shard_map/ppermute | solution.py:50
  401.9 15.2 %collective-permute-start.53 = (bf16[128,1024]{1,0:T(8,128)(2,1)S(1)}, bf16[128,1024]{1,0:T(8,128)(2,1)S(1)}, u32[]{:S(2)}, u32[]{:S(2)}) collective-permute-start(bf16[128,1024]{1,0:T(8,128)(2,1)S(1)} %constant_dynamic-update-slice_fusion.15), channel_id=1, source_target_pairs={{0,2},{1,3},{2,0},{3,1},{4,6},{5,7},{6,4},{7,5},{8,10},{9,11},{10,... | collective-permute-start | bytes 786440 | tf_op jit(solution)/shard_map/ppermute | solution.py:56
  420.8 19.0 %collective-permute-start.55 = (bf16[256,1024]{1,0:T(8,128)(2,1)S(1)}, bf16[256,1024]{1,0:T(8,128)(2,1)S(1)}, u32[]{:S(2)}, u32[]{:S(2)}) collective-permute-start(bf16[256,1024]{1,0:T(8,128)(2,1)S(1)} %pad_maximum_fusion.34), channel_id=1, source_target_pairs={{0,1},{1,0},{2,3},{3,2},{4,5},{5,4},{6,7},{7,6},{8,9},{9,8},{10,11... | collective-permute-start | bytes 1572872 | tf_op jit(solution)/shard_map/ppermute | solution.py:53
  430.4 14.6 %collective-permute-start.68 = (bf16[128,1024]{1,0:T(8,128)(2,1)S(1)}, bf16[128,1024]{1,0:T(8,128)(2,1)S(1)}, u32[]{:S(2)}, u32[]{:S(2)}) collective-permute-start(bf16[128,1024]{1,0:T(8,128)(2,1)S(1)} %get-tuple-element.104), channel_id=1, source_target_pairs={{0,1},{1,0},{2,3},{3,2},{4,5},{5,4},{6,7},{7,6},{8,9},{9,8},{10,11... | collective-permute-start | bytes 786440 | tf_op jit(solution)/shard_map/ppermute | solution.py:53
  495.7 13.2 %collective-permute-start.70 = (bf16[64,512]{1,0:T(8,128)(2,1)S(1)}, bf16[64,512]{1,0:T(8,128)(2,1)S(1)}, u32[]{:S(2)}, u32[]{:S(2)}) collective-permute-start(bf16[64,512]{1,0:T(8,128)(2,1)S(1)} %get-tuple-element.246), channel_id=1, source_target_pairs={{0,4},{4,0},{8,12},{12,8},{1,5},{5,1},{9,13},{13,9},{2,6},{6,2},{1... | collective-permute-start | bytes 196616 | tf_op jit(solution)/shard_map/ppermute | solution.py:59
  497.1 11.7 %collective-permute-start.71 = (bf16[64,512]{1,0:T(8,128)(2,1)S(1)}, bf16[64,512]{1,0:T(8,128)(2,1)}, u32[]{:S(2)}, u32[]{:S(2)}) collective-permute-start(bf16[64,512]{1,0:T(8,128)(2,1)S(1)} %get-tuple-element.245), channel_id=1, source_target_pairs={{0,8},{4,12},{8,0},{12,4},{1,9},{5,13},{9,1},{13,5},{2,10},{6,14},... | collective-permute-start | bytes 196616 | tf_op jit(solution)/shard_map/ppermute | solution.py:59
  497.7 11.2 %collective-permute-start.72 = (bf16[64,512]{1,0:T(8,128)(2,1)S(1)}, bf16[64,512]{1,0:T(8,128)(2,1)}, u32[]{:S(2)}, u32[]{:S(2)}) collective-permute-start(bf16[64,512]{1,0:T(8,128)(2,1)S(1)} %get-tuple-element.244), channel_id=1, source_target_pairs={{0,12},{4,8},{8,4},{12,0},{1,13},{5,9},{9,5},{13,1},{2,14},{6,10},... | collective-permute-start | bytes 196616 | tf_op jit(solution)/shard_map/ppermute | solution.py:59
  502.6 36.9 %collective-permute-start.76 = (bf16[1568,256]{1,0:T(8,128)(2,1)}, bf16[1568,256]{1,0:T(8,128)(2,1)S(1)}, u32[]{:S(2)}, u32[]{:S(2)}) collective-permute-start(bf16[1568,256]{1,0:T(8,128)(2,1)} %slice_dynamic-update-slice_fusion.5), channel_id=1, source_target_pairs={{0,2},{1,3},{2,0},{3,1},{4,6},{5,7},{6,4},{7,5},{8,10},{9,11},{10,... | collective-permute-start | bytes 2408456 | tf_op jit(solution)/shard_map/ppermute | solution.py:56
  524.9 11.5 %collective-permute-start.74 = (bf16[3,64,512]{2,1,0:T(8,128)(2,1)S(1)}, bf16[3,64,512]{2,1,0:T(8,128)(2,1)S(1)}, u32[]{:S(2)}, u32[]{:S(2)}) collective-permute-start(bf16[3,64,512]{2,1,0:T(8,128)(2,1)S(1)} %pad_maximum_fusion.62), channel_id=1, source_target_pairs={{0,8},{4,12},{8,0},{12,4},{1,9},{5,13},{9,1},{13,5},{2,10},{6,14},... | collective-permute-start | bytes 589832 | tf_op jit(solution)/shard_map/ppermute | solution.py:59
  525.5 13.9 %collective-permute-start.75 = (bf16[3,64,512]{2,1,0:T(8,128)(2,1)S(1)}, bf16[3,64,512]{2,1,0:T(8,128)(2,1)S(1)}, u32[]{:S(2)}, u32[]{:S(2)}) collective-permute-start(bf16[3,64,512]{2,1,0:T(8,128)(2,1)S(1)} %pad_maximum_fusion.63), channel_id=1, source_target_pairs={{0,12},{4,8},{8,4},{12,0},{1,13},{5,9},{9,5},{13,1},{2,14},{6,10},... | collective-permute-start | bytes 589832 | tf_op jit(solution)/shard_map/ppermute | solution.py:59
  541.8 13.0 %collective-permute-start.90 = (bf16[768,256]{1,0:T(8,128)(2,1)S(1)}, bf16[768,256]{1,0:T(8,128)(2,1)S(1)}, u32[]{:S(2)}, u32[]{:S(2)}) collective-permute-start(bf16[768,256]{1,0:T(8,128)(2,1)S(1)} %get-tuple-element.126), channel_id=1, source_target_pairs={{0,12},{4,8},{8,4},{12,0},{1,13},{5,9},{9,5},{13,1},{2,14},{6,10},... | collective-permute-start | bytes 1179656 | tf_op jit(solution)/shard_map/ppermute | solution.py:59
  544.5 16.8 %collective-permute-start.89 = (bf16[768,256]{1,0:T(8,128)(2,1)S(1)}, bf16[768,256]{1,0:T(8,128)(2,1)S(1)}, u32[]{:S(2)}, u32[]{:S(2)}) collective-permute-start(bf16[768,256]{1,0:T(8,128)(2,1)S(1)} %get-tuple-element.127), channel_id=1, source_target_pairs={{0,8},{4,12},{8,0},{12,4},{1,9},{5,13},{9,1},{13,5},{2,10},{6,14},... | collective-permute-start | bytes 1179656 | tf_op jit(solution)/shard_map/ppermute | solution.py:59
  544.8 16.6 %collective-permute-start.88 = (bf16[768,256]{1,0:T(8,128)(2,1)S(1)}, bf16[768,256]{1,0:T(8,128)(2,1)S(1)}, u32[]{:S(2)}, u32[]{:S(2)}) collective-permute-start(bf16[768,256]{1,0:T(8,128)(2,1)S(1)} %get-tuple-element.125), channel_id=1, source_target_pairs={{0,4},{4,0},{8,12},{12,8},{1,5},{5,1},{9,13},{13,9},{2,6},{6,2},{1... | collective-permute-start | bytes 1179656 | tf_op jit(solution)/shard_map/ppermute | solution.py:59
  545.6 16.0 %collective-permute-start.93 = (bf16[1568,128]{1,0:T(8,128)(2,1)S(1)}, bf16[1568,128]{1,0:T(8,128)(2,1)S(1)}, u32[]{:S(2)}, u32[]{:S(2)}) collective-permute-start(bf16[1568,128]{1,0:T(8,128)(2,1)S(1)} %select_convert_fusion), channel_id=1, source_target_pairs={{0,16},{16,0},{1,17},{17,1},{2,18},{18,2},{3,19},{19,3},{4,20},{20... | collective-permute-start | bytes 1204232 | tf_op jit(solution)/shard_map/ppermute | solution.py:50
  547.2 16.1 %collective-permute-start.77 = (bf16[256,1024]{1,0:T(8,128)(2,1)S(1)}, bf16[256,1024]{1,0:T(8,128)(2,1)S(1)}, u32[]{:S(2)}, u32[]{:S(2)}) collective-permute-start(bf16[256,1024]{1,0:T(8,128)(2,1)S(1)} %slice.1810), channel_id=1, source_target_pairs={{0,16},{16,0},{1,17},{17,1},{2,18},{18,2},{3,19},{19,3},{4,20},{20... | collective-permute-start | bytes 1572872 | tf_op jit(solution)/shard_map/ppermute | solution.py:50
  561.6 17.4 %collective-permute-start.91 = (bf16[384,256]{1,0:T(8,128)(2,1)S(1)}, bf16[384,256]{1,0:T(8,128)(2,1)S(1)}, u32[]{:S(2)}, u32[]{:S(2)}) collective-permute-start(bf16[384,256]{1,0:T(8,128)(2,1)S(1)} %slice.1827), channel_id=1, source_target_pairs={{0,2},{1,3},{2,0},{3,1},{4,6},{5,7},{6,4},{7,5},{8,10},{9,11},{10,... | collective-permute-start | bytes 589832 | tf_op jit(solution)/shard_map/ppermute | solution.py:56
  563.6 13.5 %collective-permute-start.78 = (bf16[128,1024]{1,0:T(8,128)(2,1)S(1)}, bf16[128,1024]{1,0:T(8,128)(2,1)S(1)}, u32[]{:S(2)}, u32[]{:S(2)}) collective-permute-start(bf16[128,1024]{1,0:T(8,128)(2,1)S(1)} %slice.1818), channel_id=1, source_target_pairs={{0,1},{1,0},{2,3},{3,2},{4,5},{5,4},{6,7},{7,6},{8,9},{9,8},{10,11... | collective-permute-start | bytes 786440 | tf_op jit(solution)/shard_map/ppermute | solution.py:53
  577.8 13.9 %collective-permute-start.79 = (bf16[128,1024]{1,0:T(8,128)(2,1)S(1)}, bf16[128,1024]{1,0:T(8,128)(2,1)S(1)}, u32[]{:S(2)}, u32[]{:S(2)}) collective-permute-start(bf16[128,1024]{1,0:T(8,128)(2,1)S(1)} %constant_dynamic-update-slice_fusion.32), channel_id=1, source_target_pairs={{0,2},{1,3},{2,0},{3,1},{4,6},{5,7},{6,4},{7,5},{8,10},{9,11},{10,... | collective-permute-start | bytes 786440 | tf_op jit(solution)/shard_map/ppermute | solution.py:56
  579.1 12.8 %collective-permute-start.92 = (bf16[384,128]{1,0:T(8,128)(2,1)S(1)}, bf16[384,128]{1,0:T(8,128)(2,1)S(1)}, u32[]{:S(2)}, u32[]{:S(2)}) collective-permute-start(bf16[384,128]{1,0:T(8,128)(2,1)S(1)} %select_convert_fusion.2), channel_id=1, source_target_pairs={{0,16},{16,0},{1,17},{17,1},{2,18},{18,2},{3,19},{19,3},{4,20},{20... | collective-permute-start | bytes 294920 | tf_op jit(solution)/shard_map/ppermute | solution.py:50
  593.4 14.0 %collective-permute-start.81 = (bf16[256,1024]{1,0:T(8,128)(2,1)S(1)}, bf16[256,1024]{1,0:T(8,128)(2,1)S(1)}, u32[]{:S(2)}, u32[]{:S(2)}) collective-permute-start(bf16[256,1024]{1,0:T(8,128)(2,1)S(1)} %pad_maximum_fusion.37), channel_id=1, source_target_pairs={{0,1},{1,0},{2,3},{3,2},{4,5},{5,4},{6,7},{7,6},{8,9},{9,8},{10,11... | collective-permute-start | bytes 1572872 | tf_op jit(solution)/shard_map/ppermute | solution.py:53
  624.6 37.0 %all-to-all-start = ((bf16[4,128,1024]{2,1,0:T(8,128)(2,1)}), bf16[4,128,1024]{2,1,0:T(8,128)(2,1)S(1)}, u32[]{:S(2)}, u32[]{:S(2)}) async-start(bf16[4,128,1024]{2,1,0:T(8,128)(2,1)} %bitcast.124), calls=%async_computation.2 | async-start | bytes 2097152 | tf_op jit(solution)/shard_map/all_to_all | solution.py:660
  630.4 30.3 %collective-permute-start.94 = (bf16[1184,256]{1,0:T(8,128)(2,1)S(1)}, bf16[1184,256]{1,0:T(8,128)(2,1)S(1)}, u32[]{:S(2)}, u32[]{:S(2)}) collective-permute-start(bf16[1184,256]{1,0:T(8,128)(2,1)S(1)} %pad_maximum_fusion.26), channel_id=1, source_target_pairs={{0,2},{1,3},{2,0},{3,1},{4,6},{5,7},{6,4},{7,5},{8,10},{9,11},{10,... | collective-permute-start | bytes 1818632 | tf_op jit(solution)/shard_map/ppermute | solution.py:56
  (146 other events, 1317.1 us)
Sparse Core Ops, SparseCore 0:
  75.8 65.7 all-gather.3
  173.0 35.1 all-gather.5
  210.0 58.9 all-gather.7
  364.6 32.8 reduce-scatter.4
  400.3 30.2 reduce-scatter.10
  433.5 53.6 reduce-scatter.6
  494.2 50.6 reduce-scatter.8
